TPU v7x, 32 devices: a whole 2x2x4 slice. The times are simulated.
32 devices in a mesh: row: 4 (over z), col: 8 (over y, x, core).
Axes of the slice: x: 2, y: 2, z: 4, core: 2. Of those that a mesh axis runs over, the one named last changes fastest.
Arguments:
- observed: float32 [4096, 2048], P('row', 'col'), may hold values from -12 to 12
- kernels: float32 [8, 65, 65], replicated, may hold values from -0.0625 to 0.0625
- occupied: int32 [16, 8], replicated, may hold values from 0 to 1, as said below
- kernel_index: int32 [16, 8], replicated, may hold values from 0 to 7
Outputs:
- corrected: float32 [4096, 2048], P('row', 'col')
- residual: float32 [4096, 2048], P('row', 'col')
Inputs may be any that keep to these rules, and one draw needn't show every extreme that they name: The tiles with occupied = 1 are those whose centres lie inside one disk; at least one tile is occupied and at least one is not.
All inputs are finite; a program needn't handle non-finite values.
Results may differ from a plain program's by a relative error of at most 0.0003.
Values sent between devices are 32-bit elements; how exact they have to be, the bound alone decides.
No kernel may reach another device: no remote copies, remote signals or barrier semaphores. Data moves between devices by JAX's collectives and lax.ppermute only.
A program may use at most 128 MiB of HBM per device.

v0:
```python
import math

import jax
import jax.numpy as jnp
from jax import lax
from jax.sharding import PartitionSpec as P

TILE = 256
HALO = 64
KW = 65
ITERS = 3


def padded(block, sides, width):
    for axis, dim in sides:
        count = lax.axis_size(axis)
        forward = [(i, i + 1) for i in range(count - 1)]
        backward = [(target, source) for source, target in forward]
        low = lax.ppermute(
            lax.slice_in_dim(block, block.shape[dim] - width, None, axis=dim), axis, forward
        )
        high = lax.ppermute(lax.slice_in_dim(block, 0, width, axis=dim), axis, backward)
        block = jnp.concatenate([low, block, high], axis=dim)
    return block


def matmul(left, right):
    return jnp.dot(left, right, precision=lax.Precision.HIGHEST, preferred_element_type=jnp.float32)


def dft_tables(win_size):
    positions = jnp.arange(win_size, dtype=jnp.int32)
    phases = positions[:, None] * positions[None, :] % win_size
    angles = phases.astype(jnp.float32) * (2.0 * math.pi / win_size)
    return (jnp.cos(angles), jnp.sin(angles))


def spectrum_of(kernel, cos_t, sin_t):
    cos_left = cos_t[:, :KW]
    sin_left = sin_t[:, :KW]
    ker_cos = matmul(kernel, cos_t[:KW])
    ker_sin = matmul(kernel, sin_t[:KW])
    real_part = matmul(cos_left, ker_cos) - matmul(sin_left, ker_sin)
    imag_part = -(matmul(cos_left, ker_sin) + matmul(sin_left, ker_cos))
    return real_part * real_part + imag_part * imag_part


def convolve(window, spectrum, cos_t, sin_t):
    win_size = window.shape[0]
    win_cos = matmul(window, cos_t)
    win_sin = matmul(window, sin_t)
    real_part = spectrum * (matmul(cos_t, win_cos) - matmul(sin_t, win_sin))
    imag_part = -spectrum * (matmul(cos_t, win_sin) + matmul(sin_t, win_cos))
    inner_real = matmul(real_part, cos_t) - matmul(imag_part, sin_t)
    inner_imag = matmul(real_part, sin_t) + matmul(imag_part, cos_t)
    return (matmul(cos_t, inner_real) - matmul(sin_t, inner_imag)) / (win_size * win_size)


def cut_window(extended, slot_num, win_size):
    return lax.dynamic_slice(extended, (slot_num * TILE, 0), (win_size, win_size))


def add_window(buffer, slot_num, piece):
    row_start = slot_num * TILE
    current = lax.dynamic_slice(buffer, (row_start, 0), piece.shape)
    return lax.dynamic_update_slice(buffer, current + piece, (row_start, 0))


def fold_spill(buffer, spill):
    width_h = HALO
    block_h = buffer.shape[0] - 2 * width_h
    block_w = buffer.shape[1] - 2 * width_h
    result = buffer[width_h : width_h + block_h, width_h : width_h + block_w]
    mid_cols = slice(2 * width_h, 2 * width_h + block_w)
    mid_rows = slice(2 * width_h, 2 * width_h + block_h)
    result = result.at[:width_h, :].add(spill[:width_h, mid_cols])
    result = result.at[block_h - width_h :, :].add(spill[block_h + 3 * width_h :, mid_cols])
    result = result.at[:, :width_h].add(spill[mid_rows, :width_h])
    result = result.at[:, block_w - width_h :].add(spill[mid_rows, block_w + 3 * width_h :])
    result = result.at[:width_h, :width_h].add(spill[:width_h, :width_h])
    result = result.at[:width_h, block_w - width_h :].add(spill[:width_h, block_w + 3 * width_h :])
    result = result.at[block_h - width_h :, :width_h].add(spill[block_h + 3 * width_h :, :width_h])
    result = result.at[block_h - width_h :, block_w - width_h :].add(
        spill[block_h + 3 * width_h :, block_w + 3 * width_h :]
    )
    return result


def column_tiles(table, col_num, first_tile, tile_count):
    column = lax.dynamic_index_in_dim(table, col_num, 1, keepdims=False)
    return lax.dynamic_slice_in_dim(column, first_tile, tile_count)


def shards(observed, kernels, occupied, kernel_index):
    tile_count = observed.shape[0] // TILE
    win_size = TILE + 2 * HALO
    cos_t, sin_t = dft_tables(win_size)
    spectra = jnp.stack(
        [spectrum_of(kernels[kernel_num], cos_t, sin_t) for kernel_num in range(kernels.shape[0])]
    )
    my_row = lax.axis_index("row")
    my_col = lax.axis_index("col")
    first_tile = my_row * tile_count
    occ_mine = column_tiles(occupied, my_col, first_tile, tile_count)
    kid_mine = column_tiles(kernel_index, my_col, first_tile, tile_count)
    order_mine = jnp.argsort(1 - occ_mine, stable=True)
    count_mine = jnp.sum(occ_mine)

    def tile_product(window, kernel_num):
        spectrum = lax.dynamic_index_in_dim(spectra, kernel_num, 0, keepdims=False)
        return convolve(window, spectrum, cos_t, sin_t)

    def squares(residual):
        return lax.psum(jnp.sum(residual * residual), ("row", "col"))

    corrected = jnp.zeros_like(observed)
    residual = observed
    direction = observed
    energy = squares(residual)
    for iteration in range(ITERS):
        apply_extended = padded(direction, (("row", 0), ("col", 1)), HALO)
        extended = apply_extended

        def own_step(slot_pos, buffer):
            slot_num = order_mine[slot_pos]

            def work(current):
                window = cut_window(extended, slot_num, win_size)
                return add_window(current, slot_num, tile_product(window, kid_mine[slot_num]))

            return lax.cond(slot_pos < count_mine, work, lambda current: current, buffer)

        apply_buffer = lax.fori_loop(0, tile_count, own_step, jnp.zeros_like(extended))
        spill = padded(apply_buffer, (("row", 0), ("col", 1)), HALO)
        mapped = direction + fold_spill(apply_buffer, spill)
        step_len = energy / lax.psum(jnp.sum(direction * mapped), ("row", "col"))
        corrected = corrected + step_len * direction
        residual = residual - step_len * mapped
        fresh = squares(residual)
        direction = residual + fresh / energy * direction
        energy = fresh
    return (corrected, residual)


def solution(mesh):
    placed = (P("row", "col"), P(), P(), P())
    return jax.shard_map(
        shards,
        mesh=mesh,
        in_specs=placed,
        out_specs=(P("row", "col"), P("row", "col")),
        check_vma=False,
    )
```

profile of v0, /device:TPU:0, one launch (start us, length us, event | category | flops | bytes accessed | tf_op | source)
XLA Modules:
  0.0 943.1 jit_solution(6419256422168535399)
XLA Ops:
  3.0 5.6 collective-permute-start
  9.9 2.2 fusion.114
  12.1 2.2 fusion.113
  45.0 2.8 fusion.94
  47.8 2.8 fusion.96
  64.0 2.2 collective-permute-start.2
  67.5 6.1 copy.61
  76.7 2.5 pad_maximum_fusion
  79.2 2.8 copy.62
  83.4 6.1 while.78
  90.6 4.4 collective-permute-start.4
  98.6 110.5 %collective-permute-done.5 = f32[64,384]{0,1:T(8,128)S(1)} collective-permute-done((f32[64,384]{0,1:T(8,128)S(1)}, f32[64,384]{0,1:T(8,128)S(1)}, u32[]{:S(2)}, u32[]{:S(2)}) %collective-permute-start.5) | collective-permute-done | bytes 98336 | tf_op jit(solution)/shard_map/ppermute | solution.py:22
  209.1 2.9 concatenate.77
  211.9 1.8 fusion.204
  213.8 39.9 %collective-permute-start.6 = (f32[1280,64]{0,1:T(8,128)}, f32[1280,64]{0,1:T(8,128)}, u32[]{:S(2)}, u32[]{:S(2)}) collective-permute-start(f32[1280,64]{0,1:T(8,128)} %get-tuple-element.1482), channel_id=1, source_target_pairs={{0,1},{1,2},{2,3},{3,4},{4,5},{5,6},{6,7},{8,9},{9,10},{10,11},{11... | collective-permute-start | bytes 983048 | tf_op jit(solution)/shard_map/ppermute | solution.py:19
  258.1 1.7 fusion.116
  261.8 1.9 add_select_fusion.9
  263.7 2.1 scatter-add.89
  269.8 45.6 %all-reduce = (f32[]{:T(128)}, f32[]{:T(128)}) all-reduce(f32[]{:T(128)} %multiply_reduce_fusion.5, f32[]{:T(128)} %get-tuple-element.1475), channel_id=1, replica_groups=mesh['row'=4,'col'=8] {'row','col'}, use_global_device_ids=true, to_apply=%region_1.2 | all-reduce | flops 2 | bytes 16 | tf_op jit(solution)/shard_map/psum | solution.py:114
  317.6 39.9 %psum.44 = f32[]{:T(128)} all-reduce(f32[]{:T(128)} %multiply_reduce_fusion.3), channel_id=1, replica_groups=mesh['row'=4,'col'=8] {'row','col'}, use_global_device_ids=true, to_apply=%region_13.14 | all-reduce | flops 1 | bytes 8 | tf_op jit(solution)/shard_map/psum | solution.py:114
  359.1 4.0 collective-permute-start.8
  365.6 4.4 collective-permute-done.9
  374.3 4.8 collective-permute-done.11
  380.5 2.8 copy.69
  384.7 5.7 while.79
  391.5 2.6 collective-permute-start.12
  395.4 1.6 slice.855
  397.3 109.7 %collective-permute-done.13 = f32[64,384]{0,1:T(8,128)S(1)} collective-permute-done((f32[64,384]{0,1:T(8,128)S(1)}, f32[64,384]{0,1:T(8,128)S(1)}, u32[]{:S(2)}, u32[]{:S(2)}) %collective-permute-start.13) | collective-permute-done | bytes 98336 | tf_op jit(solution)/shard_map/ppermute | solution.py:22
  507.0 2.9 concatenate.80
  509.9 1.9 fusion.203
  511.9 43.2 %collective-permute-start.14 = (f32[1280,64]{0,1:T(8,128)}, f32[1280,64]{0,1:T(8,128)}, u32[]{:S(2)}, u32[]{:S(2)}) collective-permute-start(f32[1280,64]{0,1:T(8,128)} %get-tuple-element.1480), channel_id=1, source_target_pairs={{0,1},{1,2},{2,3},{3,4},{4,5},{5,6},{6,7},{8,9},{9,10},{10,11},{11... | collective-permute-start | bytes 983048 | tf_op jit(solution)/shard_map/ppermute | solution.py:19
  556.5 1.7 slice_add_fusion.6
  558.2 1.6 scatter-add.94
  560.8 1.7 fusion.117
  566.4 2.7 add_select_fusion.8
  569.1 2.9 scatter-add.101
  572.9 2.4 scatter-add.104
  576.1 1.7 scatter-add.105
  577.9 3.1 multiply_reduce_fusion.2
  580.9 43.1 %psum.45 = f32[]{:T(128)} all-reduce(f32[]{:T(128)} %get-tuple-element.1473), channel_id=1, replica_groups=mesh['row'=4,'col'=8] {'row','col'}, use_global_device_ids=true, to_apply=%region_19.20 | all-reduce | flops 1 | bytes 8 | tf_op jit(solution)/shard_map/psum | solution.py:136
  625.3 3.1 multiply_reduce_fusion.1
  628.4 40.0 %psum.46 = f32[]{:T(128)} all-reduce(f32[]{:T(128)} %get-tuple-element.1471), channel_id=1, replica_groups=mesh['row'=4,'col'=8] {'row','col'}, use_global_device_ids=true, to_apply=%region_21.22 | all-reduce | flops 1 | bytes 8 | tf_op jit(solution)/shard_map/psum | solution.py:114
  671.2 3.6 collective-permute-start.16
  677.3 4.4 collective-permute-done.17
  686.8 4.7 collective-permute-done.19
  692.9 1.8 copy.71
  696.1 4.5 while.80
  701.7 2.6 collective-permute-start.20
  705.6 1.6 slice.879
  707.4 109.7 %collective-permute-done.21 = f32[64,384]{0,1:T(8,128)S(1)} collective-permute-done((f32[64,384]{0,1:T(8,128)S(1)}, f32[64,384]{0,1:T(8,128)S(1)}, u32[]{:S(2)}, u32[]{:S(2)}) %collective-permute-start.21) | collective-permute-done | bytes 98336 | tf_op jit(solution)/shard_map/ppermute | solution.py:22
  817.1 2.9 concatenate.83
  820.0 2.0 fusion.202
  821.9 42.8 %collective-permute-start.22 = (f32[1280,64]{0,1:T(8,128)}, f32[1280,64]{0,1:T(8,128)}, u32[]{:S(2)}, u32[]{:S(2)}) collective-permute-start(f32[1280,64]{0,1:T(8,128)} %get-tuple-element.1478), channel_id=1, source_target_pairs={{0,1},{1,2},{2,3},{3,4},{4,5},{5,6},{6,7},{8,9},{9,10},{10,11},{11... | collective-permute-start | bytes 983048 | tf_op jit(solution)/shard_map/ppermute | solution.py:19
  866.2 1.7 slice_add_fusion.4
  867.9 1.6 scatter-add.106
  870.5 1.7 fusion.118
  876.0 2.7 add_select_fusion.7
  878.7 2.9 scatter-add.115
  882.5 2.4 scatter-add.116
  885.8 1.7 scatter-add.119
  887.5 3.1 multiply_reduce_fusion
  890.7 43.3 %psum.47 = f32[]{:T(128)} all-reduce(f32[]{:T(128)} %get-tuple-element.1469), channel_id=1, replica_groups=mesh['row'=4,'col'=8] {'row','col'}, use_global_device_ids=true, to_apply=%region_27.28 | all-reduce | flops 1 | bytes 8 | tf_op jit(solution)/shard_map/psum | solution.py:136
  935.3 3.5 multiply_subtract_fusion
  938.8 2.6 copy.72
  (234 shorter events, 117.9 us)
Async XLA Ops:
  0.6 66.8 %copy-start = (s32[16,8]{0,1:T(8,128)S(1)}, s32[16,8]{0,1:T(8,128)}, u32[]{:S(2)}) copy-start(s32[16,8]{0,1:T(8,128)} %param.67) | copy-start | bytes 1540
  0.6 13.7 %copy-start.35 = (f32[8,65,65]{2,0,1:T(8,128)S(1)}, f32[8,65,65]{2,0,1:T(8,128)}, u32[]{:S(2)}) copy-start(f32[8,65,65]{2,0,1:T(8,128)} %param.65) | copy-start | bytes 405604
  3.0 58.5 %collective-permute-start = (f32[64,256]{0,1:T(8,128)}, f32[64,256]{0,1:T(8,128)}, u32[]{:S(2)}, u32[]{:S(2)}) collective-permute-start(f32[64,256]{0,1:T(8,128)} %get-tuple-element.1500), channel_id=1, source_target_pairs={{0,8},{8,16},{16,24},{1,9},{9,17},{17,25},{2,10},{10,18},{18,26},{... | collective-permute-start | bytes 196616 | tf_op jit(solution)/shard_map/ppermute | solution.py:19
  8.6 53.0 %collective-permute-start.1 = (f32[64,256]{0,1:T(8,128)}, f32[64,256]{0,1:T(8,128)}, u32[]{:S(2)}, u32[]{:S(2)}) collective-permute-start(f32[64,256]{0,1:T(8,128)} %get-tuple-element.1499), channel_id=1, source_target_pairs={{8,0},{16,8},{24,16},{9,1},{17,9},{25,17},{10,2},{18,10},{26,18},{... | collective-permute-start | bytes 196616 | tf_op jit(solution)/shard_map/ppermute | solution.py:22
  14.8 4.4 copy-start.34
  15.4 7.3 copy-start.33
  16.0 9.4 copy-start.31
  16.6 11.7 %copy-start.29 = (f32[384,65]{0,1:T(8,128)}, f32[384,65]{0,1:T(8,128)S(1)}, u32[]{:S(2)}) copy-start(f32[384,65]{0,1:T(8,128)S(1)} %fusion.146) | copy-start | bytes 299524
  17.1 14.6 %copy-start.27 = (f32[384,65]{0,1:T(8,128)}, f32[384,65]{0,1:T(8,128)S(1)}, u32[]{:S(2)}) copy-start(f32[384,65]{0,1:T(8,128)S(1)} %fusion.144) | copy-start | bytes 299524
  17.7 17.6 %copy-start.25 = (f32[384,65]{0,1:T(8,128)}, f32[384,65]{0,1:T(8,128)S(1)}, u32[]{:S(2)}) copy-start(f32[384,65]{0,1:T(8,128)S(1)} %fusion.142) | copy-start | bytes 299524
  18.3 20.5 %copy-start.23 = (f32[384,65]{0,1:T(8,128)}, f32[384,65]{0,1:T(8,128)S(1)}, u32[]{:S(2)}) copy-start(f32[384,65]{0,1:T(8,128)S(1)} %fusion.140) | copy-start | bytes 299524
  47.8 2.8 copy-start.17
  47.8 2.8 copy-start.32
  47.8 4.3 copy-start.13
  47.8 4.3 copy-start.18
  47.8 4.3 copy-start.30
  50.6 3.0 copy-start.14
  50.6 3.0 copy-start.19
  50.6 3.0 copy-start.28
  52.1 3.5 copy-start.15
  52.1 3.5 copy-start.20
  52.1 3.5 copy-start.26
  53.6 3.5 copy-start.16
  53.6 3.5 copy-start.21
  54.1 3.1 copy-start.24
  55.6 3.1 copy-start.22
  64.0 12.7 %collective-permute-start.2 = (f32[1152,64]{0,1:T(8,128)}, f32[1152,64]{0,1:T(8,128)}, u32[]{:S(2)}, u32[]{:S(2)}) collective-permute-start(f32[1152,64]{0,1:T(8,128)} %get-tuple-element.1493), channel_id=1, source_target_pairs={{0,1},{1,2},{2,3},{3,4},{4,5},{5,6},{6,7},{8,9},{9,10},{10,11},{11... | collective-permute-start | bytes 884744 | tf_op jit(solution)/shard_map/ppermute | solution.py:19
  66.2 10.5 %collective-permute-start.3 = (f32[1152,64]{0,1:T(8,128)}, f32[1152,64]{0,1:T(8,128)}, u32[]{:S(2)}, u32[]{:S(2)}) collective-permute-start(f32[1152,64]{0,1:T(8,128)} %get-tuple-element.1494), channel_id=1, source_target_pairs={{1,0},{2,1},{3,2},{4,3},{5,4},{6,5},{7,6},{9,8},{10,9},{11,10},{12... | collective-permute-start | bytes 884744 | tf_op jit(solution)/shard_map/ppermute | solution.py:22
  67.5 7.6 copy-start.36
  67.5 8.2 copy-start.11
  90.6 8.0 collective-permute-start.4
  95.0 114.0 %collective-permute-start.5 = (f32[64,384]{0,1:T(8,128)S(1)}, f32[64,384]{0,1:T(8,128)S(1)}, u32[]{:S(2)}, u32[]{:S(2)}) collective-permute-start(f32[64,384]{0,1:T(8,128)S(1)} %get-tuple-element.1487), channel_id=1, source_target_pairs={{8,0},{16,8},{24,16},{9,1},{17,9},{25,17},{10,2},{18,10},{26,18},{... | collective-permute-start | bytes 294920 | tf_op jit(solution)/shard_map/ppermute | solution.py:22
  213.8 44.3 %collective-permute-start.6 = (f32[1280,64]{0,1:T(8,128)}, f32[1280,64]{0,1:T(8,128)}, u32[]{:S(2)}, u32[]{:S(2)}) collective-permute-start(f32[1280,64]{0,1:T(8,128)} %get-tuple-element.1482), channel_id=1, source_target_pairs={{0,1},{1,2},{2,3},{3,4},{4,5},{5,6},{6,7},{8,9},{9,10},{10,11},{11... | collective-permute-start | bytes 983048 | tf_op jit(solution)/shard_map/ppermute | solution.py:19
  253.7 6.2 collective-permute-start.7
  269.8 89.2 %copy-start.7 = (f32[1024,256]{0,1:T(8,128)}, f32[1024,256]{0,1:T(8,128)S(1)}, u32[]{:S(2)}) copy-start(f32[1024,256]{0,1:T(8,128)S(1)} %get-tuple-element.1476) | copy-start | bytes 3145732
  359.0 12.7 %copy-start.2 = (f32[1024,256]{0,1:T(8,128)}, f32[1024,256]{0,1:T(8,128)S(1)}, u32[]{:S(2)}) copy-start(f32[1024,256]{0,1:T(8,128)S(1)} %multiply_add_fusion.2) | copy-start | bytes 3145732
  359.1 6.5 collective-permute-start.8
  363.1 6.9 collective-permute-start.9
  371.6 2.7 collective-permute-start.10
  372.9 6.2 collective-permute-start.11
  391.5 5.7 collective-permute-start.12
  394.1 112.9 %collective-permute-start.13 = (f32[64,384]{0,1:T(8,128)S(1)}, f32[64,384]{0,1:T(8,128)S(1)}, u32[]{:S(2)}, u32[]{:S(2)}) collective-permute-start(f32[64,384]{0,1:T(8,128)S(1)} %get-tuple-element.1485), channel_id=1, source_target_pairs={{8,0},{16,8},{24,16},{9,1},{17,9},{25,17},{10,2},{18,10},{26,18},{... | collective-permute-start | bytes 294920 | tf_op jit(solution)/shard_map/ppermute | solution.py:22
  511.9 48.9 %collective-permute-start.14 = (f32[1280,64]{0,1:T(8,128)}, f32[1280,64]{0,1:T(8,128)}, u32[]{:S(2)}, u32[]{:S(2)}) collective-permute-start(f32[1280,64]{0,1:T(8,128)} %get-tuple-element.1480), channel_id=1, source_target_pairs={{0,1},{1,2},{2,3},{3,4},{4,5},{5,6},{6,7},{8,9},{9,10},{10,11},{11... | collective-permute-start | bytes 983048 | tf_op jit(solution)/shard_map/ppermute | solution.py:19
  555.1 22.8 %copy-start.3 = (f32[1024,256]{0,1:T(8,128)S(1)}, f32[1024,256]{0,1:T(8,128)}, u32[]{:S(2)}) copy-start(f32[1024,256]{0,1:T(8,128)} %copy-done.2) | copy-start | bytes 3145732
  555.1 7.4 collective-permute-start.15
  565.4 1.0 copy-start.9
  569.0 56.3 %copy-start.8 = (f32[1024,256]{0,1:T(8,128)S(1)}, f32[1024,256]{0,1:T(8,128)}, u32[]{:S(2)}) copy-start(f32[1024,256]{0,1:T(8,128)} %copy-done.7) | copy-start | bytes 3145732
  671.1 13.1 %copy-start.5 = (f32[1024,256]{0,1:T(8,128)}, f32[1024,256]{0,1:T(8,128)S(1)}, u32[]{:S(2)}) copy-start(f32[1024,256]{0,1:T(8,128)S(1)} %multiply_add_fusion.1) | copy-start | bytes 3145732
  671.2 6.1 collective-permute-start.16
  674.8 6.9 collective-permute-start.17
  684.2 2.6 collective-permute-start.18
  685.5 6.0 collective-permute-start.19
  701.7 5.7 collective-permute-start.20
  704.3 112.8 %collective-permute-start.21 = (f32[64,384]{0,1:T(8,128)S(1)}, f32[64,384]{0,1:T(8,128)S(1)}, u32[]{:S(2)}, u32[]{:S(2)}) collective-permute-start(f32[64,384]{0,1:T(8,128)S(1)} %get-tuple-element.1483), channel_id=1, source_target_pairs={{8,0},{16,8},{24,16},{9,1},{17,9},{25,17},{10,2},{18,10},{26,18},{... | collective-permute-start | bytes 294920 | tf_op jit(solution)/shard_map/ppermute | solution.py:22
  821.9 48.5 %collective-permute-start.22 = (f32[1280,64]{0,1:T(8,128)}, f32[1280,64]{0,1:T(8,128)}, u32[]{:S(2)}, u32[]{:S(2)}) collective-permute-start(f32[1280,64]{0,1:T(8,128)} %get-tuple-element.1478), channel_id=1, source_target_pairs={{0,1},{1,2},{2,3},{3,4},{4,5},{5,6},{6,7},{8,9},{9,10},{10,11},{11... | collective-permute-start | bytes 983048 | tf_op jit(solution)/shard_map/ppermute | solution.py:19
  864.8 22.7 %copy-start.6 = (f32[1024,256]{0,1:T(8,128)S(1)}, f32[1024,256]{0,1:T(8,128)}, u32[]{:S(2)}) copy-start(f32[1024,256]{0,1:T(8,128)} %copy-done.5) | copy-start | bytes 3145732
  864.8 7.4 collective-permute-start.23
  875.0 1.0 copy-start.10
  878.7 56.6 %copy-start.4 = (f32[1024,256]{0,1:T(8,128)S(1)}, f32[1024,256]{0,1:T(8,128)}, u32[]{:S(2)}) copy-start(f32[1024,256]{0,1:T(8,128)} %copy-done.2) | copy-start | bytes 3145732
  938.8 2.6 copy-start.12
  938.8 3.9 copy-start.1
where the time goes:
time: 959 us; the launch traced here: 943 us
  waiting for transfers between devices  351 us (37%)
  blocking collectives  212 us (22%)
  starting transfers between devices  169 us (18%)
  local copies, waits for them, and re-layouts  85.2 us (9%)
  other arithmetic  60.4 us (6%)
  matrix products  44.7 us (5%)
  loops' own time  12 us (1%)
    ppermute x12, waiting for transfers between devices, padded(): lax.ppermute(lax.slice_in_dim(block, 0, width, axis=dim), axis, backward)  348 us
    ppermute x12, starting transfers between devices, padded(): lax.ppermute(lax.slice_in_dim(block, block.shape[dim] - width, None, axis...  154 us
    psum x3, blocking collectives, squares(): return lax.psum(jnp.sum(residual * residual), ('row', 'col'))  125 us
    psum x2, blocking collectives, shards(): step_len = energy / lax.psum(jnp.sum(direction * mapped), ('row', 'col'))  86.5 us
    dot_general x48, matrix products, matmul(): jnp.dot(left, right, precision=lax.Precision.HIGHEST, preferred_element_t...  44.7 us
    unnamed x81, local copies, waits for them, and re-layouts  21.5 us
  transfers between devices with their start and end apart: 24, of which 13 were waited for; matrix products, arithmetic and copies ran while one was open for 9% of the time, Pallas kernels for 0%

commit v1 on v0

v1 whole, which is shorter than its diff:
```python
import functools
import math

import jax
import jax.numpy as jnp
import numpy as np
from jax import lax
from jax.experimental import pallas as pl
from jax.experimental.pallas import tpu as pltpu
from jax.sharding import PartitionSpec as P

TILE = 256
HALO = 64
KW = 65
ITERS = 3
WIN = TILE + 2 * HALO
THIRD = WIN // 3
HALF = THIRD // 2
SLOTS = 2 * THIRD
BF = jnp.bfloat16
F32 = jnp.float32


def hi_lo(table):
    high = table.astype(np.float32).astype(jnp.bfloat16)
    low = (table - high.astype(np.float64)).astype(np.float32).astype(jnp.bfloat16)
    return high, low


@functools.cache
def tables():
    spots = np.arange(THIRD)
    low_freq = 3 * np.arange(HALF)
    full = math.sqrt(2.0 / WIN)
    cos_part = np.cos(2 * np.pi * (low_freq[:, None] * spots % WIN) / WIN) * full
    sin_part = np.sin(2 * np.pi * (low_freq[:, None] * spots % WIN) / WIN) * full
    cos_part[0] = math.sqrt(1.0 / WIN)
    sin_part[0] = np.where(spots % 2 == 0, 1.0, -1.0) * math.sqrt(1.0 / WIN)
    small = np.concatenate([cos_part, sin_part])
    angle = 2 * np.pi * ((3 * spots[:, None] + 1) * spots % WIN) / WIN
    root = math.sqrt(3.0) / 2
    large = full * np.block(
        [[np.cos(angle), -root * np.sin(angle)], [np.sin(angle), root * np.cos(angle)]]
    )
    freqs = np.concatenate([low_freq, low_freq, 3 * spots + 1])
    freqs[HALF] = WIN // 2
    taps = np.arange(THIRD)
    turn = 2 * np.pi * (freqs[:, None] * taps % WIN) / WIN
    keep = (taps < KW)[None, :]
    sines = np.sin(turn)
    sines[0] = 0.0
    sines[HALF] = 0.0
    waves = np.concatenate([np.cos(turn) * keep, sines * keep])

    sh, sl = hi_lo(small)
    gh, gl = hi_lo(large)
    wh, wl = hi_lo(waves)
    zero = np.zeros_like(sh.T)
    return dict(
        g_right=np.concatenate([gh.T, gl.T, gh.T], 0),
        g_right_inv=np.concatenate([gh, gl, gh], 0),
        f_right=np.block([[sh.T, sl.T], [sh.T, zero]]),
        f_right_inv=np.block([[sh, sl], [sh, zero]]),
        g_left=np.concatenate([gh, gl], 0),
        g_left_inv=np.concatenate([gh.T, gl.T], 0),
        f_left=np.block([[sh, sh], [sl, zero]]),
        f_left_inv=np.block([[sh.T, sh.T], [sl.T, zero]]),
        w_left=np.concatenate([wh, wl, wh], 1),
        w_right=np.concatenate([wh.T, wl.T, wh.T], 0),
    )


NAMES = (
    "g_right", "g_right_inv", "f_right", "f_right_inv",
    "g_left", "g_left_inv", "f_left", "f_left_inv",
)


def split(value):
    high = value.astype(BF)
    return high, (value - high.astype(F32)).astype(BF)


def dot(left, right):
    return jnp.dot(left, right, preferred_element_type=F32)


def right_large(value, table):
    high, low = split(value)
    return dot(jnp.concatenate([high, high, low], 1), table[...])


def right_small(value, table):
    high, low = split(value)
    both = dot(jnp.concatenate([high, low], 1), table[...])
    return both[:, :THIRD] + both[:, THIRD:]


def left_large(value, table):
    high, low = split(value)
    both = dot(table[...], high)
    return both[:SLOTS] + both[SLOTS:] + dot(table[:SLOTS], low)


def left_small(value, table):
    high, low = split(value)
    both = dot(table[...], jnp.concatenate([high, low], 0))
    return both[:THIRD] + both[THIRD:]


def butterfly(first, second, third):
    total = second + third
    return first + total, first - 0.5 * total, second - third


def unbutterfly(plain, real, diff):
    base = plain - 0.5 * real
    return plain + real, base + diff, base - diff


def spectra_kernel(kid, occ, ker_ref, left_ref, right_ref, out_ref):
    def body(slot, carry):
        @pl.when(occ[slot] != 0)
        def _():
            high, low = split(ker_ref[kid[slot]])
            half = dot(left_ref[...], jnp.concatenate([high, high, low], 0))
            high, low = split(half)
            quads = dot(jnp.concatenate([high, high, low], 1), right_ref[...])
            cc = quads[:SLOTS, :SLOTS]
            cs = quads[:SLOTS, SLOTS:]
            sc = quads[SLOTS:, :SLOTS]
            ss = quads[SLOTS:, SLOTS:]
            out_ref[slot, 0] = cc * cc + ss * ss + (sc * sc + cs * cs)
            out_ref[slot, 1] = 2.0 * (sc * cs - cc * ss)

        return carry

    lax.fori_loop(0, out_ref.shape[0], body, 0)


def apply_spectrum(low_rows, high_rows, spec_ref, slot):
    lanes = lax.broadcasted_iota(jnp.int32, (1, THIRD), 1)
    sign = jnp.where(lanes < HALF, -1.0, 1.0).astype(F32)

    def band(cos_rows, sin_rows, cos_at, sin_at, size):
        pc = spec_ref[slot, 0, pl.ds(cos_at, size), :]
        ps = spec_ref[slot, 0, pl.ds(sin_at, size), :] if sin_at != cos_at else pc
        cross = spec_ref[slot, 1, pl.ds(cos_at, size), :]
        d0, d1 = cross[:, :THIRD] * sign, cross[:, THIRD:]
        c0, c1, c2 = (cos_rows[:, i * THIRD : (i + 1) * THIRD] for i in range(3))
        s0, s1, s2 = (sin_rows[:, i * THIRD : (i + 1) * THIRD] for i in range(3))
        new_cos = jnp.concatenate(
            [
                pc[:, :THIRD] * c0 + d0 * pltpu.roll(s0, HALF, 1),
                pc[:, THIRD:] * c1 - d1 * s2,
                pc[:, THIRD:] * c2 + d1 * s1,
            ],
            1,
        )
        new_sin = jnp.concatenate(
            [
                ps[:, :THIRD] * s0 - d0 * pltpu.roll(c0, HALF, 1),
                ps[:, THIRD:] * s1 + d1 * c2,
                ps[:, THIRD:] * s2 - d1 * c1,
            ],
            1,
        )
        return new_cos, new_sin

    low = band(low_rows[:HALF], low_rows[HALF:], 0, HALF, HALF)
    high = band(high_rows[:THIRD], high_rows[THIRD:], THIRD, THIRD, THIRD)
    return jnp.concatenate(low, 0), jnp.concatenate(high, 0)


def window_product(blocks, spec_ref, slot, tabs):
    halves = []
    for block in blocks:
        t0, t1, t2 = (block[:, i * THIRD : (i + 1) * THIRD] for i in range(3))
        plain, real, diff = butterfly(t0, t1, t2)
        halves.append(
            jnp.concatenate(
                [
                    right_small(plain, tabs["f_right"]),
                    right_large(jnp.concatenate([real, diff], 1), tabs["g_right"]),
                ],
                1,
            )
        )
    plain, real, diff = butterfly(*halves)
    low_rows = left_small(plain, tabs["f_left"])
    high_rows = left_large(jnp.concatenate([real, diff], 0), tabs["g_left"])
    low_rows, high_rows = apply_spectrum(low_rows, high_rows, spec_ref, slot)
    plain = left_small(low_rows, tabs["f_left_inv"])
    both = left_large(high_rows, tabs["g_left_inv"])
    results = []
    for block in unbutterfly(plain, both[:THIRD], both[THIRD:]):
        plain = right_small(block[:, :THIRD], tabs["f_right_inv"])
        both = right_large(block[:, THIRD:], tabs["g_right_inv"])
        results.append(
            jnp.concatenate(unbutterfly(plain, both[:, :THIRD], both[:, THIRD:]), 1)
        )
    return results


def lane_mask():
    return lax.broadcasted_iota(jnp.int32, (1, THIRD), 1) < HALF


def tile_of(block, num):
    return block[:, num * THIRD : (num + 1) * THIRD]


def fold8(value):
    rows = value.reshape(value.shape[0] // 8, 8, value.shape[1]).sum(0)
    return sum(tile_of(rows, i) for i in range(value.shape[1] // THIRD))


def matvec(occ, res_ref, spec_ref, tabs, buf_ref, left_ref, right_ref, acc_ref):
    tile_count = spec_ref.shape[0]
    buf_ref[pl.ds(0, THIRD), :] = jnp.zeros((THIRD, WIN), F32)

    def body(slot, carry):
        at = [pl.ds(pl.multiple_of(slot * TILE + i * THIRD, THIRD), THIRD) for i in range(3)]

        @pl.when(occ[slot] != 0)
        def _():
            blocks = [res_ref[here, :] for here in at]
            out = window_product(blocks, spec_ref, slot, tabs)
            for block, new in zip(blocks, out):
                acc_ref[...] += fold8(block * new)
            buf_ref[at[0], :] += out[0]
            buf_ref[at[1], :] = out[1]
            buf_ref[at[2], :] = out[2]

        @pl.when(occ[slot] == 0)
        def _():
            buf_ref[at[1], :] = jnp.zeros((THIRD, WIN), F32)
            buf_ref[at[2], :] = jnp.zeros((THIRD, WIN), F32)

        return carry

    lax.fori_loop(0, tile_count, body, 0)
    low = lane_mask()

    def edges(num, carry):
        here = pl.ds(pl.multiple_of(num * THIRD, THIRD), THIRD)
        block = buf_ref[here, :]
        left_ref[here, :] = jnp.where(low, tile_of(block, 0), tile_of(block, 2))
        right_ref[here, :] = jnp.where(low, tile_of(block, 2), tile_of(block, 1))
        return carry

    lax.fori_loop(0, 2 * tile_count + 1, edges, 0)


def total(value):
    return jnp.sum(jnp.sum(value, 0, keepdims=True), 1, keepdims=True)


def partials(out_ref, *values):
    lanes = lax.broadcasted_iota(jnp.int32, out_ref.shape, 1)
    out = jnp.zeros(out_ref.shape, F32)
    for num, value in enumerate(values):
        out = jnp.where(lanes == num, value, out)
    out_ref[...] = out


def first_kernel(
    occ, obs_ref, from_left, from_right, above, below, spec_ref, *rest
):
    tabs = dict(zip(NAMES, rest[: len(NAMES)]))
    res_ref, buf_ref, left_ref, right_ref, part_ref, acc_ref = rest[len(NAMES) :]
    rows = obs_ref.shape[0]
    res_ref[pl.ds(0, HALO), :] = above[...]
    res_ref[pl.ds(HALO + rows, HALO), :] = below[...]
    res_ref[pl.ds(HALO, rows), pl.ds(0, TILE)] = obs_ref[...]
    res_ref[pl.ds(HALO, rows), pl.ds(TILE, THIRD)] = jnp.where(
        lane_mask(), from_right[...], from_left[...]
    )
    square = fold8(obs_ref[...] * obs_ref[...])
    acc_ref[...] = square
    matvec(occ, res_ref, spec_ref, tabs, buf_ref, left_ref, right_ref, acc_ref)
    partials(part_ref, total(square), total(acc_ref[...]))


def scalars(parts_ref, coef_ref):
    sums = jnp.sum(parts_ref[...], 0, keepdims=True)
    energy, curve, cross = sums[:, 0:1], sums[:, 1:2], sums[:, 2:3]
    if coef_ref is None:
        return jnp.zeros_like(energy), energy / curve, energy, curve
    ratio = energy / coef_ref[0:1, 0:1]
    power = curve + ratio * (2.0 * cross + ratio * coef_ref[0:1, 1:2])
    return ratio, energy / power, energy, power


def next_kernel(first, last, tile_count, *refs):
    refs = list(refs)
    occ, edge = refs[:2]
    refs = refs[2:]
    parts_ref = refs.pop(0)
    coef_ref = None if first else refs.pop(0)
    buf_in, from_left, from_right, above, below, res_in = refs[:6]
    refs = refs[6:]
    if first:
        dir_in = map_in = cor_in = None
    else:
        dir_in, map_in, cor_in = refs[:3]
        refs = refs[3:]
    if last:
        cor_ref, res_ref = refs
        dir_ref = map_ref = None
    else:
        spec_ref = refs.pop(0)
        tabs = dict(zip(NAMES, refs[: len(NAMES)]))
        refs = refs[len(NAMES) :]
        (res_ref, dir_ref, map_ref, cor_ref, buf_ref, left_ref, right_ref, part_ref, coef_out,
         acc_ref, cross_ref) = refs
    ratio, step, energy, power = scalars(parts_ref, coef_ref)
    low = lane_mask()
    flags = [edge[i].astype(F32) for i in range(4)]
    halo_lanes = jnp.where(low, flags[3], flags[2])
    ext = buf_in.shape[0]

    def piece(start, size, top, bottom, in_block):
        here = pl.ds(start, size)
        block = buf_in[here, :]
        west, east = from_left[here, :], from_right[here, :]
        add = [
            tile_of(block, 0) + jnp.where(low, west, 0.0),
            tile_of(block, 1) + jnp.where(low, 0.0, east),
            tile_of(block, 2) + jnp.where(low, east, west),
        ]
        if top is not None:
            add = [a + above[pl.ds(top, size), pl.ds(i * THIRD, THIRD)] for i, a in enumerate(add)]
        if bottom is not None:
            add = [a + below[pl.ds(bottom, size), pl.ds(i * THIRD, THIRD)] for i, a in enumerate(add)]
        old = res_in[here, :]
        mapped = [a + tile_of(old, i) for i, a in enumerate(add)]
        mapped[2] = mapped[2] * halo_lanes
        if not in_block:
            mapped = [a * flags[0 if bottom is None else 1] for a in mapped]
        direct = [tile_of(old, i) for i in range(3)]
        if not first:
            past, was = map_in[here, :], dir_in[here, :]
            mapped = [a + ratio * tile_of(past, i) for i, a in enumerate(mapped)]
            direct = [a + ratio * tile_of(was, i) for i, a in enumerate(direct)]
        fresh = [tile_of(old, i) - step * a for i, a in enumerate(mapped)]
        inner = pl.ds(start - HALO, size) if in_block else None
        if in_block:
            for i in range(2):
                lanes = pl.ds(i * THIRD, THIRD)
                if first:
                    cor_ref[inner, lanes] = step * direct[i]
                else:
                    cor_ref[inner, lanes] = cor_in[inner, lanes] + step * direct[i]
        if last:
            for i in range(2):
                res_ref[inner, pl.ds(i * THIRD, THIRD)] = fresh[i]
            return
        for i in range(3):
            lanes = pl.ds(i * THIRD, THIRD)
            res_ref[here, lanes] = fresh[i]
            map_ref[here, lanes] = mapped[i]
            dir_ref[here, lanes] = direct[i]
        if in_block:
            acc_ref[...] += fold8(fresh[0] * fresh[0]) + fold8(fresh[1] * fresh[1])
            cross_ref[...] += fold8(fresh[0] * mapped[0]) + fold8(fresh[1] * mapped[1])

    if not last:
        acc_ref[...] = jnp.zeros_like(acc_ref)
        cross_ref[...] = jnp.zeros_like(cross_ref)
        piece(0, HALO, 0, None, False)
        piece(ext - HALO, HALO, None, HALO, False)
    piece(HALO, HALO, HALO, None, True)
    piece(ext - 2 * HALO, HALO, None, 0, True)

    def middle(num, carry):
        piece(pl.multiple_of((num + 1) * THIRD, THIRD), THIRD, None, None, True)
        return carry

    lax.fori_loop(0, (ext - 4 * HALO) // THIRD, middle, 0)
    if last:
        return
    square = total(acc_ref[...])
    matvec(occ, res_ref, spec_ref, tabs, buf_ref, left_ref, right_ref, acc_ref)
    partials(part_ref, square, total(acc_ref[...]), total(cross_ref[...]))
    partials(coef_out, energy, power)


def vmem(count):
    return [pl.BlockSpec(memory_space=pltpu.VMEM)] * count


def smem(count):
    return [pl.BlockSpec(memory_space=pltpu.SMEM)] * count


def shape(*dims):
    return jax.ShapeDtypeStruct(dims, F32)


PARAMS = pltpu.CompilerParams(vmem_limit_bytes=40 * 1024 * 1024)


def own_part(table, tile_count):
    column = lax.dynamic_index_in_dim(table, lax.axis_index("col"), 1, keepdims=False)
    return lax.dynamic_slice_in_dim(column, lax.axis_index("row") * tile_count, tile_count)


def shards(observed, kernels, occupied, kernel_index):
    rows, cols = observed.shape
    tile_count = rows // TILE
    ext = rows + 2 * HALO
    n_row, n_col = lax.axis_size("row"), lax.axis_size("col")
    devices = n_row * n_col
    occ = own_part(occupied, tile_count)
    kid = own_part(kernel_index, tile_count)
    my_row, my_col = lax.axis_index("row"), lax.axis_index("col")
    edge = jnp.stack([my_row > 0, my_row < n_row - 1, my_col > 0, my_col < n_col - 1]).astype(jnp.int32)
    host = tables()
    consts = [jnp.asarray(host[name]) for name in NAMES]

    def shift(value, axis, forward):
        count = lax.axis_size(axis)
        pairs = [(i, i + 1) for i in range(count - 1)]
        return lax.ppermute(value, axis, pairs if forward else [(b, a) for a, b in pairs])

    low = lax.broadcasted_iota(jnp.int32, (1, THIRD), 1) < HALF

    from_left = shift(observed[:, THIRD:], "col", True)
    from_right = shift(observed[:, :THIRD], "col", False)

    padded = jnp.pad(kernels, ((0, 0), (0, THIRD - KW), (0, THIRD - KW)))
    spec = pl.pallas_call(
        spectra_kernel,
        out_shape=shape(tile_count, 2, SLOTS, SLOTS),
        in_specs=smem(2) + vmem(3),
        out_specs=vmem(1)[0],
        compiler_params=PARAMS,
    )(kid, occ, padded, jnp.asarray(host["w_left"]), jnp.asarray(host["w_right"]))

    def halo_rows(part):
        return jnp.concatenate(
            [observed[part], jnp.where(low, from_right[part], from_left[part])], 1
        )

    above = shift(halo_rows(slice(rows - HALO, rows)), "row", True)
    below = shift(halo_rows(slice(0, HALO)), "row", False)

    out_strips = [shape(ext, WIN), shape(ext, THIRD), shape(ext, THIRD), shape(devices, THIRD)]
    res, buf, to_left, to_right, part = pl.pallas_call(
        first_kernel,
        out_shape=[shape(ext, WIN)] + out_strips,
        in_specs=smem(1) + vmem(6 + len(NAMES)),
        out_specs=vmem(5),
        scratch_shapes=[pltpu.VMEM((8, THIRD), F32)],
        compiler_params=PARAMS,
    )(occ, observed, from_left, from_right, above, below, spec, *consts)

    coef = direction = mapped = corrected = None
    for iteration in range(ITERS):
        first, last = iteration == 0, iteration == ITERS - 1
        from_left = shift(to_right, "col", True)
        from_right = shift(to_left, "col", False)
        parts = lax.all_to_all(part, ("row", "col"), 0, 0, tiled=True)

        def edge_rows(start):
            here = slice(start, start + 2 * HALO)
            west, east = from_left[here], from_right[here]
            add = [jnp.where(low, west, 0.0), jnp.where(low, 0.0, east), jnp.where(low, east, west)]
            return buf[here] + jnp.concatenate(add, 1)

        above = shift(edge_rows(rows), "row", True)
        below = shift(edge_rows(0), "row", False)
        args = [occ, edge, parts]
        args += [] if first else [coef]
        args += [buf, from_left, from_right, above, below, res]
        args += [] if first else [direction, mapped, corrected]
        if last:
            outs = [shape(rows, cols), shape(rows, cols)]
            scratch = []
        else:
            args += [spec, *consts]
            outs = [shape(ext, WIN)] * 3 + [shape(rows, cols)] + out_strips + [shape(8, THIRD)]
            scratch = [pltpu.VMEM((8, THIRD), F32)] * 2
        result = pl.pallas_call(
            functools.partial(next_kernel, first, last, tile_count),
            out_shape=outs,
            in_specs=smem(2) + vmem(len(args) - 2),
            out_specs=vmem(len(outs)),
            scratch_shapes=scratch,
            compiler_params=PARAMS,
        )(*args)
        if last:
            return tuple(result)
        res, direction, mapped, corrected, buf, to_left, to_right, part, coef = result


def solution(mesh):
    placed = (P("row", "col"), P(), P(), P())
    return jax.shard_map(
        shards,
        mesh=mesh,
        in_specs=placed,
        out_specs=(P("row", "col"), P("row", "col")),
        check_vma=False,
    )
```

time: 959 us -> 172 us (0.18); the launches traced: 943 us -> 171 us
  waiting for transfers between devices: 351 us -> 24.6 us
  blocking collectives: 212 us -> 39.7 us
  starting transfers between devices: 169 us -> 73.6 us
  local copies, waits for them, and re-layouts: 85.2 us -> 17.7 us
  other arithmetic: 60.4 us -> 0.33 us
  matrix products: 44.7 us -> 0 us
  Pallas kernels: 0 us -> 13.9 us
  loops' own time: 12 us -> 0 us
    ppermute x24 -> x16, waiting for transfers between devices: 351 us -> 17.6 us  [shift(): lax.ppermute(value, axis, pairs if forward else [(b, a) for a, b in pairs])]
    psum x5 -> x0, blocking collectives: 212 us -> none  [the longest x3 125 us: squares(): return lax.psum(jnp.sum(residual * residual), ('row', 'col'))]
    ppermute x24 -> x16, starting transfers between devices: 169 us -> 55.8 us  [shift(): lax.ppermute(value, axis, pairs if forward else [(b, a) for a, b in pairs])]
    dot_general x48 -> x0, matrix products: 44.7 us -> none  [matmul(): jnp.dot(left, right, precision=lax.Precision.HIGHEST, preferred_element_t...]
    all_to_all x0 -> x2, blocking collectives: none -> 39.7 us  [shards(): parts = lax.all_to_all(part, ('row', 'col'), 0, 0, tiled=True)]
    scatter-add x18 -> x0, local copies, waits for them, and re-layouts: 28.5 us -> none  [the longest x3 7.95 us: fold_spill(): result.at[:width_h, block_w - width_h:]]
    all_to_all x0 -> x1, starting transfers between devices: none -> 17.7 us  [shards(): parts = lax.all_to_all(part, ('row', 'col'), 0, 0, tiled=True)]
    slice x16 -> x2, local copies, waits for them, and re-layouts: 17.9 us -> 1.37 us  [the longest x1 1.36 us: shards(): from_right = shift(observed[:, :THIRD], 'col', False)]
  transfers between devices with their start and end apart: 24 -> 17, of which waited for: 13 -> 9; matrix products, arithmetic and copies ran while one was open for 9% -> 1% of each run, Pallas kernels for 0% -> 0%
where the time goes in v1:
time: 172 us; the launch traced here: 171 us
  starting transfers between devices  73.6 us (43%)
  blocking collectives  39.7 us (23%)
  waiting for transfers between devices  24.6 us (14%)
  local copies, waits for them, and re-layouts  17.7 us (10%)
  Pallas kernels  13.9 us (8%)
    ppermute x16, starting transfers between devices, shift(): lax.ppermute(value, axis, pairs if forward else [(b, a) for a, b in pairs])  55.8 us
    all_to_all x2, blocking collectives, shards(): parts = lax.all_to_all(part, ('row', 'col'), 0, 0, tiled=True)  39.7 us
    all_to_all x1, starting transfers between devices, shards(): parts = lax.all_to_all(part, ('row', 'col'), 0, 0, tiled=True)  17.7 us
    ppermute x16, waiting for transfers between devices, shift(): lax.ppermute(value, axis, pairs if forward else [(b, a) for a, b in pairs])  17.6 us
    unnamed x73, local copies, waits for them, and re-layouts  15.5 us
    pallas_call x3, Pallas kernels, shards(): pl.pallas_call(functools.partial(next_kernel, first, last, tile_count), o...  11.5 us
    all_to_all x1, waiting for transfers between devices, shards(): parts = lax.all_to_all(part, ('row', 'col'), 0, 0, tiled=True)  6.99 us
  transfers between devices with their start and end apart: 17, of which 9 were waited for; matrix products, arithmetic and copies ran while one was open for 1% of the time, Pallas kernels for 0%

profile of v1, /device:TPU:0, one launch (start us, length us, event | category | flops | bytes accessed | tf_op | source)
XLA Modules:
  0.0 171.0 jit_solution(3552294306071649033)
XLA Ops:
  0.6 1.4 fusion.1
  2.0 1.3 collective-permute-start.1
  3.3 3.1 %collective-permute-start = (f32[1024,128]{1,0:T(8,128)S(1)}, f32[1024,128]{1,0:T(8,128)S(1)}, u32[]{:S(2)}, u32[]{:S(2)}) collective-permute-start(f32[1024,128]{1,0:T(8,128)S(1)} %get-tuple-element.65), channel_id=1, source_target_pairs={{0,1},{1,2},{2,3},{3,4},{4,5},{5,6},{6,7},{8,9},{9,10},{10,11},{11... | collective-permute-start | bytes 1572872 | tf_op jit(solution)/shard_map/ppermute | solution.py:425
  6.4 1.0 copy.17
  7.5 0.3 collective-permute-done.from_left
  7.9 0.8 copy-done.28
  8.7 4.9 %collective-permute-start.2 = (f32[64,384]{1,0:T(8,128)S(1)}, f32[64,384]{1,0:T(8,128)S(1)}, u32[]{:S(2)}, u32[]{:S(2)}) collective-permute-start(f32[64,384]{1,0:T(8,128)S(1)} %pad_maximum_fusion), channel_id=1, source_target_pairs={{0,8},{8,16},{16,24},{1,9},{9,17},{17,25},{2,10},{10,18},{18,26},{... | collective-permute-start | bytes 294920 | tf_op jit(solution)/shard_map/ppermute | solution.py:425
  13.6 0.0 copy-start.2
  13.6 0.0 copy-start.3
  13.6 0.0 copy-start.8
  13.7 0.0 copy-start.10
  13.7 0.0 copy-start.16
  13.7 0.0 copy-start.18
  13.7 0.0 copy-start.20
  13.7 0.0 copy-start.22
  13.7 1.4 collective-permute-start.3
  15.2 0.8 dynamic-slice_bitcast_fusion
  16.0 1.0 copy-done.30
  17.0 1.0 copy-done.31
  18.0 0.6 shard_map.149.spec_ref.refs_9_.refs_13_
  18.6 1.8 %collective-permute-done.3.below = f32[64,384]{1,0:T(8,128)S(1)} collective-permute-done((f32[64,384]{1,0:T(8,128)S(1)}, f32[64,384]{1,0:T(8,128)S(1)}, u32[]{:S(2)}, u32[]{:S(2)}) %collective-permute-start.3) | collective-permute-done | bytes 98336 | tf_op jit(solution)/shard_map/ppermute | solution.py:425
  20.5 1.8 %shard_map.150 = (f32[1152,384]{1,0:T(8,128)S(1)}, f32[1152,384]{1,0:T(8,128)S(1)}, f32[1152,128]{1,0:T(8,128)S(1)}, f32[1152,128]{1,0:T(8,128)S(1)}, f32[32,128]{1,0:T(8,128)}) custom-call(s32[4]{0:T(128)S(1)} %get-tuple-element.79.occ.refs_0_, f32[1024,256]{1,0:T(8,128)S(1)} %copy-done.1, f32[1024,128]{1,0:T(8,128)S(1)} %copy-done.29, ...), custom_call_target="tpu_custom_call" | custom-call | tf_op jit(solution)/shard_map/pallas_call | solution.py:450
  22.3 0.0 copy-start.11
  22.3 0.0 copy-start.17
  22.3 0.0 copy-start.19
  22.3 0.0 copy-start.21
  22.4 0.0 copy-start.23
  22.4 9.1 %collective-permute-start.4 = (f32[1152,128]{1,0:T(8,128)S(1)}, f32[1152,128]{1,0:T(8,128)S(1)}, u32[]{:S(2)}, u32[]{:S(2)}) collective-permute-start(f32[1152,128]{1,0:T(8,128)S(1)} %get-tuple-element.27), channel_id=1, source_target_pairs={{0,1},{1,2},{2,3},{3,4},{4,5},{5,6},{6,7},{8,9},{9,10},{10,11},{11... | collective-permute-start | bytes 1769480 | tf_op jit(solution)/shard_map/ppermute | solution.py:425
  31.4 1.3 collective-permute-start.5
  32.7 0.3 collective-permute-done.4.refs_4_
  33.0 6.2 %collective-permute-done.5.refs_5_ = f32[1152,128]{1,0:T(8,128)S(1)} collective-permute-done((f32[1152,128]{1,0:T(8,128)S(1)}, f32[1152,128]{1,0:T(8,128)S(1)}, u32[]{:S(2)}, u32[]{:S(2)}) %collective-permute-start.5) | collective-permute-done | bytes 589856 | tf_op jit(solution)/shard_map/ppermute | solution.py:425
  39.3 0.8 copy-done.24
  40.2 1.3 copy-done.5
  41.4 1.3 collective-permute-start.7
  42.7 8.9 %collective-permute-start.6 = (f32[128,384]{1,0:T(8,128)S(1)}, f32[128,384]{1,0:T(8,128)S(1)}, u32[]{:S(2)}, u32[]{:S(2)}) collective-permute-start(f32[128,384]{1,0:T(8,128)S(1)} %get-tuple-element.53), channel_id=1, source_target_pairs={{0,8},{8,16},{16,24},{1,9},{9,17},{17,25},{2,10},{10,18},{18,26},{... | collective-permute-start | bytes 589832 | tf_op jit(solution)/shard_map/ppermute | solution.py:425
  51.7 17.7 %all-to-all-start = ((f32[32,1,128]{2,1,0:T(1,128)}), f32[32,1,128]{2,1,0:T(1,128)S(1)}, u32[]{:S(2)}, u32[]{:S(2)}) async-start(f32[32,1,128]{2,1,0:T(1,128)} %bitcast.7), calls=%async_computation | async-start | bytes 32768 | tf_op jit(solution)/shard_map/all_to_all | solution.py:464
  69.4 0.1 add_convert_fusion.refs_1_
  69.5 7.0 %all-to-all-done = f32[32,1,128]{2,1,0:T(1,128)S(1)} async-done(((f32[32,1,128]{2,1,0:T(1,128)}), f32[32,1,128]{2,1,0:T(1,128)S(1)}, u32[]{:S(2)}, u32[]{:S(2)}) %all-to-all-start) | async-done | bytes 16416 | tf_op jit(solution)/shard_map/all_to_all | solution.py:464
  76.5 0.7 copy-done.32
  77.2 0.7 copy-done.34
  77.9 1.5 copy-done.6
  79.4 1.1 copy-done.25
  80.4 0.9 copy-done.33
  81.4 0.9 copy-done.35
  82.3 3.4 %shard_map.151 = (f32[1152,384]{1,0:T(8,128)S(1)}, f32[1152,384]{1,0:T(8,128)S(1)}, f32[1152,384]{1,0:T(8,128)S(1)}, f32[1024,256]{1,0:T(8,128)S(1)}, f32[1152,3...) custom-call(s32[4]{0:T(128)S(1)} %get-tuple-element.79.occ.refs_0_, ...), custom_call_target="tpu_custom_call" | custom-call | tf_op jit(solution)/shard_map/pallas_call | solution.py:485
  85.7 1.3 copy-done.13
  87.0 1.2 copy-done.14
  88.2 1.3 copy-done.15
  89.5 3.4 %collective-permute-start.8 = (f32[1152,128]{1,0:T(8,128)S(1)}, f32[1152,128]{1,0:T(8,128)S(1)}, u32[]{:S(2)}, u32[]{:S(2)}) collective-permute-start(f32[1152,128]{1,0:T(8,128)S(1)} %get-tuple-element.33), channel_id=1, source_target_pairs={{0,1},{1,2},{2,3},{3,4},{4,5},{5,6},{6,7},{8,9},{9,10},{10,11},{11... | collective-permute-start | bytes 1769480 | tf_op jit(solution)/shard_map/ppermute | solution.py:425
  92.8 1.3 collective-permute-start.9
  94.1 0.3 collective-permute-done.8.refs_5_
  94.4 4.2 %collective-permute-done.9.refs_6_ = f32[1152,128]{1,0:T(8,128)S(1)} collective-permute-done((f32[1152,128]{1,0:T(8,128)S(1)}, f32[1152,128]{1,0:T(8,128)S(1)}, u32[]{:S(2)}, u32[]{:S(2)}) %collective-permute-start.9) | collective-permute-done | bytes 589856 | tf_op jit(solution)/shard_map/ppermute | solution.py:425
  98.7 1.3 collective-permute-start.11
  100.0 6.3 %collective-permute-start.10 = (f32[128,384]{1,0:T(8,128)S(1)}, f32[128,384]{1,0:T(8,128)S(1)}, u32[]{:S(2)}, u32[]{:S(2)}) collective-permute-start(f32[128,384]{1,0:T(8,128)S(1)} %get-tuple-element.51), channel_id=1, source_target_pairs={{0,8},{8,16},{16,24},{1,9},{9,17},{17,25},{2,10},{10,18},{18,26},{... | collective-permute-start | bytes 589832 | tf_op jit(solution)/shard_map/ppermute | solution.py:425
  106.3 19.9 %all_to_all.33 = f32[32,1,128]{2,1,0:T(1,128)S(1)} all-to-all(f32[32,1,128]{2,1,0:T(1,128)S(1)} %bitcast.24), channel_id=1, replica_groups=mesh['row'=4,'col'=8] {'row','col'}, dimensions={0} | all-to-all | bytes 32768 | tf_op jit(solution)/shard_map/all_to_all | solution.py:464
  126.1 5.5 %shard_map.152 = (f32[1152,384]{1,0:T(8,128)S(1)}, f32[1152,384]{1,0:T(8,128)S(1)}, f32[1152,384]{1,0:T(8,128)S(1)}, f32[1024,256]{1,0:T(8,128)S(1)}, f32[1152,3...) custom-call(s32[4]{0:T(128)S(1)} %get-tuple-element.79.occ.refs_0_, ...), custom_call_target="tpu_custom_call" | custom-call | tf_op jit(solution)/shard_map/pallas_call | solution.py:485
  131.6 3.4 %collective-permute-start.12 = (f32[1152,128]{1,0:T(8,128)S(1)}, f32[1152,128]{1,0:T(8,128)S(1)}, u32[]{:S(2)}, u32[]{:S(2)}) collective-permute-start(f32[1152,128]{1,0:T(8,128)S(1)} %get-tuple-element.42), channel_id=1, source_target_pairs={{0,1},{1,2},{2,3},{3,4},{4,5},{5,6},{6,7},{8,9},{9,10},{10,11},{11... | collective-permute-start | bytes 1769480 | tf_op jit(solution)/shard_map/ppermute | solution.py:425
  135.0 1.3 collective-permute-start.13
  136.3 0.3 collective-permute-done.12.refs_5_
  136.6 4.2 %collective-permute-done.13.refs_6_ = f32[1152,128]{1,0:T(8,128)S(1)} collective-permute-done((f32[1152,128]{1,0:T(8,128)S(1)}, f32[1152,128]{1,0:T(8,128)S(1)}, u32[]{:S(2)}, u32[]{:S(2)}) %collective-permute-start.13) | collective-permute-done | bytes 589856 | tf_op jit(solution)/shard_map/ppermute | solution.py:425
  140.9 1.3 collective-permute-start.15
  142.2 6.3 %collective-permute-start.14 = (f32[128,384]{1,0:T(8,128)S(1)}, f32[128,384]{1,0:T(8,128)S(1)}, u32[]{:S(2)}, u32[]{:S(2)}) collective-permute-start(f32[128,384]{1,0:T(8,128)S(1)} %get-tuple-element.49), channel_id=1, source_target_pairs={{0,8},{8,16},{16,24},{1,9},{9,17},{17,25},{2,10},{10,18},{18,26},{... | collective-permute-start | bytes 589832 | tf_op jit(solution)/shard_map/ppermute | solution.py:425
  148.5 19.9 %all_to_all.34 = f32[32,1,128]{2,1,0:T(1,128)S(1)} all-to-all(f32[32,1,128]{2,1,0:T(1,128)S(1)} %bitcast.23), channel_id=1, replica_groups=mesh['row'=4,'col'=8] {'row','col'}, dimensions={0} | all-to-all | bytes 32768 | tf_op jit(solution)/shard_map/all_to_all | solution.py:464
  168.3 2.6 %shard_map.153 = (f32[1024,256]{1,0:T(8,128)}, f32[1024,256]{1,0:T(8,128)}) custom-call(s32[4]{0:T(128)S(1)} %get-tuple-element.79.occ.refs_0_, s32[4]{0:T(128)S(1)} %add_convert_fusion.refs_1_, f32[32,128]{1,0:T(8,128)S(1)} %bitcast.22, f32[8,128]{1,0:T(8,128)S(1)} %get-tuple-element.40.refs_3_, f32[1152,384]{1,0:T(8,128)S(1)} %get-tuple-element.41.refs_4_, ...), custom_call_target="tpu_custom_call" | custom-call | tf_op jit(solution)/shard_map/pallas_call | solution.py:485
  (65 shorter events, 0.4 us)
Async XLA Ops:
  0.6 6.8 %copy-start.1 = (f32[1024,256]{1,0:T(8,128)S(1)}, f32[1024,256]{1,0:T(8,128)}, u32[]{:S(2)}) copy-start(f32[1024,256]{1,0:T(8,128)} %obs_ref.1) | copy-start | bytes 3145732
  2.0 5.5 %collective-permute-start.1 = (f32[1024,128]{1,0:T(8,128)S(1)}, f32[1024,128]{1,0:T(8,128)S(1)}, u32[]{:S(2)}, u32[]{:S(2)}) collective-permute-start(f32[1024,128]{1,0:T(8,128)S(1)} %get-tuple-element.64), channel_id=1, source_target_pairs={{1,0},{2,1},{3,2},{4,3},{5,4},{6,5},{7,6},{9,8},{10,9},{11,10},{12... | collective-permute-start | bytes 1572872 | tf_op jit(solution)/shard_map/ppermute | solution.py:425
  3.3 4.6 %collective-permute-start = (f32[1024,128]{1,0:T(8,128)S(1)}, f32[1024,128]{1,0:T(8,128)S(1)}, u32[]{:S(2)}, u32[]{:S(2)}) collective-permute-start(f32[1024,128]{1,0:T(8,128)S(1)} %get-tuple-element.65), channel_id=1, source_target_pairs={{0,1},{1,2},{2,3},{3,4},{4,5},{5,6},{6,7},{8,9},{9,10},{10,11},{11... | collective-permute-start | bytes 1572872 | tf_op jit(solution)/shard_map/ppermute | solution.py:425
  7.5 8.5 %copy-start.26 = (f32[1024,128]{1,0:T(8,128)}, f32[1024,128]{1,0:T(8,128)S(1)}, u32[]{:S(2)}) copy-start(f32[1024,128]{1,0:T(8,128)S(1)} %collective-permute-done.1.from_right) | copy-start | bytes 1572868
  7.9 0.8 copy-start.28
  8.7 9.9 %collective-permute-start.2 = (f32[64,384]{1,0:T(8,128)S(1)}, f32[64,384]{1,0:T(8,128)S(1)}, u32[]{:S(2)}, u32[]{:S(2)}) collective-permute-start(f32[64,384]{1,0:T(8,128)S(1)} %pad_maximum_fusion), channel_id=1, source_target_pairs={{0,8},{8,16},{16,24},{1,9},{9,17},{17,25},{2,10},{10,18},{18,26},{... | collective-permute-start | bytes 294920 | tf_op jit(solution)/shard_map/ppermute | solution.py:425
  13.6 6.8 %copy-start.2 = (bf16[768,256]{1,0:T(8,128)(2,1)S(1)}, bf16[768,256]{1,0:T(8,128)(2,1)}, u32[]{:S(2)}) copy-start(bf16[768,256]{1,0:T(8,128)(2,1)} %constant.74.clone.rest_1_.refs_11_.refs_15_) | copy-start | bytes 1179652
  13.6 6.8 %copy-start.3 = (bf16[768,256]{1,0:T(8,128)(2,1)S(1)}, bf16[768,256]{1,0:T(8,128)(2,1)}, u32[]{:S(2)}) copy-start(bf16[768,256]{1,0:T(8,128)(2,1)} %constant.73.clone.rest_0_.refs_10_.refs_14_) | copy-start | bytes 1179652
  13.6 6.8 %copy-start.8 = (bf16[512,256]{1,0:T(8,128)(2,1)S(1)}, bf16[512,256]{1,0:T(8,128)(2,1)}, u32[]{:S(2)}) copy-start(bf16[512,256]{1,0:T(8,128)(2,1)} %constant.78.clone.rest_5_.refs_15_.refs_19_) | copy-start | bytes 786436
  13.7 6.7 %copy-start.10 = (bf16[512,256]{1,0:T(8,128)(2,1)S(1)}, bf16[512,256]{1,0:T(8,128)(2,1)}, u32[]{:S(2)}) copy-start(bf16[512,256]{1,0:T(8,128)(2,1)} %constant.77.clone.rest_4_.refs_14_.refs_18_) | copy-start | bytes 786436
  13.7 6.7 %copy-start.16 = (bf16[256,256]{1,0:T(8,128)(2,1)S(1)}, bf16[256,256]{1,0:T(8,128)(2,1)}, u32[]{:S(2)}) copy-start(bf16[256,256]{1,0:T(8,128)(2,1)} %constant.80.clone.rest_7_.refs_17_.refs_21_) | copy-start | bytes 393220
  13.7 6.7 %copy-start.18 = (bf16[256,256]{1,0:T(8,128)(2,1)S(1)}, bf16[256,256]{1,0:T(8,128)(2,1)}, u32[]{:S(2)}) copy-start(bf16[256,256]{1,0:T(8,128)(2,1)} %constant.79.clone.rest_6_.refs_16_.refs_20_) | copy-start | bytes 393220
  13.7 6.7 %copy-start.20 = (bf16[256,256]{1,0:T(8,128)(2,1)S(1)}, bf16[256,256]{1,0:T(8,128)(2,1)}, u32[]{:S(2)}) copy-start(bf16[256,256]{1,0:T(8,128)(2,1)} %constant.76.clone.rest_3_.refs_13_.refs_17_) | copy-start | bytes 393220
  13.7 6.7 %copy-start.22 = (bf16[256,256]{1,0:T(8,128)(2,1)S(1)}, bf16[256,256]{1,0:T(8,128)(2,1)}, u32[]{:S(2)}) copy-start(bf16[256,256]{1,0:T(8,128)(2,1)} %constant.75.clone.rest_2_.refs_12_.refs_16_) | copy-start | bytes 393220
  13.7 6.7 %copy-start.29 = (f32[1024,128]{1,0:T(8,128)S(1)}, f32[1024,128]{1,0:T(8,128)}, u32[]{:S(2)}) copy-start(f32[1024,128]{1,0:T(8,128)} %copy-done.28) | copy-start | bytes 1572868
  13.7 6.6 %collective-permute-start.3 = (f32[64,384]{1,0:T(8,128)S(1)}, f32[64,384]{1,0:T(8,128)S(1)}, u32[]{:S(2)}, u32[]{:S(2)}) collective-permute-start(f32[64,384]{1,0:T(8,128)S(1)} %pad_maximum_fusion.1), channel_id=1, source_target_pairs={{8,0},{16,8},{24,16},{9,1},{17,9},{25,17},{10,2},{18,10},{26,18},{... | collective-permute-start | bytes 294920 | tf_op jit(solution)/shard_map/ppermute | solution.py:425
  16.0 1.0 copy-start.30
  17.0 1.0 copy-start.31
  18.0 2.5 %copy-start.27 = (f32[1024,128]{1,0:T(8,128)S(1)}, f32[1024,128]{1,0:T(8,128)}, u32[]{:S(2)}) copy-start(f32[1024,128]{1,0:T(8,128)} %copy-done.26) | copy-start | bytes 1572868
  18.6 3.7 %copy-start = (f32[4,2,256,256]{3,2,1,0:T(8,128)}, f32[4,2,256,256]{3,2,1,0:T(8,128)S(1)}, u32[]{:S(2)}) copy-start(f32[4,2,256,256]{3,2,1,0:T(8,128)S(1)} %shard_map.149.spec_ref.refs_9_.refs_13_) | copy-start | bytes 6291460
  22.3 17.9 %copy-start.12 = (f32[1152,384]{1,0:T(8,128)}, f32[1152,384]{1,0:T(8,128)S(1)}, u32[]{:S(2)}) copy-start(f32[1152,384]{1,0:T(8,128)S(1)} %get-tuple-element.29.refs_8_) | copy-start | bytes 5308420
  22.3 55.5 %copy-start.4 = (bf16[768,256]{1,0:T(8,128)(2,1)S(1)}, bf16[768,256]{1,0:T(8,128)(2,1)}, u32[]{:S(2)}) copy-start(bf16[768,256]{1,0:T(8,128)(2,1)} %constant.73.clone.rest_0_.refs_10_.refs_14_) | copy-start | bytes 1179652
  22.3 55.5 %copy-start.9 = (bf16[512,256]{1,0:T(8,128)(2,1)S(1)}, bf16[512,256]{1,0:T(8,128)(2,1)}, u32[]{:S(2)}) copy-start(bf16[512,256]{1,0:T(8,128)(2,1)} %constant.78.clone.rest_5_.refs_15_.refs_19_) | copy-start | bytes 786436
  22.3 55.5 %copy-start.11 = (bf16[512,256]{1,0:T(8,128)(2,1)S(1)}, bf16[512,256]{1,0:T(8,128)(2,1)}, u32[]{:S(2)}) copy-start(bf16[512,256]{1,0:T(8,128)(2,1)} %constant.77.clone.rest_4_.refs_14_.refs_18_) | copy-start | bytes 786436
  22.3 55.5 %copy-start.17 = (bf16[256,256]{1,0:T(8,128)(2,1)S(1)}, bf16[256,256]{1,0:T(8,128)(2,1)}, u32[]{:S(2)}) copy-start(bf16[256,256]{1,0:T(8,128)(2,1)} %constant.80.clone.rest_7_.refs_17_.refs_21_) | copy-start | bytes 393220
  22.3 55.5 %copy-start.19 = (bf16[256,256]{1,0:T(8,128)(2,1)S(1)}, bf16[256,256]{1,0:T(8,128)(2,1)}, u32[]{:S(2)}) copy-start(bf16[256,256]{1,0:T(8,128)(2,1)} %constant.79.clone.rest_6_.refs_16_.refs_20_) | copy-start | bytes 393220
  22.3 55.5 %copy-start.21 = (bf16[256,256]{1,0:T(8,128)(2,1)S(1)}, bf16[256,256]{1,0:T(8,128)(2,1)}, u32[]{:S(2)}) copy-start(bf16[256,256]{1,0:T(8,128)(2,1)} %constant.76.clone.rest_3_.refs_13_.refs_17_) | copy-start | bytes 393220
  22.4 55.5 %copy-start.23 = (bf16[256,256]{1,0:T(8,128)(2,1)S(1)}, bf16[256,256]{1,0:T(8,128)(2,1)}, u32[]{:S(2)}) copy-start(bf16[256,256]{1,0:T(8,128)(2,1)} %constant.75.clone.rest_2_.refs_12_.refs_16_) | copy-start | bytes 393220
  22.4 10.6 %collective-permute-start.4 = (f32[1152,128]{1,0:T(8,128)S(1)}, f32[1152,128]{1,0:T(8,128)S(1)}, u32[]{:S(2)}, u32[]{:S(2)}) collective-permute-start(f32[1152,128]{1,0:T(8,128)S(1)} %get-tuple-element.27), channel_id=1, source_target_pairs={{0,1},{1,2},{2,3},{3,4},{4,5},{5,6},{6,7},{8,9},{9,10},{10,11},{11... | collective-permute-start | bytes 1769480 | tf_op jit(solution)/shard_map/ppermute | solution.py:425
  31.4 7.8 %collective-permute-start.5 = (f32[1152,128]{1,0:T(8,128)S(1)}, f32[1152,128]{1,0:T(8,128)S(1)}, u32[]{:S(2)}, u32[]{:S(2)}) collective-permute-start(f32[1152,128]{1,0:T(8,128)S(1)} %get-tuple-element.28), channel_id=1, source_target_pairs={{1,0},{2,1},{3,2},{4,3},{5,4},{6,5},{7,6},{9,8},{10,9},{11,10},{12... | collective-permute-start | bytes 1769480 | tf_op jit(solution)/shard_map/ppermute | solution.py:425
  39.3 0.8 copy-start.24
  40.2 1.3 copy-start.5
  41.4 35.0 %collective-permute-start.7 = (f32[128,384]{1,0:T(8,128)S(1)}, f32[128,384]{1,0:T(8,128)S(1)}, u32[]{:S(2)}, u32[]{:S(2)}) collective-permute-start(f32[128,384]{1,0:T(8,128)S(1)} %get-tuple-element.52), channel_id=1, source_target_pairs={{8,0},{16,8},{24,16},{9,1},{17,9},{25,17},{10,2},{18,10},{26,18},{... | collective-permute-start | bytes 589832 | tf_op jit(solution)/shard_map/ppermute | solution.py:425
  42.7 34.4 %collective-permute-start.6 = (f32[128,384]{1,0:T(8,128)S(1)}, f32[128,384]{1,0:T(8,128)S(1)}, u32[]{:S(2)}, u32[]{:S(2)}) collective-permute-start(f32[128,384]{1,0:T(8,128)S(1)} %get-tuple-element.53), channel_id=1, source_target_pairs={{0,8},{8,16},{16,24},{1,9},{9,17},{17,25},{2,10},{10,18},{18,26},{... | collective-permute-start | bytes 589832 | tf_op jit(solution)/shard_map/ppermute | solution.py:425
  51.7 24.8 %all-to-all-start = ((f32[32,1,128]{2,1,0:T(1,128)}), f32[32,1,128]{2,1,0:T(1,128)S(1)}, u32[]{:S(2)}, u32[]{:S(2)}) async-start(f32[32,1,128]{2,1,0:T(1,128)} %bitcast.7), calls=%async_computation | async-start | bytes 32768 | tf_op jit(solution)/shard_map/all_to_all | solution.py:464
  76.5 0.7 copy-start.32
  77.2 0.7 copy-start.34
  77.9 1.5 copy-start.6
  79.4 1.1 copy-start.25
  80.4 0.9 copy-start.33
  81.4 0.9 copy-start.35
  85.7 1.3 copy-start.13
  87.0 1.2 copy-start.14
  88.2 1.3 copy-start.15
  89.5 36.7 %copy-start.7 = (f32[1152,384]{1,0:T(8,128)}, f32[1152,384]{1,0:T(8,128)S(1)}, u32[]{:S(2)}) copy-start(f32[1152,384]{1,0:T(8,128)S(1)} %get-tuple-element.32.refs_4_) | copy-start | bytes 5308420
  89.5 5.0 %collective-permute-start.8 = (f32[1152,128]{1,0:T(8,128)S(1)}, f32[1152,128]{1,0:T(8,128)S(1)}, u32[]{:S(2)}, u32[]{:S(2)}) collective-permute-start(f32[1152,128]{1,0:T(8,128)S(1)} %get-tuple-element.33), channel_id=1, source_target_pairs={{0,1},{1,2},{2,3},{3,4},{4,5},{5,6},{6,7},{8,9},{9,10},{10,11},{11... | collective-permute-start | bytes 1769480 | tf_op jit(solution)/shard_map/ppermute | solution.py:425
  92.8 5.7 %collective-permute-start.9 = (f32[1152,128]{1,0:T(8,128)S(1)}, f32[1152,128]{1,0:T(8,128)S(1)}, u32[]{:S(2)}, u32[]{:S(2)}) collective-permute-start(f32[1152,128]{1,0:T(8,128)S(1)} %get-tuple-element.34), channel_id=1, source_target_pairs={{1,0},{2,1},{3,2},{4,3},{5,4},{6,5},{7,6},{9,8},{10,9},{11,10},{12... | collective-permute-start | bytes 1769480 | tf_op jit(solution)/shard_map/ppermute | solution.py:425
  98.7 27.5 %collective-permute-start.11 = (f32[128,384]{1,0:T(8,128)S(1)}, f32[128,384]{1,0:T(8,128)S(1)}, u32[]{:S(2)}, u32[]{:S(2)}) collective-permute-start(f32[128,384]{1,0:T(8,128)S(1)} %get-tuple-element.50), channel_id=1, source_target_pairs={{8,0},{16,8},{24,16},{9,1},{17,9},{25,17},{10,2},{18,10},{26,18},{... | collective-permute-start | bytes 589832 | tf_op jit(solution)/shard_map/ppermute | solution.py:425
  100.0 26.2 %collective-permute-start.10 = (f32[128,384]{1,0:T(8,128)S(1)}, f32[128,384]{1,0:T(8,128)S(1)}, u32[]{:S(2)}, u32[]{:S(2)}) collective-permute-start(f32[128,384]{1,0:T(8,128)S(1)} %get-tuple-element.51), channel_id=1, source_target_pairs={{0,8},{8,16},{16,24},{1,9},{9,17},{17,25},{2,10},{10,18},{18,26},{... | collective-permute-start | bytes 589832 | tf_op jit(solution)/shard_map/ppermute | solution.py:425
  131.6 5.0 %collective-permute-start.12 = (f32[1152,128]{1,0:T(8,128)S(1)}, f32[1152,128]{1,0:T(8,128)S(1)}, u32[]{:S(2)}, u32[]{:S(2)}) collective-permute-start(f32[1152,128]{1,0:T(8,128)S(1)} %get-tuple-element.42), channel_id=1, source_target_pairs={{0,1},{1,2},{2,3},{3,4},{4,5},{5,6},{6,7},{8,9},{9,10},{10,11},{11... | collective-permute-start | bytes 1769480 | tf_op jit(solution)/shard_map/ppermute | solution.py:425
  135.0 5.7 %collective-permute-start.13 = (f32[1152,128]{1,0:T(8,128)S(1)}, f32[1152,128]{1,0:T(8,128)S(1)}, u32[]{:S(2)}, u32[]{:S(2)}) collective-permute-start(f32[1152,128]{1,0:T(8,128)S(1)} %get-tuple-element.43), channel_id=1, source_target_pairs={{1,0},{2,1},{3,2},{4,3},{5,4},{6,5},{7,6},{9,8},{10,9},{11,10},{12... | collective-permute-start | bytes 1769480 | tf_op jit(solution)/shard_map/ppermute | solution.py:425
  140.9 27.5 %collective-permute-start.15 = (f32[128,384]{1,0:T(8,128)S(1)}, f32[128,384]{1,0:T(8,128)S(1)}, u32[]{:S(2)}, u32[]{:S(2)}) collective-permute-start(f32[128,384]{1,0:T(8,128)S(1)} %get-tuple-element.48), channel_id=1, source_target_pairs={{8,0},{16,8},{24,16},{9,1},{17,9},{25,17},{10,2},{18,10},{26,18},{... | collective-permute-start | bytes 589832 | tf_op jit(solution)/shard_map/ppermute | solution.py:425
  142.2 26.2 %collective-permute-start.14 = (f32[128,384]{1,0:T(8,128)S(1)}, f32[128,384]{1,0:T(8,128)S(1)}, u32[]{:S(2)}, u32[]{:S(2)}) collective-permute-start(f32[128,384]{1,0:T(8,128)S(1)} %get-tuple-element.49), channel_id=1, source_target_pairs={{0,8},{8,16},{16,24},{1,9},{9,17},{17,25},{2,10},{10,18},{18,26},{... | collective-permute-start | bytes 589832 | tf_op jit(solution)/shard_map/ppermute | solution.py:425

commit v2 on v0

v2 whole, which is shorter than its diff:
```python
import functools
import math

import jax
import jax.numpy as jnp
import numpy as np
from jax import lax
from jax.experimental import pallas as pl
from jax.experimental.pallas import tpu as pltpu
from jax.sharding import PartitionSpec as P

TILE = 256
HALO = 64
KW = 65
ITERS = 3
WIN = TILE + 2 * HALO
THIRD = WIN // 3
HALF = THIRD // 2
SLOTS = 2 * THIRD
BF = jnp.bfloat16
F32 = jnp.float32


def hi_lo(table):
    high = table.astype(np.float32).astype(jnp.bfloat16)
    low = (table - high.astype(np.float64)).astype(np.float32).astype(jnp.bfloat16)
    return high, low


@functools.cache
def tables():
    spots = np.arange(THIRD)
    low_freq = 3 * np.arange(HALF)
    full = math.sqrt(2.0 / WIN)
    cos_part = np.cos(2 * np.pi * (low_freq[:, None] * spots % WIN) / WIN) * full
    sin_part = np.sin(2 * np.pi * (low_freq[:, None] * spots % WIN) / WIN) * full
    cos_part[0] = math.sqrt(1.0 / WIN)
    sin_part[0] = np.where(spots % 2 == 0, 1.0, -1.0) * math.sqrt(1.0 / WIN)
    small = np.concatenate([cos_part, sin_part])
    angle = 2 * np.pi * ((3 * spots[:, None] + 1) * spots % WIN) / WIN
    root = math.sqrt(3.0) / 2
    large = full * np.block(
        [[np.cos(angle), -root * np.sin(angle)], [np.sin(angle), root * np.cos(angle)]]
    )
    freqs = np.concatenate([low_freq, low_freq, 3 * spots + 1])
    freqs[HALF] = WIN // 2
    taps = np.arange(THIRD)
    turn = 2 * np.pi * (freqs[:, None] * taps % WIN) / WIN
    keep = (taps < KW)[None, :]
    sines = np.sin(turn)
    sines[0] = 0.0
    sines[HALF] = 0.0
    waves = np.concatenate([np.cos(turn) * keep, sines * keep])

    sh, sl = hi_lo(small)
    gh, gl = hi_lo(large)
    wh, wl = hi_lo(waves)
    return dict(
        large=np.concatenate([gh, gl]),
        large_t=np.concatenate([gh.T, gl.T]),
        small=np.concatenate([sh, sl]),
        small_t=np.concatenate([sh.T, sl.T]),
        w_left=np.concatenate([wh, wl, wh], 1),
        w_right=np.concatenate([wh.T, wl.T, wh.T], 0),
    )


NAMES = ("large", "large_t", "small", "small_t")


def split(value):
    high = value.astype(BF)
    return high, (value - high.astype(F32)).astype(BF)


def dot(left, right):
    return jnp.dot(left, right, preferred_element_type=F32)


def right_large(value, table):
    high, low = split(value)
    return dot(
        jnp.concatenate([high, high, low], 1),
        jnp.concatenate([table[...], table[:SLOTS]], 0),
    )


def right_small(value, table):
    high, low = split(value)
    coarse, fine = table[:THIRD], table[THIRD:]
    both = dot(
        jnp.concatenate([high, low], 1),
        jnp.concatenate(
            [
                jnp.concatenate([coarse, fine], 1),
                jnp.concatenate([coarse, jnp.zeros_like(fine)], 1),
            ],
            0,
        ),
    )
    return both[:, :THIRD] + both[:, THIRD:]


def left_large(value, table):
    high, low = split(value)
    both = dot(table[...], high)
    return both[:SLOTS] + both[SLOTS:] + dot(table[:SLOTS], low)


def left_small(value, table):
    high, low = split(value)
    coarse, fine = table[:THIRD], table[THIRD:]
    both = dot(
        jnp.concatenate(
            [
                jnp.concatenate([coarse, coarse], 1),
                jnp.concatenate([fine, jnp.zeros_like(fine)], 1),
            ],
            0,
        ),
        jnp.concatenate([high, low], 0),
    )
    return both[:THIRD] + both[THIRD:]


def butterfly(first, second, third):
    total = second + third
    return first + total, first - 0.5 * total, second - third


def unbutterfly(plain, real, diff):
    base = plain - 0.5 * real
    return plain + real, base + diff, base - diff


def spectra_kernel(r):
    def body(slot, carry):
        @pl.when(r.occ[slot] != 0)
        def _():
            high, low = split(r.kernels[r.kid[slot]])
            half = dot(r.w_left[...], jnp.concatenate([high, high, low], 0))
            high, low = split(half)
            quads = dot(jnp.concatenate([high, high, low], 1), r.w_right[...])
            cc = quads[:SLOTS, :SLOTS]
            cs = quads[:SLOTS, SLOTS:]
            sc = quads[SLOTS:, :SLOTS]
            ss = quads[SLOTS:, SLOTS:]
            r.spec[slot, 0] = cc * cc + ss * ss + (sc * sc + cs * cs)
            r.spec[slot, 1] = 2.0 * (sc * cs - cc * ss)

        @pl.when(r.occ[slot] == 0)
        def _():
            r.spec[slot] = jnp.zeros((2, SLOTS, SLOTS), F32)

        return carry

    lax.fori_loop(0, r.spec.shape[0], body, 0)


def tile_of(block, num):
    return block[:, num * THIRD : (num + 1) * THIRD]


def lane_mask():
    return lax.broadcasted_iota(jnp.int32, (1, THIRD), 1) < HALF


def apply_spectrum(low_rows, high_rows, spec_ref, slot):
    sign = jnp.where(lane_mask(), -1.0, 1.0).astype(F32)

    def band(cos_rows, sin_rows, cos_at, sin_at, size):
        pc = spec_ref[slot, 0, pl.ds(cos_at, size), :]
        ps = spec_ref[slot, 0, pl.ds(sin_at, size), :] if sin_at != cos_at else pc
        cross = spec_ref[slot, 1, pl.ds(cos_at, size), :]
        d0, d1 = cross[:, :THIRD] * sign, cross[:, THIRD:]
        c0, c1, c2 = (tile_of(cos_rows, i) for i in range(3))
        s0, s1, s2 = (tile_of(sin_rows, i) for i in range(3))
        new_cos = jnp.concatenate(
            [
                pc[:, :THIRD] * c0 + d0 * pltpu.roll(s0, HALF, 1),
                pc[:, THIRD:] * c1 - d1 * s2,
                pc[:, THIRD:] * c2 + d1 * s1,
            ],
            1,
        )
        new_sin = jnp.concatenate(
            [
                ps[:, :THIRD] * s0 - d0 * pltpu.roll(c0, HALF, 1),
                ps[:, THIRD:] * s1 + d1 * c2,
                ps[:, THIRD:] * s2 - d1 * c1,
            ],
            1,
        )
        return new_cos, new_sin

    low = band(low_rows[:HALF], low_rows[HALF:], 0, HALF, HALF)
    high = band(high_rows[:THIRD], high_rows[THIRD:], THIRD, THIRD, THIRD)
    return jnp.concatenate(low, 0), jnp.concatenate(high, 0)


def window_products(windows, slots, r):
    count = len(windows)
    parts = []
    for blocks in windows:
        halves = []
        for block in blocks:
            plain, real, diff = butterfly(*(tile_of(block, i) for i in range(3)))
            halves.append(
                jnp.concatenate(
                    [
                        right_small(plain, r.small_t),
                        right_large(jnp.concatenate([real, diff], 1), r.large_t),
                    ],
                    1,
                )
            )
        parts.append(butterfly(*halves))
    plain, real, diff = (jnp.concatenate([part[i] for part in parts], 1) for i in range(3))
    low_rows = left_small(plain, r.small)
    high_rows = left_large(jnp.concatenate([real, diff], 0), r.large)
    bands = []
    for num, slot in enumerate(slots):
        here = slice(num * WIN, (num + 1) * WIN)
        bands.append(apply_spectrum(low_rows[:, here], high_rows[:, here], r.spec, slot))
    low_rows, high_rows = (jnp.concatenate([band[i] for band in bands], 1) for i in range(2))
    plain = left_small(low_rows, r.small_t)
    both = left_large(high_rows, r.large_t)
    rows = unbutterfly(plain, both[:THIRD], both[THIRD:])
    results = []
    for num in range(count):
        here = slice(num * WIN, (num + 1) * WIN)
        result = []
        for block in rows:
            block = block[:, here]
            plain = right_small(block[:, :THIRD], r.small)
            both = right_large(block[:, THIRD:], r.large)
            result.append(jnp.concatenate(unbutterfly(plain, both[:, :THIRD], both[:, THIRD:]), 1))
        results.append(result)
    return results


def fold8(value):
    rows = value.reshape(value.shape[0] // 8, 8, value.shape[1]).sum(0)
    return sum(tile_of(rows, i) for i in range(value.shape[1] // THIRD))


def total(value):
    return jnp.sum(jnp.sum(value, 0, keepdims=True), 1, keepdims=True)


def lanes_of(shape, *values):
    lanes = lax.broadcasted_iota(jnp.int32, shape, 1)
    out = jnp.zeros(shape, F32)
    for num, value in enumerate(values):
        out = jnp.where(lanes == num, value, out)
    return out


def rows_at(num, count=1):
    return pl.ds(num * THIRD, count * THIRD)


def put(ref, here, tiles):
    for num, tile in enumerate(tiles):
        ref[here, pl.ds(num * THIRD, THIRD)] = tile


def own_sum(r, num):
    last = 2 * r.tiles
    terms = []
    if num <= 2:
        terms.append((r.top_sum, num))
    if 2 <= num <= last - 2:
        terms.append((r.mid_sum, num - 2))
    if num >= last - 2:
        terms.append((r.low_sum, num - last + 2))
    return terms


def scalars(r):
    sums = jnp.sum(r.parts[...], 0, keepdims=True)
    energy, curve, cross = sums[:, 0:1], sums[:, 1:2], sums[:, 2:3]
    if r.stage == 1:
        return jnp.zeros_like(energy), energy / curve, energy, curve
    ratio = energy / r.coef[0:1, 0:1]
    power = curve + ratio * (2.0 * cross + ratio * r.coef[0:1, 1:2])
    return ratio, energy / power, energy, power


def update(r, num, old_refs, here, size, offset, spill, keep):
    ratio, step = r.ratio, r.step
    low = lane_mask()
    sums = [
        ref[pl.ds(block * THIRD + offset, size), :] for ref, block in own_sum(r, num)
    ]
    wide = pl.ds(num * THIRD + offset, size)
    west, east = r.from_left[wide, :], r.from_right[wide, :]
    add = [
        jnp.where(low, west, 0.0),
        jnp.where(low, 0.0, east),
        jnp.where(low, east, west),
    ]
    for block in sums + ([] if spill is None else [spill]):
        add = [a + tile_of(block, i) for i, a in enumerate(add)]
    old_res, old_dir, old_map, old_cor = old_refs
    old = old_res[here, :]
    direct = [tile_of(old, i) for i in range(3)]
    mapped = [a + b for a, b in zip(add, direct)]
    mapped[2] = mapped[2] * jnp.where(low, r.edge[3].astype(F32), r.edge[2].astype(F32))
    if keep is not None:
        mapped = [a * keep for a in mapped]
    fresh = list(direct)
    if r.stage > 1:
        past, was = old_map[here, :], old_dir[here, :]
        mapped = [a + ratio * tile_of(past, i) for i, a in enumerate(mapped)]
        direct = [a + ratio * tile_of(was, i) for i, a in enumerate(direct)]
    fresh = [a - step * b for a, b in zip(fresh, mapped)]
    return fresh, direct, mapped


def corrected_tiles(r, old_cor, here, direct):
    moved = [r.step * a for a in direct[:2]]
    if r.stage == 1:
        return moved
    old = old_cor[here, :]
    return [tile_of(old, i) + a for i, a in enumerate(moved)]


def store_state(r, name, here, fresh, direct, mapped):
    put(getattr(r, "res_" + name + "_new"), here, fresh)
    put(getattr(r, "map_" + name + "_new"), here, mapped)
    if r.stage > 1:
        put(getattr(r, "dir_" + name + "_new"), here, direct)


def old_of(r, name):
    return tuple(getattr(r, part + name, None) for part in ("res_", "dir_", "map_", "cor_"))


def unpacked_sides(r, start, size):
    half = r.side_left.shape[0]
    low = lane_mask()
    out = []
    while size:
        upper = start < half
        count = min(size, half - start) if upper else size
        here = pl.ds(start if upper else start - half, count)
        right, left = r.side_right[here, :], r.side_left[here, :]
        if upper:
            left = pltpu.roll(left, HALF, 1)
        else:
            right = pltpu.roll(right, HALF, 1)
        out.append(jnp.where(low, right, left))
        start, size = start + count, size - count
    return out[0] if len(out) == 1 else jnp.concatenate(out, 0)


def initial(r, start, size):
    here = pl.ds(start, size)
    block = r.observed[here, :]
    return [tile_of(block, 0), tile_of(block, 1), unpacked_sides(r, start, size)]


def pack_kernel(r):
    half = r.to_left.shape[0]
    low = lane_mask()
    first = [r.observed[pl.ds(start, half), pl.ds(0, THIRD)] for start in (0, half)]
    second = [r.observed[pl.ds(start, half), pl.ds(THIRD, THIRD)] for start in (0, half)]
    r.to_left[...] = jnp.where(low, first[0], pltpu.roll(first[1], HALF, 1))
    r.to_right[...] = jnp.where(low, pltpu.roll(second[0], HALF, 1), second[1])


def halo_kernel(r):
    put(r.to_up, pl.ds(0, HALO), initial(r, 0, HALO))
    put(r.to_down, pl.ds(0, HALO), initial(r, r.observed.shape[0] - HALO, HALO))


def row_strip_kernel(r):
    low = lane_mask()
    blocks = 2 * r.tiles + 1
    size = r.to_up.shape[0]
    for side, out in ((0, r.to_up), (1, r.to_down)):
        own = (r.top_sum, r.low_sum)[side][pl.ds(side * (WIN - size), size), :]
        if r.narrow:
            here = pl.ds(side * (blocks * HALO - size), size)
            west, east = r.from_left[here, :], r.from_right[here, :]
            if side:
                west = pltpu.roll(west, HALF, 1)
            else:
                east = pltpu.roll(east, HALF, 1)
            add = [jnp.where(low, west, 0.0), jnp.where(low, 0.0, east)]
        else:
            here = pl.ds(side * (blocks * THIRD - size), size)
            west, east = r.from_left[here, :], r.from_right[here, :]
            add = [
                jnp.where(low, west, 0.0),
                jnp.where(low, 0.0, east),
                jnp.where(low, east, west),
            ]
        put(out, pl.ds(0, size), [tile_of(own, i) + a for i, a in enumerate(add)])


def middle_kernel(r):
    square = cross = jnp.zeros((8, THIRD), F32)
    blocks = 2 * r.tiles + 1
    if r.stage > 0:
        r.ratio, r.step, _, _ = scalars(r)
    for num in range(1, blocks - 1):
        here = rows_at(num - 1)
        if r.stage == 0:
            fresh = initial(r, num * THIRD - HALO, THIRD)
            put(r.res_mid_new, here, fresh)
        else:
            fresh, direct, mapped = update(r, num, old_of(r, "mid"), here, THIRD, 0, None, None)
            store_state(r, "mid", here, fresh, direct, mapped)
            put(r.cor_mid_new, here, corrected_tiles(r, old_of(r, "mid")[3], here, direct))
            cross += sum(fold8(a * b) for a, b in zip(fresh[:2], mapped))
        square += sum(fold8(a * a) for a in fresh[:2])
    r.acc[0] = square
    r.acc[1] = cross
    r.acc[2] = jnp.zeros((8, THIRD), F32)
    inner = list(range(1, r.tiles - 1))
    some = r.occ[inner[0]]
    for slot in inner[1:]:
        some = some + r.occ[slot]

    @pl.when(some != 0)
    def _():
        windows = [
            [r.res_mid_new[rows_at(2 * slot + i - 1), :] for i in range(3)] for slot in inner
        ]
        results = window_products(windows, inner, r)
        curve = jnp.zeros((8, THIRD), F32)
        for num, (window, result) in enumerate(zip(windows, results)):
            curve += sum(fold8(a * b) for a, b in zip(window, result))
            first = result[0] if num == 0 else result[0] + results[num - 1][2]
            r.mid_sum_new[rows_at(2 * num), :] = first
            r.mid_sum_new[rows_at(2 * num + 1), :] = result[1]
        r.mid_sum_new[rows_at(2 * len(inner)), :] = results[-1][2]
        r.acc[2] = curve

    @pl.when(some == 0)
    def _():
        r.mid_sum_new[...] = jnp.zeros(r.mid_sum_new.shape, F32)


def edge_kernel(r):
    square, cross = r.acc[0], r.acc[1]
    blocks = 2 * r.tiles + 1
    rows = 2 * r.tiles * THIRD
    if r.stage > 0:
        r.ratio, r.step, energy, power = scalars(r)
        r.coef_new[...] = lanes_of((8, THIRD), energy, power)
    for side in range(2):
        num = side * (blocks - 1)
        for offset in (0, HALO):
            here = pl.ds(side * THIRD + offset, HALO)
            inside = (offset > 0) == (side == 0)
            if r.stage == 0:
                if inside:
                    fresh = initial(r, side * (rows - HALO), HALO)
                else:
                    halo = (r.above, r.below)[side][...]
                    fresh = [tile_of(halo, i) for i in range(3)]
                put(r.res_edge_new, here, fresh)
            else:
                spill = (r.above, r.below)[side][pl.ds(offset, HALO), :]
                keep = None if inside else r.edge[side].astype(F32)
                fresh, direct, mapped = update(
                    r, num, old_of(r, "edge"), here, HALO, offset, spill, keep
                )
                store_state(r, "edge", here, fresh, direct, mapped)
                if inside:
                    there = pl.ds(side * HALO, HALO)
                    put(r.cor_edge_new, there, corrected_tiles(r, old_of(r, "edge")[3], there, direct))
                    cross += sum(fold8(a * b) for a, b in zip(fresh[:2], mapped))
            if inside:
                square += sum(fold8(a * a) for a in fresh[:2])
    slots = [0, r.tiles - 1]
    some = r.occ[slots[0]] + r.occ[slots[1]]

    @pl.when(some != 0)
    def _():
        far = blocks - 4
        windows = [
            [r.res_edge_new[rows_at(0), :]] + [r.res_mid_new[rows_at(i), :] for i in range(2)],
            [r.res_mid_new[rows_at(far + i), :] for i in range(2)] + [r.res_edge_new[rows_at(1), :]],
        ]
        results = window_products(windows, slots, r)
        curve = jnp.zeros((8, THIRD), F32)
        for window, result, ref in zip(windows, results, (r.top_sum_new, r.low_sum_new)):
            curve += sum(fold8(a * b) for a, b in zip(window, result))
            for num in range(3):
                ref[rows_at(num), :] = result[num]
        r.curve[...] = curve

    @pl.when(some == 0)
    def _():
        r.top_sum_new[...] = jnp.zeros((WIN, WIN), F32)
        r.low_sum_new[...] = jnp.zeros((WIN, WIN), F32)
        r.curve[...] = jnp.zeros((8, THIRD), F32)

    low = lane_mask()
    new = Refs(tiles=r.tiles, top_sum=r.top_sum_new, mid_sum=r.mid_sum_new, low_sum=r.low_sum_new)
    if r.narrow:
        half = blocks * HALO
        for start in range(0, half, HALO):
            pair = []
            for row in (start, start + half):
                terms = [
                    ref[pl.ds(block * THIRD + row % THIRD, HALO), pl.ds(2 * THIRD, THIRD)]
                    for ref, block in own_sum(new, row // THIRD)
                ]
                pair.append(sum(terms[1:], terms[0]))
            here = pl.ds(start, HALO)
            r.to_right[here, :] = jnp.where(low, pair[0], pltpu.roll(pair[1], HALF, 1))
            r.to_left[here, :] = jnp.where(low, pltpu.roll(pair[0], HALF, 1), pair[1])
    else:
        for num in range(blocks):
            terms = [ref[rows_at(block), :] for ref, block in own_sum(new, num)]
            block = sum(terms[1:], terms[0])
            r.to_left[rows_at(num), :] = jnp.where(low, tile_of(block, 0), tile_of(block, 2))
            r.to_right[rows_at(num), :] = jnp.where(low, tile_of(block, 2), tile_of(block, 1))
    gamma = total(square)
    curve = gamma + total(r.acc[2] + r.curve[...])
    r.part[...] = lanes_of(r.part.shape, gamma, curve, total(cross))


def last_kernel(r):
    blocks = 2 * r.tiles + 1
    half = blocks * HALO
    r.ratio, r.step, _, _ = scalars(r)
    low = lane_mask()
    for start in range(HALO, 2 * half - HALO, HALO):
        num, offset = start // THIRD, start % THIRD
        upper = start < half
        wide = pl.ds(start if upper else start - half, HALO)
        west, east = r.from_left[wide, :], r.from_right[wide, :]
        if upper:
            east = pltpu.roll(east, HALF, 1)
        else:
            west = pltpu.roll(west, HALF, 1)
        add = [jnp.where(low, west, 0.0), jnp.where(low, 0.0, east)]
        for ref, block in own_sum(r, num):
            there = pl.ds(block * THIRD + offset, HALO)
            add = [a + ref[there, pl.ds(i * THIRD, THIRD)] for i, a in enumerate(add)]
        if start == HALO:
            add = [a + r.above[:, pl.ds(i * THIRD, THIRD)] for i, a in enumerate(add)]
        if start == 2 * half - 2 * HALO:
            add = [a + r.below[:, pl.ds(i * THIRD, THIRD)] for i, a in enumerate(add)]
        if num == 0 or num == blocks - 1:
            side = 0 if num == 0 else 1
            old, here, there = old_of(r, "edge"), pl.ds(side * THIRD + offset, HALO), pl.ds(side * HALO, HALO)
        else:
            old, here = old_of(r, "mid"), pl.ds(start - THIRD, HALO)
            there = here
        for i, a in enumerate(add):
            lanes = pl.ds(i * THIRD, THIRD)
            res = old[0][here, lanes]
            direct = res + r.ratio * old[1][here, lanes]
            mapped = a + res + r.ratio * old[2][here, lanes]
            out = pl.ds(start - HALO, HALO)
            r.corrected[out, lanes] = old[3][there, lanes] + r.step * direct
            r.residual[out, lanes] = res - r.step * mapped


class Refs:
    def __init__(self, **names):
        self.__dict__.update(names)


SCALARS = ("occ", "kid", "edge")
PARAMS = pltpu.CompilerParams(vmem_limit_bytes=16 * 1024 * 1024)


def run(body, ins, outs, scratch=None, **static):
    scratch = scratch or {}
    names = [*ins, *outs, *scratch]

    def kernel(*refs):
        body(Refs(**static, **dict(zip(names, refs))))

    result = pl.pallas_call(
        kernel,
        name=body.__name__,
        out_shape=[jax.ShapeDtypeStruct(dims, F32) for dims in outs.values()],
        in_specs=[
            pl.BlockSpec(memory_space=pltpu.SMEM if name in SCALARS else pltpu.VMEM) for name in ins
        ],
        out_specs=[pl.BlockSpec(memory_space=pltpu.VMEM)] * len(outs),
        scratch_shapes=[pltpu.VMEM(dims, F32) for dims in scratch.values()],
        compiler_params=PARAMS,
    )(*ins.values())
    return dict(zip(outs, result))


def own_part(table, tile_count):
    column = lax.dynamic_index_in_dim(table, lax.axis_index("col"), 1, keepdims=False)
    return lax.dynamic_slice_in_dim(column, lax.axis_index("row") * tile_count, tile_count)


def shift(value, axis, forward):
    count = lax.axis_size(axis)
    pairs = [(i, i + 1) for i in range(count - 1)]
    return lax.ppermute(value, axis, pairs if forward else [(b, a) for a, b in pairs])


def shards(observed, kernels, occupied, kernel_index):
    rows, cols = observed.shape
    tiles = rows // TILE
    half, mid, ext = rows // 2, rows - 2 * HALO, rows + 2 * HALO
    n_row, n_col = lax.axis_size("row"), lax.axis_size("col")
    devices = n_row * n_col
    my_row, my_col = lax.axis_index("row"), lax.axis_index("col")
    occ = own_part(occupied, tiles)
    edge = jnp.stack([my_row > 0, my_row < n_row - 1, my_col > 0, my_col < n_col - 1])
    host = {name: jnp.asarray(table) for name, table in tables().items()}
    sent = run(pack_kernel, dict(observed=observed), dict(to_left=(half, THIRD), to_right=(half, THIRD)))
    side_left = shift(sent["to_right"], "col", True)
    side_right = shift(sent["to_left"], "col", False)
    spec = run(
        spectra_kernel,
        dict(
            kid=own_part(kernel_index, tiles),
            occ=occ,
            kernels=jnp.pad(kernels, ((0, 0), (0, THIRD - KW), (0, THIRD - KW))),
            w_left=host["w_left"],
            w_right=host["w_right"],
        ),
        dict(spec=(tiles, 2, SLOTS, SLOTS)),
    )["spec"]
    side_left, side_right, spec, edge = lax.optimization_barrier(
        (side_left, side_right, spec, edge.astype(jnp.int32))
    )
    sides = dict(observed=observed, side_left=side_left, side_right=side_right)
    sent = run(halo_kernel, sides, dict(to_up=(HALO, WIN), to_down=(HALO, WIN)))
    above = shift(sent["to_down"], "row", True)
    below = shift(sent["to_up"], "row", False)
    fixed = dict(occ=occ, spec=spec, **{name: host[name] for name in NAMES})
    state = {}
    for stage in range(ITERS):
        narrow = stage == ITERS - 1
        moving = dict(sides) if stage == 0 else dict(from_left=from_left, from_right=from_right, parts=parts)
        if stage:
            moving["edge"] = edge
            if stage > 1:
                moving["coef"] = state["coef"]

        def old(names, where):
            parts_of = ["res_", "dir_", "map_", "cor_"] if stage > 1 else ["res_"] if stage else []
            return {name: state[name] for name in [a + where for a in parts_of] + (names if stage else [])}

        def new(where, height, cor_height):
            out = {"res_" + where + "_new": (height, WIN)}
            if stage:
                out["map_" + where + "_new"] = (height, WIN)
                out["cor_" + where + "_new"] = (cor_height, TILE)
            if stage > 1:
                out["dir_" + where + "_new"] = (height, WIN)
            return out

        sums = ["top_sum", "mid_sum", "low_sum"]
        middle = run(
            middle_kernel,
            {**fixed, **moving, **old(sums, "mid")},
            {**new("mid", mid, mid), "mid_sum_new": (mid - TILE, WIN), "acc": (3, 8, THIRD)},
            stage=stage,
            tiles=tiles,
        )
        outs = {**new("edge", TILE, THIRD), "top_sum_new": (WIN, WIN), "low_sum_new": (WIN, WIN)}
        strip = (ext // 2 if narrow else ext, THIRD)
        outs.update(to_left=strip, to_right=strip, part=(devices, THIRD))
        if stage:
            outs["coef_new"] = (8, THIRD)
        edges = run(
            edge_kernel,
            {
                **fixed,
                **moving,
                **old(["top_sum", "low_sum"], "edge"),
                "above": above,
                "below": below,
                **{name: middle[name] for name in ("res_mid_new", "mid_sum_new", "acc")},
            },
            outs,
            dict(curve=(8, THIRD)),
            stage=stage,
            tiles=tiles,
            narrow=narrow,
        )
        fresh = {**middle, **edges}
        if stage == 1:
            state["dir_mid"], state["dir_edge"] = state["res_mid"], state["res_edge"]
        for name, value in fresh.items():
            if name.endswith("_new"):
                state[name[:-4]] = value
        from_left = shift(edges["to_right"], "col", True)
        from_right = shift(edges["to_left"], "col", False)
        parts = lax.all_to_all(edges["part"], ("row", "col"), 0, 0, tiled=True)
        from_left, from_right, parts = lax.optimization_barrier((from_left, from_right, parts))

        strip = (HALO, TILE) if narrow else (THIRD, WIN)
        sent = run(
            row_strip_kernel,
            dict(
                from_left=from_left,
                from_right=from_right,
                top_sum=state["top_sum"],
                low_sum=state["low_sum"],
            ),
            dict(to_up=strip, to_down=strip),
            tiles=tiles,
            narrow=narrow,
        )
        above = shift(sent["to_down"], "row", True)
        below = shift(sent["to_up"], "row", False)

    names = [a + b for b in ("mid", "edge") for a in ("res_", "dir_", "map_", "cor_")]
    out = run(
        last_kernel,
        dict(
            parts=parts,
            from_left=from_left,
            from_right=from_right,
            above=above,
            below=below,
            **{name: state[name] for name in names + ["coef", "top_sum", "mid_sum", "low_sum"]},
        ),
        dict(corrected=(rows, cols), residual=(rows, cols)),
        stage=ITERS,
        tiles=tiles,
    )
    return out["corrected"], out["residual"]


def solution(mesh):
    placed = (P("row", "col"), P(), P(), P())
    return jax.shard_map(
        shards,
        mesh=mesh,
        in_specs=placed,
        out_specs=(P("row", "col"), P("row", "col")),
        check_vma=False,
    )
```

time: 959 us -> 123 us (0.13); the launches traced: 943 us -> 122 us
  waiting for transfers between devices: 351 us -> 21.5 us
  blocking collectives: 212 us -> 48.3 us
  starting transfers between devices: 169 us -> 37.4 us
  local copies, waits for them, and re-layouts: 85.2 us -> 3.09 us
  other arithmetic: 60.4 us -> 0.08 us
  matrix products: 44.7 us -> 0 us
  loops' own time: 12 us -> 0 us
  Pallas kernels: 0 us -> 10.9 us
    ppermute x24 -> x16, waiting for transfers between devices: 351 us -> 21.5 us  [shift(): lax.ppermute(value, axis, pairs if forward else [(b, a) for a, b in pairs])]
    psum x5 -> x0, blocking collectives: 212 us -> none  [the longest x3 125 us: squares(): return lax.psum(jnp.sum(residual * residual), ('row', 'col'))]
    ppermute x24 -> x16, starting transfers between devices: 169 us -> 37.4 us  [shift(): lax.ppermute(value, axis, pairs if forward else [(b, a) for a, b in pairs])]
    all_to_all x0 -> x3, blocking collectives: none -> 48.3 us  [shards(): parts = lax.all_to_all(edges['part'], ('row', 'col'), 0, 0, tiled=True)]
    dot_general x48 -> x0, matrix products: 44.7 us -> none  [matmul(): jnp.dot(left, right, precision=lax.Precision.HIGHEST, preferred_element_t...]
    scatter-add x18 -> x0, local copies, waits for them, and re-layouts: 28.5 us -> none  [the longest x3 7.95 us: fold_spill(): result.at[:width_h, block_w - width_h:]]
    unnamed x81 -> x17, local copies, waits for them, and re-layouts: 21.5 us -> 2.27 us
    slice x16 -> x0, local copies, waits for them, and re-layouts: 17.9 us -> none  [the longest x9 10.1 us: padded(): lax.slice_in_dim(block, 0, width, axis=dim)]
  transfers between devices with their start and end apart: 24 -> 16, of which waited for: 13 -> 8; matrix products, arithmetic and copies ran while one was open for 9% -> 2% of each run, Pallas kernels for 0% -> 4%
where the time goes in v2:
time: 123 us; the launch traced here: 122 us
  blocking collectives  48.3 us (39%)
  starting transfers between devices  37.4 us (30%)
  waiting for transfers between devices  21.5 us (17%)
  Pallas kernels  10.9 us (9%)
  local copies, waits for them, and re-layouts  3.09 us (3%)
    all_to_all x3, blocking collectives, shards(): parts = lax.all_to_all(edges['part'], ('row', 'col'), 0, 0, tiled=True)  48.3 us
    ppermute x16, starting transfers between devices, shift(): lax.ppermute(value, axis, pairs if forward else [(b, a) for a, b in pairs])  37.4 us
    ppermute x16, waiting for transfers between devices, shift(): lax.ppermute(value, axis, pairs if forward else [(b, a) for a, b in pairs])  21.5 us
    pallas_call x13, Pallas kernels, run(): pl.pallas_call(kernel, name=body.__name__, out_shape=[jax.ShapeDtypeStruc...  10.9 us
  transfers between devices with their start and end apart: 16, of which 8 were waited for; matrix products, arithmetic and copies ran while one was open for 2% of the time, Pallas kernels for 4%

profile of v2, /device:TPU:0, one launch (start us, length us, event | category | flops | bytes accessed | tf_op | source)
XLA Modules:
  0.0 122.2 jit_solution(3832055778156728923)
XLA Ops:
  0.6 0.0 copy-start
  0.6 1.2 copy-done
  1.9 0.0 copy-start.6
  1.9 0.0 copy-start.7
  1.9 0.2 pack_kernel.1
  2.1 2.5 %collective-permute-start = (f32[512,128]{1,0:T(8,128)S(1)}, f32[512,128]{1,0:T(8,128)S(1)}, u32[]{:S(2)}, u32[]{:S(2)}) collective-permute-start(f32[512,128]{1,0:T(8,128)S(1)} %get-tuple-element.64), channel_id=1, source_target_pairs={{0,1},{1,2},{2,3},{3,4},{4,5},{5,6},{6,7},{8,9},{9,10},{10,11},{11... | collective-permute-start | bytes 786440 | tf_op jit(solution)/shard_map/ppermute | solution.py:605
  4.6 1.3 %collective-permute-start.1 = (f32[512,128]{1,0:T(8,128)S(1)}, f32[512,128]{1,0:T(8,128)S(1)}, u32[]{:S(2)}, u32[]{:S(2)}) collective-permute-start(f32[512,128]{1,0:T(8,128)S(1)} %get-tuple-element.65), channel_id=1, source_target_pairs={{1,0},{2,1},{3,2},{4,3},{5,4},{6,5},{7,6},{9,8},{10,9},{11,10},{12... | collective-permute-start | bytes 786440 | tf_op jit(solution)/shard_map/ppermute | solution.py:605
  5.9 1.0 copy.13
  7.0 0.8 dynamic-slice_bitcast_fusion
  7.7 0.0 copy-done.6
  7.7 0.0 copy-done.7
  7.8 0.8 spectra_kernel.1.refs_1_
  8.5 0.0 copy-start.2
  8.5 0.0 copy-start.3
  8.5 0.0 copy-start.4
  8.6 0.0 copy-start.5
  8.6 0.1 add_convert_fusion.refs_9_
  8.6 0.0 collective-permute-done.refs_1_.refs_7_
  8.7 1.4 %collective-permute-done.1.refs_2_.refs_8_ = f32[512,128]{1,0:T(8,128)S(1)} collective-permute-done((f32[512,128]{1,0:T(8,128)S(1)}, f32[512,128]{1,0:T(8,128)S(1)}, u32[]{:S(2)}, u32[]{:S(2)}) %collective-permute-start.1) | collective-permute-done | bytes 262176 | tf_op jit(solution)/shard_map/ppermute | solution.py:605
  10.1 0.0 copy-done.1
  10.1 0.1 halo_kernel.1
  10.2 3.5 %collective-permute-start.2 = (f32[64,384]{1,0:T(8,128)S(1)}, f32[64,384]{1,0:T(8,128)S(1)}, u32[]{:S(2)}, u32[]{:S(2)}) collective-permute-start(f32[64,384]{1,0:T(8,128)S(1)} %get-tuple-element.69), channel_id=1, source_target_pairs={{0,8},{8,16},{16,24},{1,9},{9,17},{17,25},{2,10},{10,18},{18,26},{... | collective-permute-start | bytes 294920 | tf_op jit(solution)/shard_map/ppermute | solution.py:605
  13.7 1.3 %collective-permute-start.3 = (f32[64,384]{1,0:T(8,128)S(1)}, f32[64,384]{1,0:T(8,128)S(1)}, u32[]{:S(2)}, u32[]{:S(2)}) collective-permute-start(f32[64,384]{1,0:T(8,128)S(1)} %get-tuple-element.70), channel_id=1, source_target_pairs={{8,0},{16,8},{24,16},{9,1},{17,9},{25,17},{10,2},{18,10},{26,18},{... | collective-permute-start | bytes 294920 | tf_op jit(solution)/shard_map/ppermute | solution.py:605
  15.0 0.0 copy-done.2
  15.0 0.0 copy-done.3
  15.0 0.0 copy-done.4
  15.0 0.0 copy-done.5
  15.0 0.8 middle_kernel.3
  15.9 0.0 collective-permute-done.2.refs_9_
  15.9 4.4 %collective-permute-done.3.refs_10_ = f32[64,384]{1,0:T(8,128)S(1)} collective-permute-done((f32[64,384]{1,0:T(8,128)S(1)}, f32[64,384]{1,0:T(8,128)S(1)}, u32[]{:S(2)}, u32[]{:S(2)}) %collective-permute-start.3) | collective-permute-done | bytes 98336 | tf_op jit(solution)/shard_map/ppermute | solution.py:605
  20.3 0.8 edge_kernel.3
  21.1 5.3 %collective-permute-start.4 = (f32[1152,128]{1,0:T(8,128)S(1)}, f32[1152,128]{1,0:T(8,128)S(1)}, u32[]{:S(2)}, u32[]{:S(2)}) collective-permute-start(f32[1152,128]{1,0:T(8,128)S(1)} %get-tuple-element.74), channel_id=1, source_target_pairs={{0,1},{1,2},{2,3},{3,4},{4,5},{5,6},{6,7},{8,9},{9,10},{10,11},{11... | collective-permute-start | bytes 1769480 | tf_op jit(solution)/shard_map/ppermute | solution.py:605
  26.4 1.3 %collective-permute-start.5 = (f32[1152,128]{1,0:T(8,128)S(1)}, f32[1152,128]{1,0:T(8,128)S(1)}, u32[]{:S(2)}, u32[]{:S(2)}) collective-permute-start(f32[1152,128]{1,0:T(8,128)S(1)} %get-tuple-element.75), channel_id=1, source_target_pairs={{1,0},{2,1},{3,2},{4,3},{5,4},{6,5},{7,6},{9,8},{10,9},{11,10},{12... | collective-permute-start | bytes 1769480 | tf_op jit(solution)/shard_map/ppermute | solution.py:605
  27.7 17.7 %all_to_all.36 = f32[32,1,128]{2,1,0:T(1,128)S(1)} all-to-all(f32[32,1,128]{2,1,0:T(1,128)S(1)} %bitcast.27), channel_id=1, replica_groups=mesh['row'=4,'col'=8] {'row','col'}, dimensions={0} | all-to-all | bytes 32768 | tf_op jit(solution)/shard_map/all_to_all | solution.py:699
  45.4 0.0 collective-permute-done.4.refs_0_.refs_6_
  45.4 0.0 collective-permute-done.5.refs_1_.refs_7_
  45.5 5.3 %collective-permute-start.6 = (f32[128,384]{1,0:T(8,128)S(1)}, f32[128,384]{1,0:T(8,128)S(1)}, u32[]{:S(2)}, u32[]{:S(2)}) collective-permute-start(f32[128,384]{1,0:T(8,128)S(1)} %get-tuple-element.84), channel_id=1, source_target_pairs={{0,8},{8,16},{16,24},{1,9},{9,17},{17,25},{2,10},{10,18},{18,26},{... | collective-permute-start | bytes 589832 | tf_op jit(solution)/shard_map/ppermute | solution.py:605
  50.7 1.3 %collective-permute-start.7 = (f32[128,384]{1,0:T(8,128)S(1)}, f32[128,384]{1,0:T(8,128)S(1)}, u32[]{:S(2)}, u32[]{:S(2)}) collective-permute-start(f32[128,384]{1,0:T(8,128)S(1)} %get-tuple-element.85), channel_id=1, source_target_pairs={{8,0},{16,8},{24,16},{9,1},{17,9},{25,17},{10,2},{18,10},{26,18},{... | collective-permute-start | bytes 589832 | tf_op jit(solution)/shard_map/ppermute | solution.py:605
  52.0 1.4 %middle_kernel.4 = (f32[896,384]{1,0:T(8,128)S(1)}, f32[896,384]{1,0:T(8,128)S(1)}, f32[896,256]{1,0:T(8,128)S(1)}, f32[640,384]{1,0:T(8,128)S(1)}, f32[3,8,128]{2,1,0:T(8,128)S(1)}) custom-call(s32[4]{0:T(128)S(1)} %get-tuple-element.127.refs_1_.refs_0_, f32[4,2,256,256]{3,2,1,0:T(8,128)S(1)} %spectra_kernel.1.refs_1_, bf16[512,256]{1,0:T(8,128)(2,1)S(1)} %copy-done.3, ...), custom_call_target="tpu_custom_call" | custom-call | tf_op jit(solution)/shard_map/middle_kernel/pallas_call | solution.py:583
  53.4 1.5 %collective-permute-done.6.refs_13_ = f32[128,384]{1,0:T(8,128)S(1)} collective-permute-done((f32[128,384]{1,0:T(8,128)S(1)}, f32[128,384]{1,0:T(8,128)S(1)}, u32[]{:S(2)}, u32[]{:S(2)}) %collective-permute-start.6) | collective-permute-done | bytes 196640 | tf_op jit(solution)/shard_map/ppermute | solution.py:605
  54.9 4.1 %collective-permute-done.7.refs_14_ = f32[128,384]{1,0:T(8,128)S(1)} collective-permute-done((f32[128,384]{1,0:T(8,128)S(1)}, f32[128,384]{1,0:T(8,128)S(1)}, u32[]{:S(2)}, u32[]{:S(2)}) %collective-permute-start.7) | collective-permute-done | bytes 196640 | tf_op jit(solution)/shard_map/ppermute | solution.py:605
  59.0 1.1 edge_kernel.4
  60.2 1.3 %collective-permute-start.8 = (f32[1152,128]{1,0:T(8,128)S(1)}, f32[1152,128]{1,0:T(8,128)S(1)}, u32[]{:S(2)}, u32[]{:S(2)}) collective-permute-start(f32[1152,128]{1,0:T(8,128)S(1)} %get-tuple-element.89), channel_id=1, source_target_pairs={{0,1},{1,2},{2,3},{3,4},{4,5},{5,6},{6,7},{8,9},{9,10},{10,11},{11... | collective-permute-start | bytes 1769480 | tf_op jit(solution)/shard_map/ppermute | solution.py:605
  61.5 1.3 %collective-permute-start.9 = (f32[1152,128]{1,0:T(8,128)S(1)}, f32[1152,128]{1,0:T(8,128)S(1)}, u32[]{:S(2)}, u32[]{:S(2)}) collective-permute-start(f32[1152,128]{1,0:T(8,128)S(1)} %get-tuple-element.90), channel_id=1, source_target_pairs={{1,0},{2,1},{3,2},{4,3},{5,4},{6,5},{7,6},{9,8},{10,9},{11,10},{12... | collective-permute-start | bytes 1769480 | tf_op jit(solution)/shard_map/ppermute | solution.py:605
  62.8 15.8 %all_to_all.37 = f32[32,1,128]{2,1,0:T(1,128)S(1)} all-to-all(f32[32,1,128]{2,1,0:T(1,128)S(1)} %bitcast.26), channel_id=1, replica_groups=mesh['row'=4,'col'=8] {'row','col'}, dimensions={0} | all-to-all | bytes 32768 | tf_op jit(solution)/shard_map/all_to_all | solution.py:699
  78.6 0.0 collective-permute-done.8.refs_0_.refs_6_
  78.6 0.0 collective-permute-done.9.refs_1_.refs_7_
  78.7 5.5 %collective-permute-start.10 = (f32[128,384]{1,0:T(8,128)S(1)}, f32[128,384]{1,0:T(8,128)S(1)}, u32[]{:S(2)}, u32[]{:S(2)}) collective-permute-start(f32[128,384]{1,0:T(8,128)S(1)} %get-tuple-element.101), channel_id=1, source_target_pairs={{0,8},{8,16},{16,24},{1,9},{9,17},{17,25},{2,10},{10,18},{18,26},{... | collective-permute-start | bytes 589832 | tf_op jit(solution)/shard_map/ppermute | solution.py:605
  84.2 1.3 %collective-permute-start.11 = (f32[128,384]{1,0:T(8,128)S(1)}, f32[128,384]{1,0:T(8,128)S(1)}, u32[]{:S(2)}, u32[]{:S(2)}) collective-permute-start(f32[128,384]{1,0:T(8,128)S(1)} %get-tuple-element.102), channel_id=1, source_target_pairs={{8,0},{16,8},{24,16},{9,1},{17,9},{25,17},{10,2},{18,10},{26,18},{... | collective-permute-start | bytes 589832 | tf_op jit(solution)/shard_map/ppermute | solution.py:605
  85.5 2.0 %middle_kernel.5 = (f32[896,384]{1,0:T(8,128)S(1)}, f32[896,384]{1,0:T(8,128)S(1)}, f32[896,256]{1,0:T(8,128)S(1)}, f32[896,384]{1,0:T(8,128)S(1)}, f32[640,384]{1,0:T(8,128)S(1)}, /*index=5*/f32[3,8,128]{2,1,0:T(8,128)S(1)}) custom-call(s32[4]{0:T(128)S(1)} %get-tuple-element.127.refs_1_.refs_0_, f32[4,2,256,256]{3,2,1,0:T(8,128)S(1)} %spectra_kernel.1.refs_1_, ...), custom_call_target="tpu_custom_call" | custom-call | tf_op jit(solution)/shard_map/middle_kernel/pallas_call | solution.py:583
  87.4 0.9 collective-permute-done.10.refs_17_
  88.4 4.1 %collective-permute-done.11.refs_18_ = f32[128,384]{1,0:T(8,128)S(1)} collective-permute-done((f32[128,384]{1,0:T(8,128)S(1)}, f32[128,384]{1,0:T(8,128)S(1)}, u32[]{:S(2)}, u32[]{:S(2)}) %collective-permute-start.11) | collective-permute-done | bytes 196640 | tf_op jit(solution)/shard_map/ppermute | solution.py:605
  92.5 1.4 %edge_kernel.5 = (f32[256,384]{1,0:T(8,128)S(1)}, f32[256,384]{1,0:T(8,128)S(1)}, f32[128,256]{1,0:T(8,128)S(1)}, f32[256,384]{1,0:T(8,128)S(1)}, f32[384,384]{1...) custom-call(s32[4]{0:T(128)S(1)} %get-tuple-element.127.refs_1_.refs, ...), custom_call_target="tpu_custom_call" | custom-call | tf_op jit(solution)/shard_map/edge_kernel/pallas_call | solution.py:583
  93.9 1.3 %collective-permute-start.12 = (f32[576,128]{1,0:T(8,128)S(1)}, f32[576,128]{1,0:T(8,128)S(1)}, u32[]{:S(2)}, u32[]{:S(2)}) collective-permute-start(f32[576,128]{1,0:T(8,128)S(1)} %get-tuple-element.108), channel_id=1, source_target_pairs={{0,1},{1,2},{2,3},{3,4},{4,5},{5,6},{6,7},{8,9},{9,10},{10,11},{11... | collective-permute-start | bytes 884744 | tf_op jit(solution)/shard_map/ppermute | solution.py:605
  95.2 1.3 %collective-permute-start.13 = (f32[576,128]{1,0:T(8,128)S(1)}, f32[576,128]{1,0:T(8,128)S(1)}, u32[]{:S(2)}, u32[]{:S(2)}) collective-permute-start(f32[576,128]{1,0:T(8,128)S(1)} %get-tuple-element.109), channel_id=1, source_target_pairs={{1,0},{2,1},{3,2},{4,3},{5,4},{6,5},{7,6},{9,8},{10,9},{11,10},{12... | collective-permute-start | bytes 884744 | tf_op jit(solution)/shard_map/ppermute | solution.py:605
  96.5 14.8 %all_to_all.38 = f32[32,1,128]{2,1,0:T(1,128)S(1)} all-to-all(f32[32,1,128]{2,1,0:T(1,128)S(1)} %bitcast.25), channel_id=1, replica_groups=mesh['row'=4,'col'=8] {'row','col'}, dimensions={0} | all-to-all | bytes 32768 | tf_op jit(solution)/shard_map/all_to_all | solution.py:699
  111.3 0.0 collective-permute-done.12.refs_0_.refs_1_
  111.3 0.0 collective-permute-done.13.refs_1_.refs_2_
  111.3 0.1 row_strip_kernel.5
  111.4 2.5 %collective-permute-start.14 = (f32[64,256]{1,0:T(8,128)S(1)}, f32[64,256]{1,0:T(8,128)S(1)}, u32[]{:S(2)}, u32[]{:S(2)}) collective-permute-start(f32[64,256]{1,0:T(8,128)S(1)} %get-tuple-element.116), channel_id=1, source_target_pairs={{0,8},{8,16},{16,24},{1,9},{9,17},{17,25},{2,10},{10,18},{18,26},{... | collective-permute-start | bytes 196616 | tf_op jit(solution)/shard_map/ppermute | solution.py:605
  113.9 1.3 %collective-permute-start.15 = (f32[64,256]{1,0:T(8,128)S(1)}, f32[64,256]{1,0:T(8,128)S(1)}, u32[]{:S(2)}, u32[]{:S(2)}) collective-permute-start(f32[64,256]{1,0:T(8,128)S(1)} %get-tuple-element.117), channel_id=1, source_target_pairs={{8,0},{16,8},{24,16},{9,1},{17,9},{25,17},{10,2},{18,10},{26,18},{... | collective-permute-start | bytes 196616 | tf_op jit(solution)/shard_map/ppermute | solution.py:605
  115.2 0.6 collective-permute-done.14.refs_3_
  115.8 4.3 %collective-permute-done.15.refs_4_ = f32[64,256]{1,0:T(8,128)S(1)} collective-permute-done((f32[64,256]{1,0:T(8,128)S(1)}, f32[64,256]{1,0:T(8,128)S(1)}, u32[]{:S(2)}, u32[]{:S(2)}) %collective-permute-start.15) | collective-permute-done | bytes 65568 | tf_op jit(solution)/shard_map/ppermute | solution.py:605
  120.0 2.2 %last_kernel.1 = (f32[1024,256]{1,0:T(8,128)}, f32[1024,256]{1,0:T(8,128)}) custom-call(f32[32,128]{1,0:T(8,128)S(1)} %bitcast.24, f32[576,128]{1,0:T(8,128)S(1)} %collective-permute-done.12.refs_0_.refs_1_, f32[576,128]{1,0:T(8,128)S(1)} %collective-permute-done.13.refs_1_.refs_2_, f32[64,256]{1,0:T(8,128)S(1)} %collective-permute-done.14.refs_3_, ...), custom_call_target="tpu_custom_call" | custom-call | tf_op jit(solution)/shard_map/last_kernel/pallas_call | solution.py:583
  (4 shorter events, 0.1 us)
Async XLA Ops:
  0.6 1.2 %copy-start = (f32[1024,256]{1,0:T(8,128)S(1)}, f32[1024,256]{1,0:T(8,128)}, u32[]{:S(2)}) copy-start(f32[1024,256]{1,0:T(8,128)} %refs_6_.3) | copy-start | bytes 3145732
  1.9 5.9 %copy-start.6 = (bf16[384,512]{1,0:T(8,128)(2,1)S(1)}, bf16[384,512]{1,0:T(8,128)(2,1)}, u32[]{:S(2)}) copy-start(bf16[384,512]{1,0:T(8,128)(2,1)} %constant.67.clone.refs_4_) | copy-start | bytes 1179652
  1.9 5.9 %copy-start.7 = (bf16[512,384]{1,0:T(8,128)(2,1)S(1)}, bf16[512,384]{1,0:T(8,128)(2,1)}, u32[]{:S(2)}) copy-start(bf16[512,384]{1,0:T(8,128)(2,1)} %constant.66.clone.refs_3_) | copy-start | bytes 1179652
  2.1 6.6 %collective-permute-start = (f32[512,128]{1,0:T(8,128)S(1)}, f32[512,128]{1,0:T(8,128)S(1)}, u32[]{:S(2)}, u32[]{:S(2)}) collective-permute-start(f32[512,128]{1,0:T(8,128)S(1)} %get-tuple-element.64), channel_id=1, source_target_pairs={{0,1},{1,2},{2,3},{3,4},{4,5},{5,6},{6,7},{8,9},{9,10},{10,11},{11... | collective-permute-start | bytes 786440 | tf_op jit(solution)/shard_map/ppermute | solution.py:605
  4.6 5.5 %collective-permute-start.1 = (f32[512,128]{1,0:T(8,128)S(1)}, f32[512,128]{1,0:T(8,128)S(1)}, u32[]{:S(2)}, u32[]{:S(2)}) collective-permute-start(f32[512,128]{1,0:T(8,128)S(1)} %get-tuple-element.65), channel_id=1, source_target_pairs={{1,0},{2,1},{3,2},{4,3},{5,4},{6,5},{7,6},{9,8},{10,9},{11,10},{12... | collective-permute-start | bytes 786440 | tf_op jit(solution)/shard_map/ppermute | solution.py:605
  7.8 2.4 %copy-start.1 = (f32[1024,256]{1,0:T(8,128)S(1)}, f32[1024,256]{1,0:T(8,128)}, u32[]{:S(2)}) copy-start(f32[1024,256]{1,0:T(8,128)} %refs_6_.3) | copy-start | bytes 3145732
  8.5 6.5 %copy-start.2 = (bf16[512,256]{1,0:T(8,128)(2,1)S(1)}, bf16[512,256]{1,0:T(8,128)(2,1)}, u32[]{:S(2)}) copy-start(bf16[512,256]{1,0:T(8,128)(2,1)} %constant.63.clone.refs_3_) | copy-start | bytes 786436
  8.5 6.5 %copy-start.3 = (bf16[512,256]{1,0:T(8,128)(2,1)S(1)}, bf16[512,256]{1,0:T(8,128)(2,1)}, u32[]{:S(2)}) copy-start(bf16[512,256]{1,0:T(8,128)(2,1)} %constant.62.clone.refs_2_) | copy-start | bytes 786436
  8.5 6.5 %copy-start.4 = (bf16[256,128]{1,0:T(8,128)(2,1)S(1)}, bf16[256,128]{1,0:T(8,128)(2,1)}, u32[]{:S(2)}) copy-start(bf16[256,128]{1,0:T(8,128)(2,1)} %constant.65.clone.refs_5_) | copy-start | bytes 196612
  8.6 6.5 %copy-start.5 = (bf16[256,128]{1,0:T(8,128)(2,1)S(1)}, bf16[256,128]{1,0:T(8,128)(2,1)}, u32[]{:S(2)}) copy-start(bf16[256,128]{1,0:T(8,128)(2,1)} %constant.64.clone.refs_4_) | copy-start | bytes 196612
  10.2 5.7 %collective-permute-start.2 = (f32[64,384]{1,0:T(8,128)S(1)}, f32[64,384]{1,0:T(8,128)S(1)}, u32[]{:S(2)}, u32[]{:S(2)}) collective-permute-start(f32[64,384]{1,0:T(8,128)S(1)} %get-tuple-element.69), channel_id=1, source_target_pairs={{0,8},{8,16},{16,24},{1,9},{9,17},{17,25},{2,10},{10,18},{18,26},{... | collective-permute-start | bytes 294920 | tf_op jit(solution)/shard_map/ppermute | solution.py:605
  13.7 6.6 %collective-permute-start.3 = (f32[64,384]{1,0:T(8,128)S(1)}, f32[64,384]{1,0:T(8,128)S(1)}, u32[]{:S(2)}, u32[]{:S(2)}) collective-permute-start(f32[64,384]{1,0:T(8,128)S(1)} %get-tuple-element.70), channel_id=1, source_target_pairs={{8,0},{16,8},{24,16},{9,1},{17,9},{25,17},{10,2},{18,10},{26,18},{... | collective-permute-start | bytes 294920 | tf_op jit(solution)/shard_map/ppermute | solution.py:605
  21.1 24.3 %collective-permute-start.4 = (f32[1152,128]{1,0:T(8,128)S(1)}, f32[1152,128]{1,0:T(8,128)S(1)}, u32[]{:S(2)}, u32[]{:S(2)}) collective-permute-start(f32[1152,128]{1,0:T(8,128)S(1)} %get-tuple-element.74), channel_id=1, source_target_pairs={{0,1},{1,2},{2,3},{3,4},{4,5},{5,6},{6,7},{8,9},{9,10},{10,11},{11... | collective-permute-start | bytes 1769480 | tf_op jit(solution)/shard_map/ppermute | solution.py:605
  26.4 19.0 %collective-permute-start.5 = (f32[1152,128]{1,0:T(8,128)S(1)}, f32[1152,128]{1,0:T(8,128)S(1)}, u32[]{:S(2)}, u32[]{:S(2)}) collective-permute-start(f32[1152,128]{1,0:T(8,128)S(1)} %get-tuple-element.75), channel_id=1, source_target_pairs={{1,0},{2,1},{3,2},{4,3},{5,4},{6,5},{7,6},{9,8},{10,9},{11,10},{12... | collective-permute-start | bytes 1769480 | tf_op jit(solution)/shard_map/ppermute | solution.py:605
  45.5 9.5 %collective-permute-start.6 = (f32[128,384]{1,0:T(8,128)S(1)}, f32[128,384]{1,0:T(8,128)S(1)}, u32[]{:S(2)}, u32[]{:S(2)}) collective-permute-start(f32[128,384]{1,0:T(8,128)S(1)} %get-tuple-element.84), channel_id=1, source_target_pairs={{0,8},{8,16},{16,24},{1,9},{9,17},{17,25},{2,10},{10,18},{18,26},{... | collective-permute-start | bytes 589832 | tf_op jit(solution)/shard_map/ppermute | solution.py:605
  50.7 8.3 %collective-permute-start.7 = (f32[128,384]{1,0:T(8,128)S(1)}, f32[128,384]{1,0:T(8,128)S(1)}, u32[]{:S(2)}, u32[]{:S(2)}) collective-permute-start(f32[128,384]{1,0:T(8,128)S(1)} %get-tuple-element.85), channel_id=1, source_target_pairs={{8,0},{16,8},{24,16},{9,1},{17,9},{25,17},{10,2},{18,10},{26,18},{... | collective-permute-start | bytes 589832 | tf_op jit(solution)/shard_map/ppermute | solution.py:605
  60.2 18.5 %collective-permute-start.8 = (f32[1152,128]{1,0:T(8,128)S(1)}, f32[1152,128]{1,0:T(8,128)S(1)}, u32[]{:S(2)}, u32[]{:S(2)}) collective-permute-start(f32[1152,128]{1,0:T(8,128)S(1)} %get-tuple-element.89), channel_id=1, source_target_pairs={{0,1},{1,2},{2,3},{3,4},{4,5},{5,6},{6,7},{8,9},{9,10},{10,11},{11... | collective-permute-start | bytes 1769480 | tf_op jit(solution)/shard_map/ppermute | solution.py:605
  61.5 17.1 %collective-permute-start.9 = (f32[1152,128]{1,0:T(8,128)S(1)}, f32[1152,128]{1,0:T(8,128)S(1)}, u32[]{:S(2)}, u32[]{:S(2)}) collective-permute-start(f32[1152,128]{1,0:T(8,128)S(1)} %get-tuple-element.90), channel_id=1, source_target_pairs={{1,0},{2,1},{3,2},{4,3},{5,4},{6,5},{7,6},{9,8},{10,9},{11,10},{12... | collective-permute-start | bytes 1769480 | tf_op jit(solution)/shard_map/ppermute | solution.py:605
  78.7 9.7 %collective-permute-start.10 = (f32[128,384]{1,0:T(8,128)S(1)}, f32[128,384]{1,0:T(8,128)S(1)}, u32[]{:S(2)}, u32[]{:S(2)}) collective-permute-start(f32[128,384]{1,0:T(8,128)S(1)} %get-tuple-element.101), channel_id=1, source_target_pairs={{0,8},{8,16},{16,24},{1,9},{9,17},{17,25},{2,10},{10,18},{18,26},{... | collective-permute-start | bytes 589832 | tf_op jit(solution)/shard_map/ppermute | solution.py:605
  84.2 8.3 %collective-permute-start.11 = (f32[128,384]{1,0:T(8,128)S(1)}, f32[128,384]{1,0:T(8,128)S(1)}, u32[]{:S(2)}, u32[]{:S(2)}) collective-permute-start(f32[128,384]{1,0:T(8,128)S(1)} %get-tuple-element.102), channel_id=1, source_target_pairs={{8,0},{16,8},{24,16},{9,1},{17,9},{25,17},{10,2},{18,10},{26,18},{... | collective-permute-start | bytes 589832 | tf_op jit(solution)/shard_map/ppermute | solution.py:605
  93.9 17.4 %collective-permute-start.12 = (f32[576,128]{1,0:T(8,128)S(1)}, f32[576,128]{1,0:T(8,128)S(1)}, u32[]{:S(2)}, u32[]{:S(2)}) collective-permute-start(f32[576,128]{1,0:T(8,128)S(1)} %get-tuple-element.108), channel_id=1, source_target_pairs={{0,1},{1,2},{2,3},{3,4},{4,5},{5,6},{6,7},{8,9},{9,10},{10,11},{11... | collective-permute-start | bytes 884744 | tf_op jit(solution)/shard_map/ppermute | solution.py:605
  95.2 16.1 %collective-permute-start.13 = (f32[576,128]{1,0:T(8,128)S(1)}, f32[576,128]{1,0:T(8,128)S(1)}, u32[]{:S(2)}, u32[]{:S(2)}) collective-permute-start(f32[576,128]{1,0:T(8,128)S(1)} %get-tuple-element.109), channel_id=1, source_target_pairs={{1,0},{2,1},{3,2},{4,3},{5,4},{6,5},{7,6},{9,8},{10,9},{11,10},{12... | collective-permute-start | bytes 884744 | tf_op jit(solution)/shard_map/ppermute | solution.py:605
  111.4 4.4 %collective-permute-start.14 = (f32[64,256]{1,0:T(8,128)S(1)}, f32[64,256]{1,0:T(8,128)S(1)}, u32[]{:S(2)}, u32[]{:S(2)}) collective-permute-start(f32[64,256]{1,0:T(8,128)S(1)} %get-tuple-element.116), channel_id=1, source_target_pairs={{0,8},{8,16},{16,24},{1,9},{9,17},{17,25},{2,10},{10,18},{18,26},{... | collective-permute-start | bytes 196616 | tf_op jit(solution)/shard_map/ppermute | solution.py:605
  113.9 6.2 %collective-permute-start.15 = (f32[64,256]{1,0:T(8,128)S(1)}, f32[64,256]{1,0:T(8,128)S(1)}, u32[]{:S(2)}, u32[]{:S(2)}) collective-permute-start(f32[64,256]{1,0:T(8,128)S(1)} %get-tuple-element.117), channel_id=1, source_target_pairs={{8,0},{16,8},{24,16},{9,1},{17,9},{25,17},{10,2},{18,10},{26,18},{... | collective-permute-start | bytes 196616 | tf_op jit(solution)/shard_map/ppermute | solution.py:605

commit v3 on v2

--- a/solution.py
+++ b/solution.py
@@ -281,20 +281,50 @@
     sums = jnp.sum(r.parts[...], 0, keepdims=True)
     energy, curve, cross = sums[:, 0:1], sums[:, 1:2], sums[:, 2:3]
     if r.stage == 1:
-        return jnp.zeros_like(energy), energy / curve, energy, curve
-    ratio = energy / r.coef[0:1, 0:1]
-    power = curve + ratio * (2.0 * cross + ratio * r.coef[0:1, 1:2])
-    return ratio, energy / power, energy, power
-
-
-def update(r, num, old_refs, here, size, offset, spill, keep):
-    ratio, step = r.ratio, r.step
+        r.steps, r.ratios = [energy / curve], []
+        return energy, curve
+    past = r.coef[0:1, :]
+    ratio = energy / past[:, 0:1]
+    power = curve + ratio * (2.0 * cross + ratio * past[:, 1:2])
+    before = r.stage - 1
+    r.steps = [past[:, 2 + i : 3 + i] for i in range(before)] + [energy / power]
+    r.ratios = [past[:, 2 + ITERS + i : 3 + ITERS + i] for i in range(before - 1)] + [ratio]
+    r.back = ratio / r.steps[-2]
+    return energy, power
+
+
+def pick(odd, first, second):
+    return jnp.where(odd, first, second), jnp.where(odd, second, first)
+
+
+def from_columns(r, here):
+    return pick(r.edge[4] != 0, r.side_a[here, :], r.side_b[here, :])
+
+
+def from_rows(r, side, here):
+    return pick(r.edge[5] != 0, r.row_a[here, :], r.row_b[here, :])[side]
+
+
+def send_columns(r, here, to_left, to_right):
+    r.to_a[here, :], r.to_b[here, :] = pick(r.edge[4] != 0, to_left, to_right)
+
+
+def send_rows(r, above, below):
+    odd = r.edge[5] != 0
+    here = pl.ds(0, r.to_a.shape[0])
+    pairs = [pick(odd, a, b) for a, b in zip(above, below)]
+    put(r.to_a, here, [a for a, _ in pairs])
+    put(r.to_b, here, [b for _, b in pairs])
+
+
+def old_of(r, name):
+    return [getattr(r, "res%d_%s" % (i, name)) for i in range(r.stage)]
+
+
+def update(r, num, name, here, size, offset, spill, keep):
     low = lane_mask()
-    sums = [
-        ref[pl.ds(block * THIRD + offset, size), :] for ref, block in own_sum(r, num)
-    ]
-    wide = pl.ds(num * THIRD + offset, size)
-    west, east = r.from_left[wide, :], r.from_right[wide, :]
+    sums = [ref[pl.ds(block * THIRD + offset, size), :] for ref, block in own_sum(r, num)]
+    west, east = from_columns(r, pl.ds(num * THIRD + offset, size))
     add = [
         jnp.where(low, west, 0.0),
         jnp.where(low, 0.0, east),
@@ -302,50 +332,26 @@
     ]
     for block in sums + ([] if spill is None else [spill]):
         add = [a + tile_of(block, i) for i, a in enumerate(add)]
-    old_res, old_dir, old_map, old_cor = old_refs
-    old = old_res[here, :]
-    direct = [tile_of(old, i) for i in range(3)]
-    mapped = [a + b for a, b in zip(add, direct)]
+    olds = [ref[here, :] for ref in old_of(r, name)[-2:]]
+    old = [tile_of(olds[-1], i) for i in range(3)]
+    mapped = [a + b for a, b in zip(add, old)]
     mapped[2] = mapped[2] * jnp.where(low, r.edge[3].astype(F32), r.edge[2].astype(F32))
     if keep is not None:
         mapped = [a * keep for a in mapped]
-    fresh = list(direct)
     if r.stage > 1:
-        past, was = old_map[here, :], old_dir[here, :]
-        mapped = [a + ratio * tile_of(past, i) for i, a in enumerate(mapped)]
-        direct = [a + ratio * tile_of(was, i) for i, a in enumerate(direct)]
-    fresh = [a - step * b for a, b in zip(fresh, mapped)]
-    return fresh, direct, mapped
-
-
-def corrected_tiles(r, old_cor, here, direct):
-    moved = [r.step * a for a in direct[:2]]
-    if r.stage == 1:
-        return moved
-    old = old_cor[here, :]
-    return [tile_of(old, i) + a for i, a in enumerate(moved)]
-
-
-def store_state(r, name, here, fresh, direct, mapped):
-    put(getattr(r, "res_" + name + "_new"), here, fresh)
-    put(getattr(r, "map_" + name + "_new"), here, mapped)
-    if r.stage > 1:
-        put(getattr(r, "dir_" + name + "_new"), here, direct)
-
-
-def old_of(r, name):
-    return tuple(getattr(r, part + name, None) for part in ("res_", "dir_", "map_", "cor_"))
+        mapped = [a + r.back * (tile_of(olds[0], i) - old[i]) for i, a in enumerate(mapped)]
+    return [a - r.steps[-1] * b for a, b in zip(old, mapped)], mapped
 
 
 def unpacked_sides(r, start, size):
-    half = r.side_left.shape[0]
+    half = r.side_a.shape[0]
     low = lane_mask()
     out = []
     while size:
         upper = start < half
         count = min(size, half - start) if upper else size
         here = pl.ds(start if upper else start - half, count)
-        right, left = r.side_right[here, :], r.side_left[here, :]
+        left, right = from_columns(r, here)
         if upper:
             left = pltpu.roll(left, HALF, 1)
         else:
@@ -362,59 +368,60 @@
 
 
 def pack_kernel(r):
-    half = r.to_left.shape[0]
+    half = r.to_a.shape[0]
     low = lane_mask()
     first = [r.observed[pl.ds(start, half), pl.ds(0, THIRD)] for start in (0, half)]
     second = [r.observed[pl.ds(start, half), pl.ds(THIRD, THIRD)] for start in (0, half)]
-    r.to_left[...] = jnp.where(low, first[0], pltpu.roll(first[1], HALF, 1))
-    r.to_right[...] = jnp.where(low, pltpu.roll(second[0], HALF, 1), second[1])
+    send_columns(
+        r,
+        pl.ds(0, half),
+        jnp.where(low, first[0], pltpu.roll(first[1], HALF, 1)),
+        jnp.where(low, pltpu.roll(second[0], HALF, 1), second[1]),
+    )
 
 
 def halo_kernel(r):
-    put(r.to_up, pl.ds(0, HALO), initial(r, 0, HALO))
-    put(r.to_down, pl.ds(0, HALO), initial(r, r.observed.shape[0] - HALO, HALO))
+    send_rows(r, initial(r, 0, HALO), initial(r, r.observed.shape[0] - HALO, HALO))
 
 
 def row_strip_kernel(r):
     low = lane_mask()
     blocks = 2 * r.tiles + 1
-    size = r.to_up.shape[0]
-    for side, out in ((0, r.to_up), (1, r.to_down)):
-        own = (r.top_sum, r.low_sum)[side][pl.ds(side * (WIN - size), size), :]
+    size = r.to_a.shape[0]
+    strips = []
+    for side, ref in ((0, r.top_sum), (1, r.low_sum)):
+        own = ref[pl.ds(side * (WIN - size), size), :]
         if r.narrow:
-            here = pl.ds(side * (blocks * HALO - size), size)
-            west, east = r.from_left[here, :], r.from_right[here, :]
+            west, east = from_columns(r, pl.ds(side * (blocks * HALO - size), size))
             if side:
                 west = pltpu.roll(west, HALF, 1)
             else:
                 east = pltpu.roll(east, HALF, 1)
             add = [jnp.where(low, west, 0.0), jnp.where(low, 0.0, east)]
         else:
-            here = pl.ds(side * (blocks * THIRD - size), size)
-            west, east = r.from_left[here, :], r.from_right[here, :]
+            west, east = from_columns(r, pl.ds(side * (blocks * THIRD - size), size))
             add = [
                 jnp.where(low, west, 0.0),
                 jnp.where(low, 0.0, east),
                 jnp.where(low, east, west),
             ]
-        put(out, pl.ds(0, size), [tile_of(own, i) + a for i, a in enumerate(add)])
+        strips.append([tile_of(own, i) + a for i, a in enumerate(add)])
+    send_rows(r, *strips)
 
 
 def middle_kernel(r):
     square = cross = jnp.zeros((8, THIRD), F32)
     blocks = 2 * r.tiles + 1
     if r.stage > 0:
-        r.ratio, r.step, _, _ = scalars(r)
+        scalars(r)
     for num in range(1, blocks - 1):
         here = rows_at(num - 1)
         if r.stage == 0:
             fresh = initial(r, num * THIRD - HALO, THIRD)
-            put(r.res_mid_new, here, fresh)
         else:
-            fresh, direct, mapped = update(r, num, old_of(r, "mid"), here, THIRD, 0, None, None)
-            store_state(r, "mid", here, fresh, direct, mapped)
-            put(r.cor_mid_new, here, corrected_tiles(r, old_of(r, "mid")[3], here, direct))
+            fresh, mapped = update(r, num, "mid", here, THIRD, 0, None, None)
             cross += sum(fold8(a * b) for a, b in zip(fresh[:2], mapped))
+        put(r.res_mid_new, here, fresh)
         square += sum(fold8(a * a) for a in fresh[:2])
     r.acc[0] = square
     r.acc[1] = cross
@@ -449,8 +456,9 @@
     blocks = 2 * r.tiles + 1
     rows = 2 * r.tiles * THIRD
     if r.stage > 0:
-        r.ratio, r.step, energy, power = scalars(r)
-        r.coef_new[...] = lanes_of((8, THIRD), energy, power)
+        energy, power = scalars(r)
+        fill = [jnp.zeros_like(energy)] * (ITERS - len(r.steps))
+        r.coef_new[...] = lanes_of((8, THIRD), energy, power, *r.steps, *fill, *r.ratios)
     for side in range(2):
         num = side * (blocks - 1)
         for offset in (0, HALO):
@@ -460,20 +468,15 @@
                 if inside:
                     fresh = initial(r, side * (rows - HALO), HALO)
                 else:
-                    halo = (r.above, r.below)[side][...]
+                    halo = from_rows(r, side, pl.ds(0, HALO))
                     fresh = [tile_of(halo, i) for i in range(3)]
-                put(r.res_edge_new, here, fresh)
             else:
-                spill = (r.above, r.below)[side][pl.ds(offset, HALO), :]
+                spill = from_rows(r, side, pl.ds(offset, HALO))
                 keep = None if inside else r.edge[side].astype(F32)
-                fresh, direct, mapped = update(
-                    r, num, old_of(r, "edge"), here, HALO, offset, spill, keep
-                )
-                store_state(r, "edge", here, fresh, direct, mapped)
+                fresh, mapped = update(r, num, "edge", here, HALO, offset, spill, keep)
                 if inside:
-                    there = pl.ds(side * HALO, HALO)
-                    put(r.cor_edge_new, there, corrected_tiles(r, old_of(r, "edge")[3], there, direct))
                     cross += sum(fold8(a * b) for a, b in zip(fresh[:2], mapped))
+            put(r.res_edge_new, here, fresh)
             if inside:
                 square += sum(fold8(a * a) for a in fresh[:2])
     slots = [0, r.tiles - 1]
@@ -513,14 +516,22 @@
                 ]
                 pair.append(sum(terms[1:], terms[0]))
             here = pl.ds(start, HALO)
-            r.to_right[here, :] = jnp.where(low, pair[0], pltpu.roll(pair[1], HALF, 1))
-            r.to_left[here, :] = jnp.where(low, pltpu.roll(pair[0], HALF, 1), pair[1])
+            send_columns(
+                r,
+                here,
+                jnp.where(low, pltpu.roll(pair[0], HALF, 1), pair[1]),
+                jnp.where(low, pair[0], pltpu.roll(pair[1], HALF, 1)),
+            )
     else:
         for num in range(blocks):
             terms = [ref[rows_at(block), :] for ref, block in own_sum(new, num)]
             block = sum(terms[1:], terms[0])
-            r.to_left[rows_at(num), :] = jnp.where(low, tile_of(block, 0), tile_of(block, 2))
-            r.to_right[rows_at(num), :] = jnp.where(low, tile_of(block, 2), tile_of(block, 1))
+            send_columns(
+                r,
+                rows_at(num),
+                jnp.where(low, tile_of(block, 0), tile_of(block, 2)),
+                jnp.where(low, tile_of(block, 2), tile_of(block, 1)),
+            )
     gamma = total(square)
     curve = gamma + total(r.acc[2] + r.curve[...])
     r.part[...] = lanes_of(r.part.shape, gamma, curve, total(cross))
@@ -529,13 +540,13 @@
 def last_kernel(r):
     blocks = 2 * r.tiles + 1
     half = blocks * HALO
-    r.ratio, r.step, _, _ = scalars(r)
+    scalars(r)
     low = lane_mask()
     for start in range(HALO, 2 * half - HALO, HALO):
         num, offset = start // THIRD, start % THIRD
         upper = start < half
         wide = pl.ds(start if upper else start - half, HALO)
-        west, east = r.from_left[wide, :], r.from_right[wide, :]
+        west, east = from_columns(r, wide)
         if upper:
             east = pltpu.roll(east, HALF, 1)
         else:
@@ -544,24 +555,26 @@
         for ref, block in own_sum(r, num):
             there = pl.ds(block * THIRD + offset, HALO)
             add = [a + ref[there, pl.ds(i * THIRD, THIRD)] for i, a in enumerate(add)]
-        if start == HALO:
-            add = [a + r.above[:, pl.ds(i * THIRD, THIRD)] for i, a in enumerate(add)]
-        if start == 2 * half - 2 * HALO:
-            add = [a + r.below[:, pl.ds(i * THIRD, THIRD)] for i, a in enumerate(add)]
+        for side, edge in ((0, HALO), (1, 2 * half - 2 * HALO)):
+            if start == edge:
+                spill = from_rows(r, side, pl.ds(0, HALO))
+                add = [a + tile_of(spill, i) for i, a in enumerate(add)]
         if num == 0 or num == blocks - 1:
-            side = 0 if num == 0 else 1
-            old, here, there = old_of(r, "edge"), pl.ds(side * THIRD + offset, HALO), pl.ds(side * HALO, HALO)
+            olds, here = old_of(r, "edge"), pl.ds((0 if num == 0 else THIRD) + offset, HALO)
         else:
-            old, here = old_of(r, "mid"), pl.ds(start - THIRD, HALO)
-            there = here
+            olds, here = old_of(r, "mid"), pl.ds(start - THIRD, HALO)
         for i, a in enumerate(add):
             lanes = pl.ds(i * THIRD, THIRD)
-            res = old[0][here, lanes]
-            direct = res + r.ratio * old[1][here, lanes]
-            mapped = a + res + r.ratio * old[2][here, lanes]
+            past = [ref[here, lanes] for ref in olds]
+            direct = past[0]
+            moved = r.steps[0] * direct
+            for old, ratio, step in zip(past[1:], r.ratios, r.steps[1:]):
+                direct = old + ratio * direct
+                moved = moved + step * direct
+            mapped = a + past[-1] + r.back * (past[-2] - past[-1])
             out = pl.ds(start - HALO, HALO)
-            r.corrected[out, lanes] = old[3][there, lanes] + r.step * direct
-            r.residual[out, lanes] = res - r.step * mapped
+            r.corrected[out, lanes] = moved
+            r.residual[out, lanes] = past[-1] - r.steps[-1] * mapped
 
 
 class Refs:
@@ -599,10 +612,13 @@
     return lax.dynamic_slice_in_dim(column, lax.axis_index("row") * tile_count, tile_count)
 
 
-def shift(value, axis, forward):
+def exchange(to_a, to_b, axis):
     count = lax.axis_size(axis)
-    pairs = [(i, i + 1) for i in range(count - 1)]
-    return lax.ppermute(value, axis, pairs if forward else [(b, a) for a, b in pairs])
+    out = []
+    for value, first in ((to_b, 1), (to_a, 0)):
+        pairs = [(i, i + 1) for i in range(first, count - 1, 2)]
+        out.append(lax.ppermute(value, axis, pairs + [(b, a) for a, b in pairs]))
+    return out[1], out[0]
 
 
 def shards(observed, kernels, occupied, kernel_index):
@@ -613,11 +629,12 @@
     devices = n_row * n_col
     my_row, my_col = lax.axis_index("row"), lax.axis_index("col")
     occ = own_part(occupied, tiles)
-    edge = jnp.stack([my_row > 0, my_row < n_row - 1, my_col > 0, my_col < n_col - 1])
+    edge = jnp.stack(
+        [my_row > 0, my_row < n_row - 1, my_col > 0, my_col < n_col - 1, my_col % 2 == 1, my_row % 2 == 1]
+    ).astype(jnp.int32)
     host = {name: jnp.asarray(table) for name, table in tables().items()}
-    sent = run(pack_kernel, dict(observed=observed), dict(to_left=(half, THIRD), to_right=(half, THIRD)))
-    side_left = shift(sent["to_right"], "col", True)
-    side_right = shift(sent["to_left"], "col", False)
+    sent = run(pack_kernel, dict(edge=edge, observed=observed), dict(to_a=(half, THIRD), to_b=(half, THIRD)))
+    side_a, side_b = exchange(sent["to_a"], sent["to_b"], "col")
     spec = run(
         spectra_kernel,
         dict(
@@ -629,47 +646,36 @@
         ),
         dict(spec=(tiles, 2, SLOTS, SLOTS)),
     )["spec"]
-    side_left, side_right, spec, edge = lax.optimization_barrier(
-        (side_left, side_right, spec, edge.astype(jnp.int32))
-    )
-    sides = dict(observed=observed, side_left=side_left, side_right=side_right)
-    sent = run(halo_kernel, sides, dict(to_up=(HALO, WIN), to_down=(HALO, WIN)))
-    above = shift(sent["to_down"], "row", True)
-    below = shift(sent["to_up"], "row", False)
+    side_a, side_b, spec = lax.optimization_barrier((side_a, side_b, spec))
+    sides = dict(edge=edge, side_a=side_a, side_b=side_b)
+    sent = run(halo_kernel, dict(observed=observed, **sides), dict(to_a=(HALO, WIN), to_b=(HALO, WIN)))
+    row_a, row_b = exchange(sent["to_a"], sent["to_b"], "row")
     fixed = dict(occ=occ, spec=spec, **{name: host[name] for name in NAMES})
     state = {}
     for stage in range(ITERS):
         narrow = stage == ITERS - 1
-        moving = dict(sides) if stage == 0 else dict(from_left=from_left, from_right=from_right, parts=parts)
-        if stage:
-            moving["edge"] = edge
-            if stage > 1:
-                moving["coef"] = state["coef"]
-
-        def old(names, where):
-            parts_of = ["res_", "dir_", "map_", "cor_"] if stage > 1 else ["res_"] if stage else []
-            return {name: state[name] for name in [a + where for a in parts_of] + (names if stage else [])}
-
-        def new(where, height, cor_height):
-            out = {"res_" + where + "_new": (height, WIN)}
-            if stage:
-                out["map_" + where + "_new"] = (height, WIN)
-                out["cor_" + where + "_new"] = (cor_height, TILE)
-            if stage > 1:
-                out["dir_" + where + "_new"] = (height, WIN)
-            return out
-
-        sums = ["top_sum", "mid_sum", "low_sum"]
+        moving = dict(sides)
+        if stage == 0:
+            moving["observed"] = observed
+        else:
+            moving["parts"] = parts
+        if stage > 1:
+            moving["coef"] = state["coef_new"]
+
+        def old(where, *sums):
+            names = ["res%d_%s" % (i, where) for i in range(stage)]
+            return {name: state[name] for name in names + list(sums) if stage}
+
         middle = run(
             middle_kernel,
-            {**fixed, **moving, **old(sums, "mid")},
-            {**new("mid", mid, mid), "mid_sum_new": (mid - TILE, WIN), "acc": (3, 8, THIRD)},
+            {**fixed, **moving, **old("mid", "top_sum", "mid_sum", "low_sum")},
+            {"res_mid_new": (mid, WIN), "mid_sum_new": (mid - TILE, WIN), "acc": (3, 8, THIRD)},
             stage=stage,
             tiles=tiles,
         )
-        outs = {**new("edge", TILE, THIRD), "top_sum_new": (WIN, WIN), "low_sum_new": (WIN, WIN)}
+        outs = {"res_edge_new": (TILE, WIN), "top_sum_new": (WIN, WIN), "low_sum_new": (WIN, WIN)}
         strip = (ext // 2 if narrow else ext, THIRD)
-        outs.update(to_left=strip, to_right=strip, part=(devices, THIRD))
+        outs.update(to_a=strip, to_b=strip, part=(devices, THIRD))
         if stage:
             outs["coef_new"] = (8, THIRD)
         edges = run(
@@ -677,9 +683,9 @@
             {
                 **fixed,
                 **moving,
-                **old(["top_sum", "low_sum"], "edge"),
-                "above": above,
-                "below": below,
+                **old("edge", "top_sum", "low_sum"),
+                "row_a": row_a,
+                "row_b": row_b,
                 **{name: middle[name] for name in ("res_mid_new", "mid_sum_new", "acc")},
             },
             outs,
@@ -688,43 +694,36 @@
             tiles=tiles,
             narrow=narrow,
         )
-        fresh = {**middle, **edges}
-        if stage == 1:
-            state["dir_mid"], state["dir_edge"] = state["res_mid"], state["res_edge"]
-        for name, value in fresh.items():
-            if name.endswith("_new"):
-                state[name[:-4]] = value
-        from_left = shift(edges["to_right"], "col", True)
-        from_right = shift(edges["to_left"], "col", False)
+        state["res%d_mid" % stage] = middle["res_mid_new"]
+        state["res%d_edge" % stage] = edges["res_edge_new"]
+        state["mid_sum"] = middle["mid_sum_new"]
+        state["top_sum"] = edges["top_sum_new"]
+        state["low_sum"] = edges["low_sum_new"]
+        state["coef_new"] = edges.get("coef_new")
+        side_a, side_b = exchange(edges["to_a"], edges["to_b"], "col")
         parts = lax.all_to_all(edges["part"], ("row", "col"), 0, 0, tiled=True)
-        from_left, from_right, parts = lax.optimization_barrier((from_left, from_right, parts))
-
+        side_a, side_b, parts = lax.optimization_barrier((side_a, side_b, parts))
+        sides = dict(edge=edge, side_a=side_a, side_b=side_b)
         strip = (HALO, TILE) if narrow else (THIRD, WIN)
         sent = run(
             row_strip_kernel,
-            dict(
-                from_left=from_left,
-                from_right=from_right,
-                top_sum=state["top_sum"],
-                low_sum=state["low_sum"],
-            ),
-            dict(to_up=strip, to_down=strip),
+            dict(top_sum=state["top_sum"], low_sum=state["low_sum"], **sides),
+            dict(to_a=strip, to_b=strip),
             tiles=tiles,
             narrow=narrow,
         )
-        above = shift(sent["to_down"], "row", True)
-        below = shift(sent["to_up"], "row", False)
-
-    names = [a + b for b in ("mid", "edge") for a in ("res_", "dir_", "map_", "cor_")]
+        row_a, row_b = exchange(sent["to_a"], sent["to_b"], "row")
+
+    names = ["res%d_%s" % (i, where) for i in range(ITERS) for where in ("mid", "edge")]
     out = run(
         last_kernel,
         dict(
             parts=parts,
-            from_left=from_left,
-            from_right=from_right,
-            above=above,
-            below=below,
-            **{name: state[name] for name in names + ["coef", "top_sum", "mid_sum", "low_sum"]},
+            coef=state["coef_new"],
+            row_a=row_a,
+            row_b=row_b,
+            **sides,
+            **{name: state[name] for name in names + ["top_sum", "mid_sum", "low_sum"]},
         ),
         dict(corrected=(rows, cols), residual=(rows, cols)),
         stage=ITERS,

time: 123 us -> 113 us (0.919)
  starting transfers between devices: 37.4 us -> 23.3 us
  waiting for transfers between devices: 21.5 us -> 9.56 us
  blocking collectives: 48.3 us -> 59.9 us
  Pallas kernels: 10.9 us -> 14 us
    ppermute x16, starting transfers between devices: 37.4 us -> 23.3 us  [exchange(): out.append(lax.ppermute(value, axis, pairs + [(b, a) for a, b in pairs]))]
    ppermute x16, waiting for transfers between devices: 21.5 us -> 9.56 us  [exchange(): out.append(lax.ppermute(value, axis, pairs + [(b, a) for a, b in pairs]))]
    all_to_all x3, blocking collectives: 48.3 us -> 59.9 us  [shards(): parts = lax.all_to_all(edges['part'], ('row', 'col'), 0, 0, tiled=True)]
    pallas_call x13, Pallas kernels: 10.9 us -> 14 us  [run(): pl.pallas_call(kernel, name=body.__name__, out_shape=[jax.ShapeDtypeStruc...]
  transfers between devices with their start and end apart: 16 -> 16, of which waited for: 8 -> 4; matrix products, arithmetic and copies ran while one was open for 2% -> 2% of each run, Pallas kernels for 4% -> 4%
where the time goes in v3:
time: 113 us; the launch traced here: 111 us
  blocking collectives  59.9 us (53%)
  starting transfers between devices  23.3 us (21%)
  Pallas kernels  14 us (12%)
  waiting for transfers between devices  9.56 us (8%)
  local copies, waits for them, and re-layouts  3.59 us (3%)
    all_to_all x3, blocking collectives, shards(): parts = lax.all_to_all(edges['part'], ('row', 'col'), 0, 0, tiled=True)  59.9 us
    ppermute x16, starting transfers between devices, exchange(): out.append(lax.ppermute(value, axis, pairs + [(b, a) for a, b in pairs]))  23.3 us
    pallas_call x13, Pallas kernels, run(): pl.pallas_call(kernel, name=body.__name__, out_shape=[jax.ShapeDtypeStruc...  14 us
    ppermute x16, waiting for transfers between devices, exchange(): out.append(lax.ppermute(value, axis, pairs + [(b, a) for a, b in pairs]))  9.56 us
    unnamed x17, local copies, waits for them, and re-layouts  2.66 us
  transfers between devices with their start and end apart: 16, of which 4 were waited for; matrix products, arithmetic and copies ran while one was open for 2% of the time, Pallas kernels for 4%

profile of v3, /device:TPU:0, one launch (start us, length us, event | category | flops | bytes accessed | tf_op | source)
XLA Modules:
  0.0 111.3 jit_solution(18267727457627297205)
XLA Ops:
  0.7 0.1 stack.27
  0.8 0.0 copy-start
  0.8 1.2 %copy-done = f32[1024,256]{1,0:T(8,128)S(1)} copy-done((f32[1024,256]{1,0:T(8,128)S(1)}, f32[1024,256]{1,0:T(8,128)}, u32[]{:S(2)}) %copy-start) | copy-done | bytes 1048600
  2.0 0.7 pack_kernel.1
  2.7 0.5 collective-permute-start
  3.3 0.7 collective-permute-start.1
  3.9 1.0 copy.13
  5.0 0.8 dynamic-slice_bitcast_fusion
  5.8 0.0 copy-done.6
  5.8 0.0 copy-done.7
  5.8 0.8 spectra_kernel.1.refs_1_
  6.6 0.0 copy-start.2
  6.6 0.0 copy-start.3
  6.6 0.0 copy-start.4
  6.6 0.0 copy-start.5
  6.6 0.0 collective-permute-done.refs_2_.refs_7_
  6.6 0.0 collective-permute-done.1.refs_3_.refs_8_
  6.6 0.4 copy-done.1
  7.0 0.6 halo_kernel.1
  7.7 2.7 %collective-permute-start.2 = (f32[64,384]{1,0:T(8,128)S(1)}, f32[64,384]{1,0:T(8,128)S(1)}, u32[]{:S(2)}, u32[]{:S(2)}) collective-permute-start(f32[64,384]{1,0:T(8,128)S(1)} %get-tuple-element.58), channel_id=1, source_target_pairs={{0,8},{16,24},{8,0},{24,16},{1,9},{17,25},{9,1},{25,17},{2,10},{18... | collective-permute-start | bytes 294920 | tf_op jit(solution)/shard_map/ppermute | solution.py:620
  10.3 0.7 collective-permute-start.3
  11.0 0.0 copy-done.2
  11.0 0.0 copy-done.3
  11.0 0.0 copy-done.4
  11.0 0.0 copy-done.5
  11.0 0.9 middle_kernel.3
  11.9 1.0 collective-permute-done.2.refs_10_
  12.9 0.0 collective-permute-done.3.refs_11_
  12.9 0.8 edge_kernel.3
  13.8 6.1 %collective-permute-start.4 = (f32[1152,128]{1,0:T(8,128)S(1)}, f32[1152,128]{1,0:T(8,128)S(1)}, u32[]{:S(2)}, u32[]{:S(2)}) collective-permute-start(f32[1152,128]{1,0:T(8,128)S(1)} %get-tuple-element.63), channel_id=1, source_target_pairs={{0,1},{2,3},{4,5},{6,7},{1,0},{3,2},{5,4},{7,6},{8,9},{10,11},{12,... | collective-permute-start | bytes 1769480 | tf_op jit(solution)/shard_map/ppermute | solution.py:620
  19.9 0.7 collective-permute-start.5
  20.6 22.1 %all_to_all.36 = f32[32,1,128]{2,1,0:T(1,128)S(1)} all-to-all(f32[32,1,128]{2,1,0:T(1,128)S(1)} %bitcast.29), channel_id=1, replica_groups=mesh['row'=4,'col'=8] {'row','col'}, dimensions={0} | all-to-all | bytes 32768 | tf_op jit(solution)/shard_map/all_to_all | solution.py:704
  42.6 0.0 collective-permute-done.4.refs_3_.refs_7_
  42.6 0.0 collective-permute-done.5.refs_4_.refs_8_
  42.6 0.6 row_strip_kernel.3
  43.3 4.2 %collective-permute-start.6 = (f32[128,384]{1,0:T(8,128)S(1)}, f32[128,384]{1,0:T(8,128)S(1)}, u32[]{:S(2)}, u32[]{:S(2)}) collective-permute-start(f32[128,384]{1,0:T(8,128)S(1)} %get-tuple-element.72), channel_id=1, source_target_pairs={{0,8},{16,24},{8,0},{24,16},{1,9},{17,25},{9,1},{25,17},{2,10},{18... | collective-permute-start | bytes 589832 | tf_op jit(solution)/shard_map/ppermute | solution.py:620
  47.4 0.7 collective-permute-start.7
  48.1 1.3 %middle_kernel.4 = (f32[896,384]{1,0:T(8,128)S(1)}, f32[640,384]{1,0:T(8,128)S(1)}, f32[3,8,128]{2,1,0:T(8,128)S(1)}) custom-call(s32[4]{0:T(128)S(1)} %get-tuple-element.105.refs_1_.refs_0_, f32[4,2,256,256]{3,2,1,0:T(8,128)S(1)} %spectra_kernel.1.refs_1_, bf16[512,256]{1,0:T(8,128)(2,1)S(1)} %copy-done.3, bf16[512,256]{1,0:T(8,128)(2,1)S(1)} %copy-done.2, ...), custom_call_target="tpu_custom_call" | custom-call | tf_op jit(solution)/shard_map/middle_kernel/pallas_call | solution.py:596
  49.4 3.0 %collective-permute-done.6.refs_13_ = f32[128,384]{1,0:T(8,128)S(1)} collective-permute-done((f32[128,384]{1,0:T(8,128)S(1)}, f32[128,384]{1,0:T(8,128)S(1)}, u32[]{:S(2)}, u32[]{:S(2)}) %collective-permute-start.6) | collective-permute-done | bytes 196640 | tf_op jit(solution)/shard_map/ppermute | solution.py:620
  52.3 0.0 collective-permute-done.7.refs_14_
  52.3 1.2 %edge_kernel.4 = (f32[256,384]{1,0:T(8,128)S(1)}, f32[384,384]{1,0:T(8,128)S(1)}, f32[384,384]{1,0:T(8,128)S(1)}, f32[1152,128]{1,0:T(8,128)S(1)}, f32[1152,128]...) custom-call(s32[4]{0:T(128)S(1)} %get-tuple-element.105.refs_1_.refs_0_, ...), custom_call_target="tpu_custom_call" | custom-call | tf_op jit(solution)/shard_map/edge_kernel/pallas_call | solution.py:596
  53.5 0.1 collective-permute-start.8
  53.6 0.7 collective-permute-start.9
  54.3 19.8 %all_to_all.37 = f32[32,1,128]{2,1,0:T(1,128)S(1)} all-to-all(f32[32,1,128]{2,1,0:T(1,128)S(1)} %bitcast.28), channel_id=1, replica_groups=mesh['row'=4,'col'=8] {'row','col'}, dimensions={0} | all-to-all | bytes 32768 | tf_op jit(solution)/shard_map/all_to_all | solution.py:704
  74.1 0.0 collective-permute-done.8.refs_3_.refs_7_
  74.1 0.0 collective-permute-done.9.refs_4_.refs_8_
  74.1 0.6 row_strip_kernel.4
  74.7 3.7 %collective-permute-start.10 = (f32[128,384]{1,0:T(8,128)S(1)}, f32[128,384]{1,0:T(8,128)S(1)}, u32[]{:S(2)}, u32[]{:S(2)}) collective-permute-start(f32[128,384]{1,0:T(8,128)S(1)} %get-tuple-element.87), channel_id=1, source_target_pairs={{0,8},{16,24},{8,0},{24,16},{1,9},{17,25},{9,1},{25,17},{2,10},{18... | collective-permute-start | bytes 589832 | tf_op jit(solution)/shard_map/ppermute | solution.py:620
  78.4 0.7 collective-permute-start.11
  79.1 1.7 %middle_kernel.5 = (f32[896,384]{1,0:T(8,128)S(1)}, f32[640,384]{1,0:T(8,128)S(1)}, f32[3,8,128]{2,1,0:T(8,128)S(1)}) custom-call(s32[4]{0:T(128)S(1)} %get-tuple-element.105.refs_1_.refs_0_, f32[4,2,256,256]{3,2,1,0:T(8,128)S(1)} %spectra_kernel.1.refs_1_, bf16[512,256]{1,0:T(8,128)(2,1)S(1)} %copy-done.3, bf16[512,256]{1,0:T(8,128)(2,1)S(1)} %copy-done.2, ...), custom_call_target="tpu_custom_call" | custom-call | tf_op jit(solution)/shard_map/middle_kernel/pallas_call | solution.py:596
  80.8 2.5 %collective-permute-done.10.refs_15_ = f32[128,384]{1,0:T(8,128)S(1)} collective-permute-done((f32[128,384]{1,0:T(8,128)S(1)}, f32[128,384]{1,0:T(8,128)S(1)}, u32[]{:S(2)}, u32[]{:S(2)}) %collective-permute-start.10) | collective-permute-done | bytes 196640 | tf_op jit(solution)/shard_map/ppermute | solution.py:620
  83.3 0.0 collective-permute-done.11.refs_16_
  83.3 1.4 %edge_kernel.5 = (f32[256,384]{1,0:T(8,128)S(1)}, f32[384,384]{1,0:T(8,128)S(1)}, f32[384,384]{1,0:T(8,128)S(1)}, f32[576,128]{1,0:T(8,128)S(1)}, f32[576,128]{1...) custom-call(s32[4]{0:T(128)S(1)} %get-tuple-element.105.refs_1_.refs_0_, ...), custom_call_target="tpu_custom_call" | custom-call | tf_op jit(solution)/shard_map/edge_kernel/pallas_call | solution.py:596
  84.7 0.1 collective-permute-start.12
  84.8 0.7 collective-permute-start.13
  85.5 18.1 %all_to_all.38 = f32[32,1,128]{2,1,0:T(1,128)S(1)} all-to-all(f32[32,1,128]{2,1,0:T(1,128)S(1)} %bitcast.27), channel_id=1, replica_groups=mesh['row'=4,'col'=8] {'row','col'}, dimensions={0} | all-to-all | bytes 32768 | tf_op jit(solution)/shard_map/all_to_all | solution.py:704
  103.6 0.0 collective-permute-done.12.refs_3_.refs_5_
  103.6 0.0 collective-permute-done.13.refs_4_.refs_6_
  103.6 0.6 row_strip_kernel.5
  104.2 0.6 collective-permute-start.14
  104.9 0.7 collective-permute-start.15
  105.5 3.0 %collective-permute-done.14.refs_2_ = f32[64,256]{1,0:T(8,128)S(1)} collective-permute-done((f32[64,256]{1,0:T(8,128)S(1)}, f32[64,256]{1,0:T(8,128)S(1)}, u32[]{:S(2)}, u32[]{:S(2)}) %collective-permute-start.14) | collective-permute-done | bytes 65568 | tf_op jit(solution)/shard_map/ppermute | solution.py:620
  108.6 0.0 collective-permute-done.15.refs_3_
  108.6 2.8 %last_kernel.1 = (f32[1024,256]{1,0:T(8,128)}, f32[1024,256]{1,0:T(8,128)}) custom-call(f32[32,128]{1,0:T(8,128)S(1)} %bitcast.26, f32[8,128]{1,0:T(8,128)S(1)} %get-tuple-element.96.refs_1_, f32[64,256]{1,0:T(8,128)S(1)} %collective-permute-done.14.refs_2_, f32[64,256]{1,0:T(8,128)S(1)} %collective-permute-done.15.refs_3_, ...), custom_call_target="tpu_custom_call" | custom-call | tf_op jit(solution)/shard_map/last_kernel/pallas_call | solution.py:596
  (5 shorter events, 0.0 us)
Async XLA Ops:
  0.8 1.2 %copy-start = (f32[1024,256]{1,0:T(8,128)S(1)}, f32[1024,256]{1,0:T(8,128)}, u32[]{:S(2)}) copy-start(f32[1024,256]{1,0:T(8,128)} %refs_9_.3) | copy-start | bytes 3145732
  2.0 3.8 %copy-start.6 = (bf16[384,512]{1,0:T(8,128)(2,1)S(1)}, bf16[384,512]{1,0:T(8,128)(2,1)}, u32[]{:S(2)}) copy-start(bf16[384,512]{1,0:T(8,128)(2,1)} %constant.84.clone.refs_4_) | copy-start | bytes 1179652
  2.0 3.8 %copy-start.7 = (bf16[512,384]{1,0:T(8,128)(2,1)S(1)}, bf16[512,384]{1,0:T(8,128)(2,1)}, u32[]{:S(2)}) copy-start(bf16[512,384]{1,0:T(8,128)(2,1)} %constant.83.clone.refs_3_) | copy-start | bytes 1179652
  2.7 3.9 %collective-permute-start = (f32[512,128]{1,0:T(8,128)S(1)}, f32[512,128]{1,0:T(8,128)S(1)}, u32[]{:S(2)}, u32[]{:S(2)}) collective-permute-start(f32[512,128]{1,0:T(8,128)S(1)} %get-tuple-element.53), channel_id=1, source_target_pairs={{0,1},{2,3},{4,5},{6,7},{1,0},{3,2},{5,4},{7,6},{8,9},{10,11},{12,... | collective-permute-start | bytes 786440 | tf_op jit(solution)/shard_map/ppermute | solution.py:620
  3.3 3.4 %collective-permute-start.1 = (f32[512,128]{1,0:T(8,128)S(1)}, f32[512,128]{1,0:T(8,128)S(1)}, u32[]{:S(2)}, u32[]{:S(2)}) collective-permute-start(f32[512,128]{1,0:T(8,128)S(1)} %get-tuple-element.54), channel_id=1, source_target_pairs={{1,2},{3,4},{5,6},{2,1},{4,3},{6,5},{9,10},{11,12},{13,14},{10,9},... | collective-permute-start | bytes 786440 | tf_op jit(solution)/shard_map/ppermute | solution.py:620
  5.8 1.2 %copy-start.1 = (f32[1024,256]{1,0:T(8,128)S(1)}, f32[1024,256]{1,0:T(8,128)}, u32[]{:S(2)}) copy-start(f32[1024,256]{1,0:T(8,128)} %refs_9_.3) | copy-start | bytes 3145732
  6.6 4.4 %copy-start.2 = (bf16[512,256]{1,0:T(8,128)(2,1)S(1)}, bf16[512,256]{1,0:T(8,128)(2,1)}, u32[]{:S(2)}) copy-start(bf16[512,256]{1,0:T(8,128)(2,1)} %constant.80.clone.refs_3_) | copy-start | bytes 786436
  6.6 4.4 %copy-start.3 = (bf16[512,256]{1,0:T(8,128)(2,1)S(1)}, bf16[512,256]{1,0:T(8,128)(2,1)}, u32[]{:S(2)}) copy-start(bf16[512,256]{1,0:T(8,128)(2,1)} %constant.79.clone.refs_2_) | copy-start | bytes 786436
  6.6 4.4 %copy-start.4 = (bf16[256,128]{1,0:T(8,128)(2,1)S(1)}, bf16[256,128]{1,0:T(8,128)(2,1)}, u32[]{:S(2)}) copy-start(bf16[256,128]{1,0:T(8,128)(2,1)} %constant.82.clone.refs_5_) | copy-start | bytes 196612
  6.6 4.4 %copy-start.5 = (bf16[256,128]{1,0:T(8,128)(2,1)S(1)}, bf16[256,128]{1,0:T(8,128)(2,1)}, u32[]{:S(2)}) copy-start(bf16[256,128]{1,0:T(8,128)(2,1)} %constant.81.clone.refs_4_) | copy-start | bytes 196612
  7.7 5.3 %collective-permute-start.2 = (f32[64,384]{1,0:T(8,128)S(1)}, f32[64,384]{1,0:T(8,128)S(1)}, u32[]{:S(2)}, u32[]{:S(2)}) collective-permute-start(f32[64,384]{1,0:T(8,128)S(1)} %get-tuple-element.58), channel_id=1, source_target_pairs={{0,8},{16,24},{8,0},{24,16},{1,9},{17,25},{9,1},{25,17},{2,10},{18... | collective-permute-start | bytes 294920 | tf_op jit(solution)/shard_map/ppermute | solution.py:620
  10.3 2.6 %collective-permute-start.3 = (f32[64,384]{1,0:T(8,128)S(1)}, f32[64,384]{1,0:T(8,128)S(1)}, u32[]{:S(2)}, u32[]{:S(2)}) collective-permute-start(f32[64,384]{1,0:T(8,128)S(1)} %get-tuple-element.59), channel_id=1, source_target_pairs={{8,16},{16,8},{9,17},{17,9},{10,18},{18,10},{11,19},{19,11},{12,20... | collective-permute-start | bytes 294920 | tf_op jit(solution)/shard_map/ppermute | solution.py:620
  13.8 28.9 %collective-permute-start.4 = (f32[1152,128]{1,0:T(8,128)S(1)}, f32[1152,128]{1,0:T(8,128)S(1)}, u32[]{:S(2)}, u32[]{:S(2)}) collective-permute-start(f32[1152,128]{1,0:T(8,128)S(1)} %get-tuple-element.63), channel_id=1, source_target_pairs={{0,1},{2,3},{4,5},{6,7},{1,0},{3,2},{5,4},{7,6},{8,9},{10,11},{12,... | collective-permute-start | bytes 1769480 | tf_op jit(solution)/shard_map/ppermute | solution.py:620
  19.9 22.8 %collective-permute-start.5 = (f32[1152,128]{1,0:T(8,128)S(1)}, f32[1152,128]{1,0:T(8,128)S(1)}, u32[]{:S(2)}, u32[]{:S(2)}) collective-permute-start(f32[1152,128]{1,0:T(8,128)S(1)} %get-tuple-element.64), channel_id=1, source_target_pairs={{1,2},{3,4},{5,6},{2,1},{4,3},{6,5},{9,10},{11,12},{13,14},{10,9},... | collective-permute-start | bytes 1769480 | tf_op jit(solution)/shard_map/ppermute | solution.py:620
  43.3 9.1 %collective-permute-start.6 = (f32[128,384]{1,0:T(8,128)S(1)}, f32[128,384]{1,0:T(8,128)S(1)}, u32[]{:S(2)}, u32[]{:S(2)}) collective-permute-start(f32[128,384]{1,0:T(8,128)S(1)} %get-tuple-element.72), channel_id=1, source_target_pairs={{0,8},{16,24},{8,0},{24,16},{1,9},{17,25},{9,1},{25,17},{2,10},{18... | collective-permute-start | bytes 589832 | tf_op jit(solution)/shard_map/ppermute | solution.py:620
  47.4 4.9 %collective-permute-start.7 = (f32[128,384]{1,0:T(8,128)S(1)}, f32[128,384]{1,0:T(8,128)S(1)}, u32[]{:S(2)}, u32[]{:S(2)}) collective-permute-start(f32[128,384]{1,0:T(8,128)S(1)} %get-tuple-element.73), channel_id=1, source_target_pairs={{8,16},{16,8},{9,17},{17,9},{10,18},{18,10},{11,19},{19,11},{12,20... | collective-permute-start | bytes 589832 | tf_op jit(solution)/shard_map/ppermute | solution.py:620
  53.5 20.6 %collective-permute-start.8 = (f32[1152,128]{1,0:T(8,128)S(1)}, f32[1152,128]{1,0:T(8,128)S(1)}, u32[]{:S(2)}, u32[]{:S(2)}) collective-permute-start(f32[1152,128]{1,0:T(8,128)S(1)} %get-tuple-element.77), channel_id=1, source_target_pairs={{0,1},{2,3},{4,5},{6,7},{1,0},{3,2},{5,4},{7,6},{8,9},{10,11},{12,... | collective-permute-start | bytes 1769480 | tf_op jit(solution)/shard_map/ppermute | solution.py:620
  53.6 20.5 %collective-permute-start.9 = (f32[1152,128]{1,0:T(8,128)S(1)}, f32[1152,128]{1,0:T(8,128)S(1)}, u32[]{:S(2)}, u32[]{:S(2)}) collective-permute-start(f32[1152,128]{1,0:T(8,128)S(1)} %get-tuple-element.78), channel_id=1, source_target_pairs={{1,2},{3,4},{5,6},{2,1},{4,3},{6,5},{9,10},{11,12},{13,14},{10,9},... | collective-permute-start | bytes 1769480 | tf_op jit(solution)/shard_map/ppermute | solution.py:620
  74.7 8.6 %collective-permute-start.10 = (f32[128,384]{1,0:T(8,128)S(1)}, f32[128,384]{1,0:T(8,128)S(1)}, u32[]{:S(2)}, u32[]{:S(2)}) collective-permute-start(f32[128,384]{1,0:T(8,128)S(1)} %get-tuple-element.87), channel_id=1, source_target_pairs={{0,8},{16,24},{8,0},{24,16},{1,9},{17,25},{9,1},{25,17},{2,10},{18... | collective-permute-start | bytes 589832 | tf_op jit(solution)/shard_map/ppermute | solution.py:620
  78.4 4.9 %collective-permute-start.11 = (f32[128,384]{1,0:T(8,128)S(1)}, f32[128,384]{1,0:T(8,128)S(1)}, u32[]{:S(2)}, u32[]{:S(2)}) collective-permute-start(f32[128,384]{1,0:T(8,128)S(1)} %get-tuple-element.88), channel_id=1, source_target_pairs={{8,16},{16,8},{9,17},{17,9},{10,18},{18,10},{11,19},{19,11},{12,20... | collective-permute-start | bytes 589832 | tf_op jit(solution)/shard_map/ppermute | solution.py:620
  84.7 18.9 %collective-permute-start.12 = (f32[576,128]{1,0:T(8,128)S(1)}, f32[576,128]{1,0:T(8,128)S(1)}, u32[]{:S(2)}, u32[]{:S(2)}) collective-permute-start(f32[576,128]{1,0:T(8,128)S(1)} %get-tuple-element.92), channel_id=1, source_target_pairs={{0,1},{2,3},{4,5},{6,7},{1,0},{3,2},{5,4},{7,6},{8,9},{10,11},{12,... | collective-permute-start | bytes 884744 | tf_op jit(solution)/shard_map/ppermute | solution.py:620
  84.8 18.8 %collective-permute-start.13 = (f32[576,128]{1,0:T(8,128)S(1)}, f32[576,128]{1,0:T(8,128)S(1)}, u32[]{:S(2)}, u32[]{:S(2)}) collective-permute-start(f32[576,128]{1,0:T(8,128)S(1)} %get-tuple-element.93), channel_id=1, source_target_pairs={{1,2},{3,4},{5,6},{2,1},{4,3},{6,5},{9,10},{11,12},{13,14},{10,9},... | collective-permute-start | bytes 884744 | tf_op jit(solution)/shard_map/ppermute | solution.py:620
  104.2 4.3 %collective-permute-start.14 = (f32[64,256]{1,0:T(8,128)S(1)}, f32[64,256]{1,0:T(8,128)S(1)}, u32[]{:S(2)}, u32[]{:S(2)}) collective-permute-start(f32[64,256]{1,0:T(8,128)S(1)} %get-tuple-element.101), channel_id=1, source_target_pairs={{0,8},{16,24},{8,0},{24,16},{1,9},{17,25},{9,1},{25,17},{2,10},{18... | collective-permute-start | bytes 196616 | tf_op jit(solution)/shard_map/ppermute | solution.py:620
  104.9 3.7 %collective-permute-start.15 = (f32[64,256]{1,0:T(8,128)S(1)}, f32[64,256]{1,0:T(8,128)S(1)}, u32[]{:S(2)}, u32[]{:S(2)}) collective-permute-start(f32[64,256]{1,0:T(8,128)S(1)} %get-tuple-element.102), channel_id=1, source_target_pairs={{8,16},{16,8},{9,17},{17,9},{10,18},{18,10},{11,19},{19,11},{12,20... | collective-permute-start | bytes 196616 | tf_op jit(solution)/shard_map/ppermute | solution.py:620

commit v4 on v3

--- a/solution.py
+++ b/solution.py
@@ -297,8 +297,18 @@
     return jnp.where(odd, first, second), jnp.where(odd, second, first)
 
 
-def from_columns(r, here):
-    return pick(r.edge[4] != 0, r.side_a[here, :], r.side_b[here, :])
+def from_columns(r, start, size):
+    second = getattr(r, "side_b", None)
+    there = start
+    if second is None:
+        middle = r.side_mid.shape[0]
+        if start < WIN:
+            second = r.side_end
+        elif start < WIN + middle:
+            second, there = r.side_mid, start - WIN
+        else:
+            second, there = r.side_end, start - middle
+    return pick(r.edge[4] != 0, r.side_z[pl.ds(start, size), :], second[pl.ds(there, size), :])
 
 
 def from_rows(r, side, here):
@@ -307,6 +317,16 @@
 
 def send_columns(r, here, to_left, to_right):
     r.to_a[here, :], r.to_b[here, :] = pick(r.edge[4] != 0, to_left, to_right)
+
+
+def strips_of(terms):
+    low = lane_mask()
+    pieces = [ref[rows_at(block), :] for ref, block in terms]
+    block = sum(pieces[1:], pieces[0])
+    return (
+        jnp.where(low, tile_of(block, 0), tile_of(block, 2)),
+        jnp.where(low, tile_of(block, 2), tile_of(block, 1)),
+    )
 
 
 def send_rows(r, above, below):
@@ -324,7 +344,7 @@
 def update(r, num, name, here, size, offset, spill, keep):
     low = lane_mask()
     sums = [ref[pl.ds(block * THIRD + offset, size), :] for ref, block in own_sum(r, num)]
-    west, east = from_columns(r, pl.ds(num * THIRD + offset, size))
+    west, east = from_columns(r, num * THIRD + offset, size)
     add = [
         jnp.where(low, west, 0.0),
         jnp.where(low, 0.0, east),
@@ -344,14 +364,13 @@
 
 
 def unpacked_sides(r, start, size):
-    half = r.side_a.shape[0]
+    half = r.side_z.shape[0]
     low = lane_mask()
     out = []
     while size:
         upper = start < half
         count = min(size, half - start) if upper else size
-        here = pl.ds(start if upper else start - half, count)
-        left, right = from_columns(r, here)
+        left, right = from_columns(r, start if upper else start - half, count)
         if upper:
             left = pltpu.roll(left, HALF, 1)
         else:
@@ -392,14 +411,14 @@
     for side, ref in ((0, r.top_sum), (1, r.low_sum)):
         own = ref[pl.ds(side * (WIN - size), size), :]
         if r.narrow:
-            west, east = from_columns(r, pl.ds(side * (blocks * HALO - size), size))
+            west, east = from_columns(r, side * (blocks * HALO - size), size)
             if side:
                 west = pltpu.roll(west, HALF, 1)
             else:
                 east = pltpu.roll(east, HALF, 1)
             add = [jnp.where(low, west, 0.0), jnp.where(low, 0.0, east)]
         else:
-            west, east = from_columns(r, pl.ds(side * (blocks * THIRD - size), size))
+            west, east = from_columns(r, side * (blocks * THIRD - size), size)
             add = [
                 jnp.where(low, west, 0.0),
                 jnp.where(low, 0.0, east),
@@ -449,6 +468,11 @@
     @pl.when(some == 0)
     def _():
         r.mid_sum_new[...] = jnp.zeros(r.mid_sum_new.shape, F32)
+
+    if r.parted:
+        for num in range(r.to_mid.shape[0] // THIRD):
+            strips = strips_of([(r.mid_sum_new, num + 1)])
+            r.to_mid[rows_at(num), :] = pick(r.edge[4] != 0, *strips)[1]
 
 
 def edge_kernel(r):
@@ -523,58 +547,75 @@
                 jnp.where(low, pair[0], pltpu.roll(pair[1], HALF, 1)),
             )
     else:
+        middle = blocks - 6
         for num in range(blocks):
-            terms = [ref[rows_at(block), :] for ref, block in own_sum(new, num)]
-            block = sum(terms[1:], terms[0])
-            send_columns(
-                r,
-                rows_at(num),
-                jnp.where(low, tile_of(block, 0), tile_of(block, 2)),
-                jnp.where(low, tile_of(block, 2), tile_of(block, 1)),
-            )
+            to_a, to_b = pick(r.edge[4] != 0, *strips_of(own_sum(new, num)))
+            r.to_a[rows_at(num), :] = to_a
+            if not r.parted:
+                r.to_b[rows_at(num), :] = to_b
+            elif num < 3 or num >= 3 + middle:
+                r.to_end[rows_at(num if num < 3 else num - middle), :] = to_b
     gamma = total(square)
     curve = gamma + total(r.acc[2] + r.curve[...])
     r.part[...] = lanes_of(r.part.shape, gamma, curve, total(cross))
 
 
-def last_kernel(r):
+def last_rows(r, start, corrected, residual, at):
     blocks = 2 * r.tiles + 1
     half = blocks * HALO
+    low = lane_mask()
+    num, offset = start // THIRD, start % THIRD
+    upper = start < half
+    west, east = from_columns(r, start if upper else start - half, HALO)
+    if upper:
+        east = pltpu.roll(east, HALF, 1)
+    else:
+        west = pltpu.roll(west, HALF, 1)
+    add = [jnp.where(low, west, 0.0), jnp.where(low, 0.0, east)]
+    for ref, block in own_sum(r, num):
+        there = pl.ds(block * THIRD + offset, HALO)
+        add = [a + ref[there, pl.ds(i * THIRD, THIRD)] for i, a in enumerate(add)]
+    if num == 0 or num == blocks - 1:
+        spill = from_rows(r, 0 if num == 0 else 1, pl.ds(0, HALO))
+        add = [a + tile_of(spill, i) for i, a in enumerate(add)]
+        olds, here = old_of(r, "edge"), pl.ds((0 if num == 0 else THIRD) + offset, HALO)
+    else:
+        olds, here = old_of(r, "mid"), pl.ds(start - THIRD, HALO)
+    for i, a in enumerate(add):
+        lanes = pl.ds(i * THIRD, THIRD)
+        past = [ref[here, lanes] for ref in olds]
+        direct = past[0]
+        moved = r.steps[0] * direct
+        for old, ratio, step in zip(past[1:], r.ratios, r.steps[1:]):
+            direct = old + ratio * direct
+            moved = moved + step * direct
+        mapped = a + past[-1] + r.back * (past[-2] - past[-1])
+        corrected[pl.ds(at, HALO), lanes] = moved
+        residual[pl.ds(at, HALO), lanes] = past[-1] - r.steps[-1] * mapped
+
+
+def last_middle_kernel(r):
     scalars(r)
-    low = lane_mask()
-    for start in range(HALO, 2 * half - HALO, HALO):
-        num, offset = start // THIRD, start % THIRD
-        upper = start < half
-        wide = pl.ds(start if upper else start - half, HALO)
-        west, east = from_columns(r, wide)
-        if upper:
-            east = pltpu.roll(east, HALF, 1)
-        else:
-            west = pltpu.roll(west, HALF, 1)
-        add = [jnp.where(low, west, 0.0), jnp.where(low, 0.0, east)]
-        for ref, block in own_sum(r, num):
-            there = pl.ds(block * THIRD + offset, HALO)
-            add = [a + ref[there, pl.ds(i * THIRD, THIRD)] for i, a in enumerate(add)]
-        for side, edge in ((0, HALO), (1, 2 * half - 2 * HALO)):
-            if start == edge:
-                spill = from_rows(r, side, pl.ds(0, HALO))
-                add = [a + tile_of(spill, i) for i, a in enumerate(add)]
-        if num == 0 or num == blocks - 1:
-            olds, here = old_of(r, "edge"), pl.ds((0 if num == 0 else THIRD) + offset, HALO)
-        else:
-            olds, here = old_of(r, "mid"), pl.ds(start - THIRD, HALO)
-        for i, a in enumerate(add):
-            lanes = pl.ds(i * THIRD, THIRD)
-            past = [ref[here, lanes] for ref in olds]
-            direct = past[0]
-            moved = r.steps[0] * direct
-            for old, ratio, step in zip(past[1:], r.ratios, r.steps[1:]):
-                direct = old + ratio * direct
-                moved = moved + step * direct
-            mapped = a + past[-1] + r.back * (past[-2] - past[-1])
-            out = pl.ds(start - HALO, HALO)
-            r.corrected[out, lanes] = moved
-            r.residual[out, lanes] = past[-1] - r.steps[-1] * mapped
+    for start in range(THIRD, 2 * r.tiles * THIRD, HALO):
+        last_rows(r, start, r.corrected, r.residual, start - HALO)
+
+
+def last_edge_kernel(r):
+    scalars(r)
+    rows = 2 * r.tiles * THIRD
+    copies = []
+    for side in range(2):
+        last_rows(r, HALO + side * (rows - HALO), r.corrected_rows, r.residual_rows, side * HALO)
+        here = pl.ds(side * HALO, HALO)
+        there = pl.ds(side * (rows - HALO), HALO)
+        for num, (source, target) in enumerate(
+            ((r.corrected_rows, r.corrected), (r.residual_rows, r.residual))
+        ):
+            copy = pltpu.make_async_copy(source.at[here, :], target.at[there, :], r.sems.at[side, num])
+            copy.start()
+            copies.append(copy)
+    for copy in copies:
+        copy.wait()
 
 
 class Refs:
@@ -586,25 +627,32 @@
 PARAMS = pltpu.CompilerParams(vmem_limit_bytes=16 * 1024 * 1024)
 
 
-def run(body, ins, outs, scratch=None, **static):
-    scratch = scratch or {}
-    names = [*ins, *outs, *scratch]
+def run(body, ins, outs, scratch=None, onto=None, **static):
+    scratch, onto = scratch or {}, onto or {}
+    names = [*ins, *("old_" + name for name in onto), *outs, *onto, *scratch]
 
     def kernel(*refs):
         body(Refs(**static, **dict(zip(names, refs))))
 
+    whole = pl.BlockSpec(memory_space=pltpu.VMEM)
+    placed = [pl.BlockSpec(memory_space=pl.ANY)] * len(onto)
+    shapes = [*outs.values(), *(value.shape for value in onto.values())]
     result = pl.pallas_call(
         kernel,
         name=body.__name__,
-        out_shape=[jax.ShapeDtypeStruct(dims, F32) for dims in outs.values()],
+        out_shape=[jax.ShapeDtypeStruct(dims, F32) for dims in shapes],
         in_specs=[
-            pl.BlockSpec(memory_space=pltpu.SMEM if name in SCALARS else pltpu.VMEM) for name in ins
+            pl.BlockSpec(memory_space=pltpu.SMEM) if name in SCALARS else whole for name in ins
+        ]
+        + placed,
+        out_specs=[whole] * len(outs) + placed,
+        scratch_shapes=[
+            pltpu.VMEM(dims, F32) if isinstance(dims, tuple) else dims for dims in scratch.values()
         ],
-        out_specs=[pl.BlockSpec(memory_space=pltpu.VMEM)] * len(outs),
-        scratch_shapes=[pltpu.VMEM(dims, F32) for dims in scratch.values()],
+        input_output_aliases={len(ins) + i: len(outs) + i for i in range(len(onto))},
         compiler_params=PARAMS,
-    )(*ins.values())
-    return dict(zip(outs, result))
+    )(*ins.values(), *onto.values())
+    return dict(zip([*outs, *onto], result))
 
 
 def own_part(table, tile_count):
@@ -612,13 +660,9 @@
     return lax.dynamic_slice_in_dim(column, lax.axis_index("row") * tile_count, tile_count)
 
 
-def exchange(to_a, to_b, axis):
-    count = lax.axis_size(axis)
-    out = []
-    for value, first in ((to_b, 1), (to_a, 0)):
-        pairs = [(i, i + 1) for i in range(first, count - 1, 2)]
-        out.append(lax.ppermute(value, axis, pairs + [(b, a) for a, b in pairs]))
-    return out[1], out[0]
+def swap(value, axis, first):
+    pairs = [(i, i + 1) for i in range(first, lax.axis_size(axis) - 1, 2)]
+    return lax.ppermute(value, axis, pairs + [(b, a) for a, b in pairs])
 
 
 def shards(observed, kernels, occupied, kernel_index):
@@ -634,7 +678,8 @@
     ).astype(jnp.int32)
     host = {name: jnp.asarray(table) for name, table in tables().items()}
     sent = run(pack_kernel, dict(edge=edge, observed=observed), dict(to_a=(half, THIRD), to_b=(half, THIRD)))
-    side_a, side_b = exchange(sent["to_a"], sent["to_b"], "col")
+    side_b = swap(sent["to_b"], "col", 1)
+    side_z = swap(sent["to_a"], "col", 0)
     spec = run(
         spectra_kernel,
         dict(
@@ -646,14 +691,16 @@
         ),
         dict(spec=(tiles, 2, SLOTS, SLOTS)),
     )["spec"]
-    side_a, side_b, spec = lax.optimization_barrier((side_a, side_b, spec))
-    sides = dict(edge=edge, side_a=side_a, side_b=side_b)
+    side_b, side_z, spec = lax.optimization_barrier((side_b, side_z, spec))
+    sides = dict(edge=edge, side_b=side_b, side_z=side_z)
     sent = run(halo_kernel, dict(observed=observed, **sides), dict(to_a=(HALO, WIN), to_b=(HALO, WIN)))
-    row_a, row_b = exchange(sent["to_a"], sent["to_b"], "row")
+    sides, sent = lax.optimization_barrier((sides, sent))
+    row_b, row_a = swap(sent["to_b"], "row", 1), swap(sent["to_a"], "row", 0)
     fixed = dict(occ=occ, spec=spec, **{name: host[name] for name in NAMES})
     state = {}
     for stage in range(ITERS):
         narrow = stage == ITERS - 1
+        parted = 0 < stage < ITERS - 1
         moving = dict(sides)
         if stage == 0:
             moving["observed"] = observed
@@ -669,13 +716,22 @@
         middle = run(
             middle_kernel,
             {**fixed, **moving, **old("mid", "top_sum", "mid_sum", "low_sum")},
-            {"res_mid_new": (mid, WIN), "mid_sum_new": (mid - TILE, WIN), "acc": (3, 8, THIRD)},
+            {
+                "res_mid_new": (mid, WIN),
+                "mid_sum_new": (mid - TILE, WIN),
+                "acc": (3, 8, THIRD),
+                **({"to_mid": (ext - 2 * WIN, THIRD)} if parted else {}),
+            },
             stage=stage,
             tiles=tiles,
+            parted=parted,
         )
+        if parted:
+            side_mid = swap(middle["to_mid"], "col", 1)
         outs = {"res_edge_new": (TILE, WIN), "top_sum_new": (WIN, WIN), "low_sum_new": (WIN, WIN)}
-        strip = (ext // 2 if narrow else ext, THIRD)
-        outs.update(to_a=strip, to_b=strip, part=(devices, THIRD))
+        outs["to_a"] = (ext // 2 if narrow else ext, THIRD)
+        outs["to_end" if parted else "to_b"] = (2 * WIN if parted else outs["to_a"][0], THIRD)
+        outs["part"] = (devices, THIRD)
         if stage:
             outs["coef_new"] = (8, THIRD)
         edges = run(
@@ -684,14 +740,15 @@
                 **fixed,
                 **moving,
                 **old("edge", "top_sum", "low_sum"),
+                "row_b": row_b,
                 "row_a": row_a,
-                "row_b": row_b,
                 **{name: middle[name] for name in ("res_mid_new", "mid_sum_new", "acc")},
             },
             outs,
             dict(curve=(8, THIRD)),
             stage=stage,
             tiles=tiles,
+            parted=parted,
             narrow=narrow,
         )
         state["res%d_mid" % stage] = middle["res_mid_new"]
@@ -700,10 +757,20 @@
         state["top_sum"] = edges["top_sum_new"]
         state["low_sum"] = edges["low_sum_new"]
         state["coef_new"] = edges.get("coef_new")
-        side_a, side_b = exchange(edges["to_a"], edges["to_b"], "col")
-        parts = lax.all_to_all(edges["part"], ("row", "col"), 0, 0, tiled=True)
-        side_a, side_b, parts = lax.optimization_barrier((side_a, side_b, parts))
-        sides = dict(edge=edge, side_a=side_a, side_b=side_b)
+        part, to_a = edges["part"], edges["to_a"]
+        sides = {}
+        if parted:
+            sides["side_mid"], part, to_a, to_end = lax.optimization_barrier(
+                (side_mid, part, to_a, edges["to_end"])
+            )
+        sides["side_z"] = swap(to_a, "col", 0)
+        if parted:
+            sides["side_end"] = swap(to_end, "col", 1)
+        else:
+            sides["side_b"] = swap(edges["to_b"], "col", 1)
+        parts = lax.all_to_all(part, ("row", "col"), 0, 0, tiled=True)
+        sides, parts = lax.optimization_barrier((sides, parts))
+        sides["edge"] = edge
         strip = (HALO, TILE) if narrow else (THIRD, WIN)
         sent = run(
             row_strip_kernel,
@@ -712,20 +779,30 @@
             tiles=tiles,
             narrow=narrow,
         )
-        row_a, row_b = exchange(sent["to_a"], sent["to_b"], "row")
-
-    names = ["res%d_%s" % (i, where) for i in range(ITERS) for where in ("mid", "edge")]
+        row_b, row_a = swap(sent["to_b"], "row", 1), swap(sent["to_a"], "row", 0)
+
+    def olds(where):
+        return {name: state[name] for name in ["res%d_%s" % (i, where) for i in range(ITERS)]}
+
+    ends = {name: state[name] for name in ("coef_new", "top_sum", "low_sum")}
+    ends["coef"] = ends.pop("coef_new")
     out = run(
-        last_kernel,
+        last_middle_kernel,
+        dict(parts=parts, mid_sum=state["mid_sum"], **ends, **sides, **olds("mid")),
+        dict(corrected=(rows, cols), residual=(rows, cols)),
+        stage=ITERS,
+        tiles=tiles,
+    )
+    out = run(
+        last_edge_kernel,
+        dict(parts=parts, row_b=row_b, row_a=row_a, **ends, **sides, **olds("edge")),
+        {},
         dict(
-            parts=parts,
-            coef=state["coef_new"],
-            row_a=row_a,
-            row_b=row_b,
-            **sides,
-            **{name: state[name] for name in names + ["top_sum", "mid_sum", "low_sum"]},
+            corrected_rows=(2 * HALO, cols),
+            residual_rows=(2 * HALO, cols),
+            sems=pltpu.SemaphoreType.DMA((2, 2)),
         ),
-        dict(corrected=(rows, cols), residual=(rows, cols)),
+        out,
         stage=ITERS,
         tiles=tiles,
     )

time: 113 us -> 109 us (0.965); the launches traced: 111 us -> 109 us
  blocking collectives: 59.9 us -> 38.9 us
  starting transfers between devices: 23.3 us -> 42.9 us
  waiting for transfers between devices: 9.56 us -> 7.38 us
  Pallas kernels: 14 us -> 15.6 us
    all_to_all x3, blocking collectives: 59.9 us -> 38.9 us  [shards(): parts = lax.all_to_all(part, ('row', 'col'), 0, 0, tiled=True)]
    ppermute x16 -> x17, starting transfers between devices: 23.3 us -> 42.9 us  [swap(): return lax.ppermute(value, axis, pairs + [(b, a) for a, b in pairs])]
    ppermute x16 -> x17, waiting for transfers between devices: 9.56 us -> 7.38 us  [swap(): return lax.ppermute(value, axis, pairs + [(b, a) for a, b in pairs])]
    pallas_call x13 -> x14, Pallas kernels: 14 us -> 15.6 us  [run(): pl.pallas_call(kernel, name=body.__name__, out_shape=[jax.ShapeDtypeStruc...]
  transfers between devices with their start and end apart: 16 -> 17, of which waited for: 4 -> 3; matrix products, arithmetic and copies ran while one was open for 2% -> 2% of each run, Pallas kernels for 4% -> 8%
where the time goes in v4:
time: 109 us
  starting transfers between devices  42.9 us (39%)
  blocking collectives  38.9 us (36%)
  Pallas kernels  15.6 us (14%)
  waiting for transfers between devices  7.38 us (7%)
  local copies, waits for them, and re-layouts  3.59 us (3%)
    ppermute x17, starting transfers between devices, swap(): return lax.ppermute(value, axis, pairs + [(b, a) for a, b in pairs])  42.9 us
    all_to_all x3, blocking collectives, shards(): parts = lax.all_to_all(part, ('row', 'col'), 0, 0, tiled=True)  38.9 us
    pallas_call x14, Pallas kernels, run(): pl.pallas_call(kernel, name=body.__name__, out_shape=[jax.ShapeDtypeStruc...  15.6 us
    ppermute x17, waiting for transfers between devices, swap(): return lax.ppermute(value, axis, pairs + [(b, a) for a, b in pairs])  7.38 us
    unnamed x17, local copies, waits for them, and re-layouts  2.66 us
  transfers between devices with their start and end apart: 17, of which 3 were waited for; matrix products, arithmetic and copies ran while one was open for 2% of the time, Pallas kernels for 8%

profile of v4, /device:TPU:0, one launch (start us, length us, event | category | flops | bytes accessed | tf_op | source)
XLA Modules:
  0.0 109.5 jit_solution(5196147955283953043)
XLA Ops:
  0.7 0.1 stack.27
  0.8 1.2 %copy-done = f32[1024,256]{1,0:T(8,128)S(1)} copy-done((f32[1024,256]{1,0:T(8,128)S(1)}, f32[1024,256]{1,0:T(8,128)}, u32[]{:S(2)}) %copy-start) | copy-done | bytes 1048600
  2.0 0.7 pack_kernel.1
  2.7 0.7 collective-permute-start
  3.4 4.3 %collective-permute-start.1 = (f32[512,128]{1,0:T(8,128)S(1)}, f32[512,128]{1,0:T(8,128)S(1)}, u32[]{:S(2)}, u32[]{:S(2)}) collective-permute-start(f32[512,128]{1,0:T(8,128)S(1)} %get-tuple-element.67), channel_id=1, source_target_pairs={{0,1},{2,3},{4,5},{6,7},{1,0},{3,2},{5,4},{7,6},{8,9},{10,11},{12,... | collective-permute-start | bytes 786440 | tf_op jit(solution)/shard_map/ppermute | solution.py:665
  7.8 1.0 copy.15
  8.8 0.8 dynamic-slice_bitcast_fusion
  9.6 0.0 copy-done.6
  9.6 0.0 copy-done.7
  9.6 0.8 spectra_kernel.1.refs_1_
  10.4 0.0 copy-start.2
  10.4 0.0 copy-start.3
  10.4 0.0 copy-start.4
  10.4 0.0 copy-start.5
  10.5 0.0 collective-permute-done.refs_2_.refs_7_
  10.5 0.0 collective-permute-done.1.refs_3_.refs_8_
  10.5 0.4 copy-done.1
  10.9 0.6 halo_kernel.1
  11.5 0.7 collective-permute-start.2
  12.2 4.5 %collective-permute-start.3 = (f32[64,384]{1,0:T(8,128)S(1)}, f32[64,384]{1,0:T(8,128)S(1)}, u32[]{:S(2)}, u32[]{:S(2)}) collective-permute-start(f32[64,384]{1,0:T(8,128)S(1)} %get-tuple-element.77), channel_id=1, source_target_pairs={{0,8},{16,24},{8,0},{24,16},{1,9},{17,25},{9,1},{25,17},{2,10},{18... | collective-permute-start | bytes 294920 | tf_op jit(solution)/shard_map/ppermute | solution.py:665
  16.6 0.0 copy-done.2
  16.6 0.0 copy-done.4
  16.6 0.9 middle_kernel.3
  17.5 0.0 collective-permute-done.2.refs_10_
  17.5 1.7 %collective-permute-done.3.refs_11_ = f32[64,384]{1,0:T(8,128)S(1)} collective-permute-done((f32[64,384]{1,0:T(8,128)S(1)}, f32[64,384]{1,0:T(8,128)S(1)}, u32[]{:S(2)}, u32[]{:S(2)}) %collective-permute-start.3) | collective-permute-done | bytes 98336 | tf_op jit(solution)/shard_map/ppermute | solution.py:665
  19.2 0.8 edge_kernel.3
  20.1 0.7 collective-permute-start.4
  20.8 6.4 %collective-permute-start.5 = (f32[1152,128]{1,0:T(8,128)S(1)}, f32[1152,128]{1,0:T(8,128)S(1)}, u32[]{:S(2)}, u32[]{:S(2)}) collective-permute-start(f32[1152,128]{1,0:T(8,128)S(1)} %get-tuple-element.82), channel_id=1, source_target_pairs={{0,1},{2,3},{4,5},{6,7},{1,0},{3,2},{5,4},{7,6},{8,9},{10,11},{12,... | collective-permute-start | bytes 1769480 | tf_op jit(solution)/shard_map/ppermute | solution.py:665
  27.2 14.1 %all_to_all.36 = f32[32,1,128]{2,1,0:T(1,128)S(1)} all-to-all(f32[32,1,128]{2,1,0:T(1,128)S(1)} %bitcast.30), channel_id=1, replica_groups=mesh['row'=4,'col'=8] {'row','col'}, dimensions={0} | all-to-all | bytes 32768 | tf_op jit(solution)/shard_map/all_to_all | solution.py:771
  41.3 0.0 collective-permute-done.4.refs_6_.refs_2_
  41.3 0.0 collective-permute-done.5.refs_7_.refs_3_
  41.3 0.6 row_strip_kernel.3
  42.0 0.7 collective-permute-start.7
  42.7 4.6 %collective-permute-start.8 = (f32[128,384]{1,0:T(8,128)S(1)}, f32[128,384]{1,0:T(8,128)S(1)}, u32[]{:S(2)}, u32[]{:S(2)}) collective-permute-start(f32[128,384]{1,0:T(8,128)S(1)} %get-tuple-element.92), channel_id=1, source_target_pairs={{0,8},{16,24},{8,0},{24,16},{1,9},{17,25},{9,1},{25,17},{2,10},{18... | collective-permute-start | bytes 589832 | tf_op jit(solution)/shard_map/ppermute | solution.py:665
  47.3 1.3 %middle_kernel.4 = (f32[896,384]{1,0:T(8,128)S(1)}, f32[640,384]{1,0:T(8,128)S(1)}, f32[3,8,128]{2,1,0:T(8,128)S(1)}, f32[384,128]{1,0:T(8,128)S(1)}) custom-call(s32[4]{0:T(128)S(1)} %get-tuple-element.131.refs_1_.refs_0_, f32[4,2,256,256]{3,2,1,0:T(8,128)S(1)} %spectra_kernel.1.refs_1_, bf16[512,256]{1,0:T(8,128)(2,1)S(1)} %copy-done.3, ...), custom_call_target="tpu_custom_call" | custom-call | tf_op jit(solution)/shard_map/middle_kernel/pallas_call | solution.py:640
  48.5 0.7 collective-permute-start.6
  49.2 0.0 collective-permute-done.7.refs_13_
  49.2 2.6 %collective-permute-done.8.refs_14_ = f32[128,384]{1,0:T(8,128)S(1)} collective-permute-done((f32[128,384]{1,0:T(8,128)S(1)}, f32[128,384]{1,0:T(8,128)S(1)}, u32[]{:S(2)}, u32[]{:S(2)}) %collective-permute-start.8) | collective-permute-done | bytes 196640 | tf_op jit(solution)/shard_map/ppermute | solution.py:665
  51.9 1.2 %edge_kernel.4 = (f32[256,384]{1,0:T(8,128)S(1)}, f32[384,384]{1,0:T(8,128)S(1)}, f32[384,384]{1,0:T(8,128)S(1)}, f32[1152,128]{1,0:T(8,128)S(1)}, f32[768,128]{...) custom-call(s32[4]{0:T(128)S(1)} %get-tuple-element.131.refs_1_.refs_0_, ...), custom_call_target="tpu_custom_call" | custom-call | tf_op jit(solution)/shard_map/edge_kernel/pallas_call | solution.py:640
  53.0 0.0 collective-permute-done.6.refs_3_.refs_7_
  53.0 5.4 %collective-permute-start.10 = (f32[1152,128]{1,0:T(8,128)S(1)}, f32[1152,128]{1,0:T(8,128)S(1)}, u32[]{:S(2)}, u32[]{:S(2)}) collective-permute-start(f32[1152,128]{1,0:T(8,128)S(1)} %get-tuple-element.101), channel_id=1, source_target_pairs={{0,1},{2,3},{4,5},{6,7},{1,0},{3,2},{5,4},{7,6},{8,9},{10,11},{12,... | collective-permute-start | bytes 1769480 | tf_op jit(solution)/shard_map/ppermute | solution.py:665
  58.4 0.7 collective-permute-start.9
  59.1 15.3 %all_to_all.37 = f32[32,1,128]{2,1,0:T(1,128)S(1)} all-to-all(f32[32,1,128]{2,1,0:T(1,128)S(1)} %bitcast.29), channel_id=1, replica_groups=mesh['row'=4,'col'=8] {'row','col'}, dimensions={0} | all-to-all | bytes 32768 | tf_op jit(solution)/shard_map/all_to_all | solution.py:771
  74.4 0.0 collective-permute-done.9.refs_2_.refs_6_
  74.4 0.0 collective-permute-done.10.refs_4_.refs_8_
  74.4 0.6 row_strip_kernel.4
  75.0 0.7 collective-permute-start.11
  75.7 3.4 %collective-permute-start.12 = (f32[128,384]{1,0:T(8,128)S(1)}, f32[128,384]{1,0:T(8,128)S(1)}, u32[]{:S(2)}, u32[]{:S(2)}) collective-permute-start(f32[128,384]{1,0:T(8,128)S(1)} %get-tuple-element.112), channel_id=1, source_target_pairs={{0,8},{16,24},{8,0},{24,16},{1,9},{17,25},{9,1},{25,17},{2,10},{18... | collective-permute-start | bytes 589832 | tf_op jit(solution)/shard_map/ppermute | solution.py:665
  79.2 1.7 %middle_kernel.5 = (f32[896,384]{1,0:T(8,128)S(1)}, f32[640,384]{1,0:T(8,128)S(1)}, f32[3,8,128]{2,1,0:T(8,128)S(1)}) custom-call(s32[4]{0:T(128)S(1)} %get-tuple-element.131.refs_1_.refs_0_, f32[4,2,256,256]{3,2,1,0:T(8,128)S(1)} %spectra_kernel.1.refs_1_, bf16[512,256]{1,0:T(8,128)(2,1)S(1)} %copy-done.3, bf16[512,256]{1,0:T(8,128)(2,1)S(1)} %copy-done.2, ...), custom_call_target="tpu_custom_call" | custom-call | tf_op jit(solution)/shard_map/middle_kernel/pallas_call | solution.py:640
  80.8 0.0 collective-permute-done.11.refs_16_
  80.9 3.0 %collective-permute-done.12.refs_17_ = f32[128,384]{1,0:T(8,128)S(1)} collective-permute-done((f32[128,384]{1,0:T(8,128)S(1)}, f32[128,384]{1,0:T(8,128)S(1)}, u32[]{:S(2)}, u32[]{:S(2)}) %collective-permute-start.12) | collective-permute-done | bytes 196640 | tf_op jit(solution)/shard_map/ppermute | solution.py:665
  83.9 1.4 %edge_kernel.5 = (f32[256,384]{1,0:T(8,128)S(1)}, f32[384,384]{1,0:T(8,128)S(1)}, f32[384,384]{1,0:T(8,128)S(1)}, f32[576,128]{1,0:T(8,128)S(1)}, f32[576,128]{1...) custom-call(s32[4]{0:T(128)S(1)} %get-tuple-element.131.refs_1_.refs_0_, ...), custom_call_target="tpu_custom_call" | custom-call | tf_op jit(solution)/shard_map/edge_kernel/pallas_call | solution.py:640
  85.3 0.7 collective-permute-start.13
  86.0 5.7 %collective-permute-start.14 = (f32[576,128]{1,0:T(8,128)S(1)}, f32[576,128]{1,0:T(8,128)S(1)}, u32[]{:S(2)}, u32[]{:S(2)}) collective-permute-start(f32[576,128]{1,0:T(8,128)S(1)} %get-tuple-element.117), channel_id=1, source_target_pairs={{0,1},{2,3},{4,5},{6,7},{1,0},{3,2},{5,4},{7,6},{8,9},{10,11},{12,... | collective-permute-start | bytes 884744 | tf_op jit(solution)/shard_map/ppermute | solution.py:665
  91.7 9.5 %all_to_all.38 = f32[32,1,128]{2,1,0:T(1,128)S(1)} all-to-all(f32[32,1,128]{2,1,0:T(1,128)S(1)} %bitcast.28), channel_id=1, replica_groups=mesh['row'=4,'col'=8] {'row','col'}, dimensions={0} | all-to-all | bytes 32768 | tf_op jit(solution)/shard_map/all_to_all | solution.py:771
  101.2 0.0 collective-permute-done.13.refs_2_.refs_5_.refs_6_
  101.2 0.0 collective-permute-done.14.refs_3_.refs_6_.refs_7_
  101.2 0.6 row_strip_kernel.5
  101.8 0.7 collective-permute-start.15
  102.5 2.5 %collective-permute-start.16 = (f32[64,256]{1,0:T(8,128)S(1)}, f32[64,256]{1,0:T(8,128)S(1)}, u32[]{:S(2)}, u32[]{:S(2)}) collective-permute-start(f32[64,256]{1,0:T(8,128)S(1)} %get-tuple-element.125), channel_id=1, source_target_pairs={{0,8},{16,24},{8,0},{24,16},{1,9},{17,25},{9,1},{25,17},{2,10},{18... | collective-permute-start | bytes 196616 | tf_op jit(solution)/shard_map/ppermute | solution.py:665
  105.0 2.7 %last_middle_kernel.1 = (f32[1024,256]{1,0:T(8,128)}, f32[1024,256]{1,0:T(8,128)}) custom-call(f32[32,128]{1,0:T(8,128)S(1)} %bitcast.26, f32[640,384]{1,0:T(8,128)S(1)} %get-tuple-element.114.refs_19_.refs_1_, f32[384,384]{1,0:T(8,128)S(1)} %get-tuple-element.120.refs_0_.refs_2_.refs_3_, f32[384,384]{1,0:T(8,128)S(1)} %get-tuple-element.121.refs_1_.refs_3_.refs_4_, ...), custom_call_target="tpu_custom_call" | custom-call | tf_op jit(solution)/shard_map/last_middle_kernel/pallas_call | solution.py:640
  107.6 0.0 collective-permute-done.15.refs_1_
  107.6 0.0 collective-permute-done.16.refs_2_
  107.6 1.7 %last_edge_kernel.1 = (f32[1024,256]{1,0:T(8,128)}, f32[1024,256]{1,0:T(8,128)}) custom-call(f32[32,128]{1,0:T(8,128)S(1)} %bitcast.27, f32[64,256]{1,0:T(8,128)S(1)} %collective-permute-done.15.refs_1_, f32[64,256]{1,0:T(8,128)S(1)} %collective-permute-done.16.refs_2_, ...), custom_call_target="tpu_custom_call", output_to_operand_aliasing={{0}: (12, {}), {1}: (13, {})} | custom-call | tf_op jit(solution)/shard_map/last_edge_kernel/pallas_call | solution.py:640
  (8 shorter events, 0.1 us)
Async XLA Ops:
  0.8 1.2 %copy-start = (f32[1024,256]{1,0:T(8,128)S(1)}, f32[1024,256]{1,0:T(8,128)}, u32[]{:S(2)}) copy-start(f32[1024,256]{1,0:T(8,128)} %refs_9_.3) | copy-start | bytes 3145732
  2.0 7.6 %copy-start.6 = (bf16[384,512]{1,0:T(8,128)(2,1)S(1)}, bf16[384,512]{1,0:T(8,128)(2,1)}, u32[]{:S(2)}) copy-start(bf16[384,512]{1,0:T(8,128)(2,1)} %constant.84.clone.refs_4_) | copy-start | bytes 1179652
  2.0 7.6 %copy-start.7 = (bf16[512,384]{1,0:T(8,128)(2,1)S(1)}, bf16[512,384]{1,0:T(8,128)(2,1)}, u32[]{:S(2)}) copy-start(bf16[512,384]{1,0:T(8,128)(2,1)} %constant.83.clone.refs_3_) | copy-start | bytes 1179652
  2.7 7.7 %collective-permute-start = (f32[512,128]{1,0:T(8,128)S(1)}, f32[512,128]{1,0:T(8,128)S(1)}, u32[]{:S(2)}, u32[]{:S(2)}) collective-permute-start(f32[512,128]{1,0:T(8,128)S(1)} %get-tuple-element.66), channel_id=1, source_target_pairs={{1,2},{3,4},{5,6},{2,1},{4,3},{6,5},{9,10},{11,12},{13,14},{10,9},... | collective-permute-start | bytes 786440 | tf_op jit(solution)/shard_map/ppermute | solution.py:665
  3.4 7.0 %collective-permute-start.1 = (f32[512,128]{1,0:T(8,128)S(1)}, f32[512,128]{1,0:T(8,128)S(1)}, u32[]{:S(2)}, u32[]{:S(2)}) collective-permute-start(f32[512,128]{1,0:T(8,128)S(1)} %get-tuple-element.67), channel_id=1, source_target_pairs={{0,1},{2,3},{4,5},{6,7},{1,0},{3,2},{5,4},{7,6},{8,9},{10,11},{12,... | collective-permute-start | bytes 786440 | tf_op jit(solution)/shard_map/ppermute | solution.py:665
  9.6 1.2 %copy-start.1 = (f32[1024,256]{1,0:T(8,128)S(1)}, f32[1024,256]{1,0:T(8,128)}, u32[]{:S(2)}) copy-start(f32[1024,256]{1,0:T(8,128)} %refs_9_.3) | copy-start | bytes 3145732
  10.4 6.2 %copy-start.2 = (bf16[512,256]{1,0:T(8,128)(2,1)S(1)}, bf16[512,256]{1,0:T(8,128)(2,1)}, u32[]{:S(2)}) copy-start(bf16[512,256]{1,0:T(8,128)(2,1)} %constant.80.clone.refs_3_) | copy-start | bytes 786436
  10.4 6.2 %copy-start.3 = (bf16[512,256]{1,0:T(8,128)(2,1)S(1)}, bf16[512,256]{1,0:T(8,128)(2,1)}, u32[]{:S(2)}) copy-start(bf16[512,256]{1,0:T(8,128)(2,1)} %constant.79.clone.refs_2_) | copy-start | bytes 786436
  10.4 6.2 %copy-start.4 = (bf16[256,128]{1,0:T(8,128)(2,1)S(1)}, bf16[256,128]{1,0:T(8,128)(2,1)}, u32[]{:S(2)}) copy-start(bf16[256,128]{1,0:T(8,128)(2,1)} %constant.82.clone.refs_5_) | copy-start | bytes 196612
  10.4 6.2 %copy-start.5 = (bf16[256,128]{1,0:T(8,128)(2,1)S(1)}, bf16[256,128]{1,0:T(8,128)(2,1)}, u32[]{:S(2)}) copy-start(bf16[256,128]{1,0:T(8,128)(2,1)} %constant.81.clone.refs_4_) | copy-start | bytes 196612
  11.5 6.0 %collective-permute-start.2 = (f32[64,384]{1,0:T(8,128)S(1)}, f32[64,384]{1,0:T(8,128)S(1)}, u32[]{:S(2)}, u32[]{:S(2)}) collective-permute-start(f32[64,384]{1,0:T(8,128)S(1)} %get-tuple-element.76), channel_id=1, source_target_pairs={{8,16},{16,8},{9,17},{17,9},{10,18},{18,10},{11,19},{19,11},{12,20... | collective-permute-start | bytes 294920 | tf_op jit(solution)/shard_map/ppermute | solution.py:665
  12.2 7.1 %collective-permute-start.3 = (f32[64,384]{1,0:T(8,128)S(1)}, f32[64,384]{1,0:T(8,128)S(1)}, u32[]{:S(2)}, u32[]{:S(2)}) collective-permute-start(f32[64,384]{1,0:T(8,128)S(1)} %get-tuple-element.77), channel_id=1, source_target_pairs={{0,8},{16,24},{8,0},{24,16},{1,9},{17,25},{9,1},{25,17},{2,10},{18... | collective-permute-start | bytes 294920 | tf_op jit(solution)/shard_map/ppermute | solution.py:665
  20.1 21.3 %collective-permute-start.4 = (f32[1152,128]{1,0:T(8,128)S(1)}, f32[1152,128]{1,0:T(8,128)S(1)}, u32[]{:S(2)}, u32[]{:S(2)}) collective-permute-start(f32[1152,128]{1,0:T(8,128)S(1)} %get-tuple-element.81), channel_id=1, source_target_pairs={{1,2},{3,4},{5,6},{2,1},{4,3},{6,5},{9,10},{11,12},{13,14},{10,9},... | collective-permute-start | bytes 1769480 | tf_op jit(solution)/shard_map/ppermute | solution.py:665
  20.8 20.6 %collective-permute-start.5 = (f32[1152,128]{1,0:T(8,128)S(1)}, f32[1152,128]{1,0:T(8,128)S(1)}, u32[]{:S(2)}, u32[]{:S(2)}) collective-permute-start(f32[1152,128]{1,0:T(8,128)S(1)} %get-tuple-element.82), channel_id=1, source_target_pairs={{0,1},{2,3},{4,5},{6,7},{1,0},{3,2},{5,4},{7,6},{8,9},{10,11},{12,... | collective-permute-start | bytes 1769480 | tf_op jit(solution)/shard_map/ppermute | solution.py:665
  42.0 7.2 %collective-permute-start.7 = (f32[128,384]{1,0:T(8,128)S(1)}, f32[128,384]{1,0:T(8,128)S(1)}, u32[]{:S(2)}, u32[]{:S(2)}) collective-permute-start(f32[128,384]{1,0:T(8,128)S(1)} %get-tuple-element.91), channel_id=1, source_target_pairs={{8,16},{16,8},{9,17},{17,9},{10,18},{18,10},{11,19},{19,11},{12,20... | collective-permute-start | bytes 589832 | tf_op jit(solution)/shard_map/ppermute | solution.py:665
  42.7 9.2 %collective-permute-start.8 = (f32[128,384]{1,0:T(8,128)S(1)}, f32[128,384]{1,0:T(8,128)S(1)}, u32[]{:S(2)}, u32[]{:S(2)}) collective-permute-start(f32[128,384]{1,0:T(8,128)S(1)} %get-tuple-element.92), channel_id=1, source_target_pairs={{0,8},{16,24},{8,0},{24,16},{1,9},{17,25},{9,1},{25,17},{2,10},{18... | collective-permute-start | bytes 589832 | tf_op jit(solution)/shard_map/ppermute | solution.py:665
  48.5 4.5 %collective-permute-start.6 = (f32[384,128]{1,0:T(8,128)S(1)}, f32[384,128]{1,0:T(8,128)S(1)}, u32[]{:S(2)}, u32[]{:S(2)}) collective-permute-start(f32[384,128]{1,0:T(8,128)S(1)} %get-tuple-element.89), channel_id=1, source_target_pairs={{1,2},{3,4},{5,6},{2,1},{4,3},{6,5},{9,10},{11,12},{13,14},{10,9},... | collective-permute-start | bytes 589832 | tf_op jit(solution)/shard_map/ppermute | solution.py:665
  53.0 21.4 %collective-permute-start.10 = (f32[1152,128]{1,0:T(8,128)S(1)}, f32[1152,128]{1,0:T(8,128)S(1)}, u32[]{:S(2)}, u32[]{:S(2)}) collective-permute-start(f32[1152,128]{1,0:T(8,128)S(1)} %get-tuple-element.101), channel_id=1, source_target_pairs={{0,1},{2,3},{4,5},{6,7},{1,0},{3,2},{5,4},{7,6},{8,9},{10,11},{12,... | collective-permute-start | bytes 1769480 | tf_op jit(solution)/shard_map/ppermute | solution.py:665
  58.4 16.0 %collective-permute-start.9 = (f32[768,128]{1,0:T(8,128)S(1)}, f32[768,128]{1,0:T(8,128)S(1)}, u32[]{:S(2)}, u32[]{:S(2)}) collective-permute-start(f32[768,128]{1,0:T(8,128)S(1)} %get-tuple-element.99), channel_id=1, source_target_pairs={{1,2},{3,4},{5,6},{2,1},{4,3},{6,5},{9,10},{11,12},{13,14},{10,9},... | collective-permute-start | bytes 1179656 | tf_op jit(solution)/shard_map/ppermute | solution.py:665
  75.0 5.8 %collective-permute-start.11 = (f32[128,384]{1,0:T(8,128)S(1)}, f32[128,384]{1,0:T(8,128)S(1)}, u32[]{:S(2)}, u32[]{:S(2)}) collective-permute-start(f32[128,384]{1,0:T(8,128)S(1)} %get-tuple-element.111), channel_id=1, source_target_pairs={{8,16},{16,8},{9,17},{17,9},{10,18},{18,10},{11,19},{19,11},{12,20... | collective-permute-start | bytes 589832 | tf_op jit(solution)/shard_map/ppermute | solution.py:665
  75.7 8.1 %collective-permute-start.12 = (f32[128,384]{1,0:T(8,128)S(1)}, f32[128,384]{1,0:T(8,128)S(1)}, u32[]{:S(2)}, u32[]{:S(2)}) collective-permute-start(f32[128,384]{1,0:T(8,128)S(1)} %get-tuple-element.112), channel_id=1, source_target_pairs={{0,8},{16,24},{8,0},{24,16},{1,9},{17,25},{9,1},{25,17},{2,10},{18... | collective-permute-start | bytes 589832 | tf_op jit(solution)/shard_map/ppermute | solution.py:665
  85.3 15.9 %collective-permute-start.13 = (f32[576,128]{1,0:T(8,128)S(1)}, f32[576,128]{1,0:T(8,128)S(1)}, u32[]{:S(2)}, u32[]{:S(2)}) collective-permute-start(f32[576,128]{1,0:T(8,128)S(1)} %get-tuple-element.116), channel_id=1, source_target_pairs={{1,2},{3,4},{5,6},{2,1},{4,3},{6,5},{9,10},{11,12},{13,14},{10,9},... | collective-permute-start | bytes 884744 | tf_op jit(solution)/shard_map/ppermute | solution.py:665
  86.0 15.2 %collective-permute-start.14 = (f32[576,128]{1,0:T(8,128)S(1)}, f32[576,128]{1,0:T(8,128)S(1)}, u32[]{:S(2)}, u32[]{:S(2)}) collective-permute-start(f32[576,128]{1,0:T(8,128)S(1)} %get-tuple-element.117), channel_id=1, source_target_pairs={{0,1},{2,3},{4,5},{6,7},{1,0},{3,2},{5,4},{7,6},{8,9},{10,11},{12,... | collective-permute-start | bytes 884744 | tf_op jit(solution)/shard_map/ppermute | solution.py:665
  101.8 5.8 %collective-permute-start.15 = (f32[64,256]{1,0:T(8,128)S(1)}, f32[64,256]{1,0:T(8,128)S(1)}, u32[]{:S(2)}, u32[]{:S(2)}) collective-permute-start(f32[64,256]{1,0:T(8,128)S(1)} %get-tuple-element.124), channel_id=1, source_target_pairs={{8,16},{16,8},{9,17},{17,9},{10,18},{18,10},{11,19},{19,11},{12,20... | collective-permute-start | bytes 196616 | tf_op jit(solution)/shard_map/ppermute | solution.py:665
  102.5 5.1 %collective-permute-start.16 = (f32[64,256]{1,0:T(8,128)S(1)}, f32[64,256]{1,0:T(8,128)S(1)}, u32[]{:S(2)}, u32[]{:S(2)}) collective-permute-start(f32[64,256]{1,0:T(8,128)S(1)} %get-tuple-element.125), channel_id=1, source_target_pairs={{0,8},{16,24},{8,0},{24,16},{1,9},{17,25},{9,1},{25,17},{2,10},{18... | collective-permute-start | bytes 196616 | tf_op jit(solution)/shard_map/ppermute | solution.py:665

commit v5 on v4

--- a/solution.py
+++ b/solution.py
@@ -165,33 +165,25 @@
     return lax.broadcasted_iota(jnp.int32, (1, THIRD), 1) < HALF
 
 
-def apply_spectrum(low_rows, high_rows, spec_ref, slot):
+def apply_spectrum(low_rows, high_rows, spec_ref, slot, mixed):
+    lanes = pl.ds(0 if mixed else THIRD, THIRD)
     sign = jnp.where(lane_mask(), -1.0, 1.0).astype(F32)
 
     def band(cos_rows, sin_rows, cos_at, sin_at, size):
-        pc = spec_ref[slot, 0, pl.ds(cos_at, size), :]
-        ps = spec_ref[slot, 0, pl.ds(sin_at, size), :] if sin_at != cos_at else pc
-        cross = spec_ref[slot, 1, pl.ds(cos_at, size), :]
-        d0, d1 = cross[:, :THIRD] * sign, cross[:, THIRD:]
-        c0, c1, c2 = (tile_of(cos_rows, i) for i in range(3))
-        s0, s1, s2 = (tile_of(sin_rows, i) for i in range(3))
-        new_cos = jnp.concatenate(
-            [
-                pc[:, :THIRD] * c0 + d0 * pltpu.roll(s0, HALF, 1),
-                pc[:, THIRD:] * c1 - d1 * s2,
-                pc[:, THIRD:] * c2 + d1 * s1,
-            ],
-            1,
+        pc = spec_ref[slot, 0, pl.ds(cos_at, size), lanes]
+        ps = spec_ref[slot, 0, pl.ds(sin_at, size), lanes] if sin_at != cos_at else pc
+        cross = spec_ref[slot, 1, pl.ds(cos_at, size), lanes]
+        if mixed:
+            cross = cross * sign
+            return (
+                pc * cos_rows + cross * pltpu.roll(sin_rows, HALF, 1),
+                ps * sin_rows - cross * pltpu.roll(cos_rows, HALF, 1),
+            )
+        c1, c2, s1, s2 = cos_rows[:, :THIRD], cos_rows[:, THIRD:], sin_rows[:, :THIRD], sin_rows[:, THIRD:]
+        return (
+            jnp.concatenate([pc * c1 - cross * s2, pc * c2 + cross * s1], 1),
+            jnp.concatenate([ps * s1 + cross * c2, ps * s2 - cross * c1], 1),
         )
-        new_sin = jnp.concatenate(
-            [
-                ps[:, :THIRD] * s0 - d0 * pltpu.roll(c0, HALF, 1),
-                ps[:, THIRD:] * s1 + d1 * c2,
-                ps[:, THIRD:] * s2 - d1 * c1,
-            ],
-            1,
-        )
-        return new_cos, new_sin
 
     low = band(low_rows[:HALF], low_rows[HALF:], 0, HALF, HALF)
     high = band(high_rows[:THIRD], high_rows[THIRD:], THIRD, THIRD, THIRD)
@@ -200,42 +192,45 @@
 
 def window_products(windows, slots, r):
     count = len(windows)
-    parts = []
-    for blocks in windows:
-        halves = []
-        for block in blocks:
-            plain, real, diff = butterfly(*(tile_of(block, i) for i in range(3)))
-            halves.append(
-                jnp.concatenate(
-                    [
-                        right_small(plain, r.small_t),
-                        right_large(jnp.concatenate([real, diff], 1), r.large_t),
-                    ],
-                    1,
-                )
-            )
-        parts.append(butterfly(*halves))
-    plain, real, diff = (jnp.concatenate([part[i] for part in parts], 1) for i in range(3))
-    low_rows = left_small(plain, r.small)
-    high_rows = left_large(jnp.concatenate([real, diff], 0), r.large)
-    bands = []
-    for num, slot in enumerate(slots):
-        here = slice(num * WIN, (num + 1) * WIN)
-        bands.append(apply_spectrum(low_rows[:, here], high_rows[:, here], r.spec, slot))
-    low_rows, high_rows = (jnp.concatenate([band[i] for band in bands], 1) for i in range(2))
-    plain = left_small(low_rows, r.small_t)
-    both = left_large(high_rows, r.large_t)
-    rows = unbutterfly(plain, both[:THIRD], both[THIRD:])
+    folded = [
+        [butterfly(*(tile_of(block, i) for i in range(3))) for block in blocks] for blocks in windows
+    ]
+    small = [[right_small(plain, r.small_t) for plain, _, _ in blocks] for blocks in folded]
+    large = [
+        [right_large(jnp.concatenate([real, diff], 1), r.large_t) for _, real, diff in blocks]
+        for blocks in folded
+    ]
+
+    def to_rows(windows):
+        parts = [butterfly(*blocks) for blocks in windows]
+        plain, real, diff = (jnp.concatenate([part[i] for part in parts], 1) for i in range(3))
+        return left_small(plain, r.small), left_large(jnp.concatenate([real, diff], 0), r.large)
+
+    def from_rows_of(bands, mixed):
+        width = THIRD if mixed else 2 * THIRD
+        done = []
+        for num, slot in enumerate(slots):
+            here = slice(num * width, (num + 1) * width)
+            done.append(apply_spectrum(bands[0][:, here], bands[1][:, here], r.spec, slot, mixed))
+        low_rows, high_rows = (jnp.concatenate([band[i] for band in done], 1) for i in range(2))
+        plain = left_small(low_rows, r.small_t)
+        both = left_large(high_rows, r.large_t)
+        return unbutterfly(plain, both[:THIRD], both[THIRD:])
+
+    small_bands, large_bands = to_rows(small), to_rows(large)
+    small = from_rows_of(small_bands, True)
+    large = from_rows_of(large_bands, False)
+    plain = [[right_small(tile_of(block, num), r.small) for block in small] for num in range(count)]
     results = []
     for num in range(count):
-        here = slice(num * WIN, (num + 1) * WIN)
-        result = []
-        for block in rows:
-            block = block[:, here]
-            plain = right_small(block[:, :THIRD], r.small)
-            both = right_large(block[:, THIRD:], r.large)
-            result.append(jnp.concatenate(unbutterfly(plain, both[:, :THIRD], both[:, THIRD:]), 1))
-        results.append(result)
+        here = slice(2 * num * THIRD, 2 * (num + 1) * THIRD)
+        both = [right_large(block[:, here], r.large) for block in large]
+        results.append(
+            [
+                jnp.concatenate(unbutterfly(a, b[:, :THIRD], b[:, THIRD:]), 1)
+                for a, b in zip(plain[num], both)
+            ]
+        )
     return results
 
 
@@ -277,20 +272,32 @@
     return terms
 
 
-def scalars(r):
+ENERGY, POWER, STEP, RATIO, BACK = 0, 1, 2, 2 + ITERS, 2 + 2 * ITERS
+COEFS = (3 + 2 * ITERS, 8, THIRD)
+
+
+def put_scalars(r):
     sums = jnp.sum(r.parts[...], 0, keepdims=True)
     energy, curve, cross = sums[:, 0:1], sums[:, 1:2], sums[:, 2:3]
-    if r.stage == 1:
-        r.steps, r.ratios = [energy / curve], []
-        return energy, curve
-    past = r.coef[0:1, :]
-    ratio = energy / past[:, 0:1]
-    power = curve + ratio * (2.0 * cross + ratio * past[:, 1:2])
-    before = r.stage - 1
-    r.steps = [past[:, 2 + i : 3 + i] for i in range(before)] + [energy / power]
-    r.ratios = [past[:, 2 + ITERS + i : 3 + ITERS + i] for i in range(before - 1)] + [ratio]
-    r.back = ratio / r.steps[-2]
-    return energy, power
+    values = {ENERGY: energy, POWER: curve}
+    last = r.stage - 1
+    if last:
+        ratio = energy / r.coef[ENERGY, 0:1, 0:1]
+        values[POWER] = curve + ratio * (2.0 * cross + ratio * r.coef[POWER, 0:1, 0:1])
+        values[RATIO + last] = ratio
+        values[BACK] = ratio / r.coef[STEP + last - 1, 0:1, 0:1]
+        for num in range(last):
+            r.coef_new[STEP + num] = r.coef[STEP + num]
+            r.coef_new[RATIO + num] = r.coef[RATIO + num]
+    values[STEP + last] = energy / values[POWER]
+    for num, value in values.items():
+        r.coef_new[num] = jnp.broadcast_to(value, (8, THIRD))
+
+
+def take_scalars(r, coef):
+    r.steps = [coef[STEP + i, 0:1, :] for i in range(r.stage)]
+    r.ratios = [coef[RATIO + i, 0:1, :] for i in range(1, r.stage)]
+    r.back = coef[BACK, 0:1, :] if r.stage > 1 else None
 
 
 def pick(odd, first, second):
@@ -426,13 +433,16 @@
             ]
         strips.append([tile_of(own, i) + a for i, a in enumerate(add)])
     send_rows(r, *strips)
+    if r.narrow:
+        put_scalars(r)
 
 
 def middle_kernel(r):
     square = cross = jnp.zeros((8, THIRD), F32)
     blocks = 2 * r.tiles + 1
     if r.stage > 0:
-        scalars(r)
+        put_scalars(r)
+        take_scalars(r, r.coef_new)
     for num in range(1, blocks - 1):
         here = rows_at(num - 1)
         if r.stage == 0:
@@ -480,9 +490,7 @@
     blocks = 2 * r.tiles + 1
     rows = 2 * r.tiles * THIRD
     if r.stage > 0:
-        energy, power = scalars(r)
-        fill = [jnp.zeros_like(energy)] * (ITERS - len(r.steps))
-        r.coef_new[...] = lanes_of((8, THIRD), energy, power, *r.steps, *fill, *r.ratios)
+        take_scalars(r, r.coef)
     for side in range(2):
         num = side * (blocks - 1)
         for offset in (0, HALO):
@@ -595,13 +603,13 @@
 
 
 def last_middle_kernel(r):
-    scalars(r)
+    take_scalars(r, r.coef)
     for start in range(THIRD, 2 * r.tiles * THIRD, HALO):
         last_rows(r, start, r.corrected, r.residual, start - HALO)
 
 
 def last_edge_kernel(r):
-    scalars(r)
+    take_scalars(r, r.coef)
     rows = 2 * r.tiles * THIRD
     copies = []
     for side in range(2):
@@ -704,10 +712,9 @@
         moving = dict(sides)
         if stage == 0:
             moving["observed"] = observed
-        else:
-            moving["parts"] = parts
+        known = dict(parts=parts) if stage else {}
         if stage > 1:
-            moving["coef"] = state["coef_new"]
+            known["coef"] = coef
 
         def old(where, *sums):
             names = ["res%d_%s" % (i, where) for i in range(stage)]
@@ -715,11 +722,12 @@
 
         middle = run(
             middle_kernel,
-            {**fixed, **moving, **old("mid", "top_sum", "mid_sum", "low_sum")},
+            {**fixed, **moving, **known, **old("mid", "top_sum", "mid_sum", "low_sum")},
             {
                 "res_mid_new": (mid, WIN),
                 "mid_sum_new": (mid - TILE, WIN),
                 "acc": (3, 8, THIRD),
+                **(dict(coef_new=COEFS) if stage else {}),
                 **({"to_mid": (ext - 2 * WIN, THIRD)} if parted else {}),
             },
             stage=stage,
@@ -732,13 +740,12 @@
         outs["to_a"] = (ext // 2 if narrow else ext, THIRD)
         outs["to_end" if parted else "to_b"] = (2 * WIN if parted else outs["to_a"][0], THIRD)
         outs["part"] = (devices, THIRD)
-        if stage:
-            outs["coef_new"] = (8, THIRD)
         edges = run(
             edge_kernel,
             {
                 **fixed,
                 **moving,
+                **(dict(coef=middle["coef_new"]) if stage else {}),
                 **old("edge", "top_sum", "low_sum"),
                 "row_b": row_b,
                 "row_a": row_a,
@@ -756,7 +763,6 @@
         state["mid_sum"] = middle["mid_sum_new"]
         state["top_sum"] = edges["top_sum_new"]
         state["low_sum"] = edges["low_sum_new"]
-        state["coef_new"] = edges.get("coef_new")
         part, to_a = edges["part"], edges["to_a"]
         sides = {}
         if parted:
@@ -772,10 +778,17 @@
         sides, parts = lax.optimization_barrier((sides, parts))
         sides["edge"] = edge
         strip = (HALO, TILE) if narrow else (THIRD, WIN)
+        coef = middle.get("coef_new")
         sent = run(
             row_strip_kernel,
-            dict(top_sum=state["top_sum"], low_sum=state["low_sum"], **sides),
-            dict(to_a=strip, to_b=strip),
+            dict(
+                **(dict(parts=parts, coef=coef) if narrow else {}),
+                top_sum=state["top_sum"],
+                low_sum=state["low_sum"],
+                **sides,
+            ),
+            dict(to_a=strip, to_b=strip, **(dict(coef_new=COEFS) if narrow else {})),
+            stage=stage + 1,
             tiles=tiles,
             narrow=narrow,
         )
@@ -784,18 +797,18 @@
     def olds(where):
         return {name: state[name] for name in ["res%d_%s" % (i, where) for i in range(ITERS)]}
 
-    ends = {name: state[name] for name in ("coef_new", "top_sum", "low_sum")}
-    ends["coef"] = ends.pop("coef_new")
+    coef = sent["coef_new"]
+    ends = dict(top_sum=state["top_sum"], low_sum=state["low_sum"])
     out = run(
         last_middle_kernel,
-        dict(parts=parts, mid_sum=state["mid_sum"], **ends, **sides, **olds("mid")),
+        dict(coef=coef, mid_sum=state["mid_sum"], **ends, **sides, **olds("mid")),
         dict(corrected=(rows, cols), residual=(rows, cols)),
         stage=ITERS,
         tiles=tiles,
     )
     out = run(
         last_edge_kernel,
-        dict(parts=parts, row_b=row_b, row_a=row_a, **ends, **sides, **olds("edge")),
+        dict(coef=coef, row_b=row_b, row_a=row_a, **ends, **sides, **olds("edge")),
         {},
         dict(
             corrected_rows=(2 * HALO, cols),

time: 109 us -> 108 us (level); the launches traced: 109 us -> 107 us
  starting transfers between devices: 42.9 us -> 35.7 us
  Pallas kernels: 15.6 us -> 21.5 us
    ppermute x17, starting transfers between devices: 42.9 us -> 35.7 us  [swap(): return lax.ppermute(value, axis, pairs + [(b, a) for a, b in pairs])]
    pallas_call x14, Pallas kernels: 15.6 us -> 21.5 us  [run(): pl.pallas_call(kernel, name=body.__name__, out_shape=[jax.ShapeDtypeStruc...]
  transfers between devices with their start and end apart: 17 -> 17, of which waited for: 3 -> 3; matrix products, arithmetic and copies ran while one was open for 2% -> 2% of each run, Pallas kernels for 8% -> 10%
where the time goes in v5:
time: 108 us; the launch traced here: 107 us
  blocking collectives  38.3 us (35%)
  starting transfers between devices  35.7 us (33%)
  Pallas kernels  21.5 us (20%)
  waiting for transfers between devices  7.41 us (7%)
  local copies, waits for them, and re-layouts  3.2 us (3%)
  between operations  1.1 us (1%)
    all_to_all x3, blocking collectives, shards(): parts = lax.all_to_all(part, ('row', 'col'), 0, 0, tiled=True)  38.3 us
    ppermute x17, starting transfers between devices, swap(): return lax.ppermute(value, axis, pairs + [(b, a) for a, b in pairs])  35.7 us
    pallas_call x14, Pallas kernels, run(): pl.pallas_call(kernel, name=body.__name__, out_shape=[jax.ShapeDtypeStruc...  21.5 us
    ppermute x17, waiting for transfers between devices, swap(): return lax.ppermute(value, axis, pairs + [(b, a) for a, b in pairs])  7.41 us
    unnamed x17, local copies, waits for them, and re-layouts  2.27 us
  transfers between devices with their start and end apart: 17, of which 3 were waited for; matrix products, arithmetic and copies ran while one was open for 2% of the time, Pallas kernels for 10%

profile of v5, /device:TPU:0, one launch (start us, length us, event | category | flops | bytes accessed | tf_op | source)
XLA Modules:
  0.0 107.2 jit_solution(8076157200211372760)
XLA Ops:
  0.7 0.1 stack.27
  0.8 1.2 %copy-done = f32[1024,256]{1,0:T(8,128)S(1)} copy-done((f32[1024,256]{1,0:T(8,128)S(1)}, f32[1024,256]{1,0:T(8,128)}, u32[]{:S(2)}) %copy-start) | copy-done | bytes 1048600
  2.0 0.7 pack_kernel.1
  2.7 0.7 collective-permute-start
  3.4 4.3 %collective-permute-start.1 = (f32[512,128]{1,0:T(8,128)S(1)}, f32[512,128]{1,0:T(8,128)S(1)}, u32[]{:S(2)}, u32[]{:S(2)}) collective-permute-start(f32[512,128]{1,0:T(8,128)S(1)} %get-tuple-element.68), channel_id=1, source_target_pairs={{0,1},{2,3},{4,5},{6,7},{1,0},{3,2},{5,4},{7,6},{8,9},{10,11},{12,... | collective-permute-start | bytes 786440 | tf_op jit(solution)/shard_map/ppermute | solution.py:673
  7.8 1.0 copy.15
  8.8 0.8 dynamic-slice_bitcast_fusion
  9.6 0.0 copy-done.6
  9.6 0.0 copy-done.7
  9.6 1.3 %spectra_kernel.1.refs_1_ = f32[4,2,256,256]{3,2,1,0:T(8,128)S(1)} custom-call(s32[4]{0:T(128)S(1)} %get-tuple-element.132.refs_0_, s32[4]{0:T(128)S(1)} %get-tuple-element.133.refs_1_.refs_0_, f32[8,128,128]{2,1,0:T(8,128)S(1)} %pad.4.refs_2_, bf16[512,384]{1,0:T(8,128)(2,1)S(1)} %copy-done.7, bf16[384,512]{1,0:T(8,128)(2,1)S(1)} %copy-done.6), custom_call_target="tpu_custom_call" | custom-call | tf_op jit(solution)/shard_map/spectra_kernel/pallas_call | solution.py:648
  11.0 0.0 copy-start.2
  11.0 0.0 copy-start.3
  11.0 0.0 copy-start.4
  11.0 0.0 copy-start.5
  11.0 0.0 collective-permute-done.refs_2_.refs_7_
  11.0 0.0 collective-permute-done.1.refs_3_.refs_8_
  11.0 0.0 copy-done.1
  11.0 0.6 halo_kernel.1
  11.7 0.7 collective-permute-start.2
  12.4 4.6 %collective-permute-start.3 = (f32[64,384]{1,0:T(8,128)S(1)}, f32[64,384]{1,0:T(8,128)S(1)}, u32[]{:S(2)}, u32[]{:S(2)}) collective-permute-start(f32[64,384]{1,0:T(8,128)S(1)} %get-tuple-element.78), channel_id=1, source_target_pairs={{0,8},{16,24},{8,0},{24,16},{1,9},{17,25},{9,1},{25,17},{2,10},{18... | collective-permute-start | bytes 294920 | tf_op jit(solution)/shard_map/ppermute | solution.py:673
  16.9 0.0 copy-done.2
  16.9 0.0 copy-done.4
  17.0 0.9 middle_kernel.3
  17.8 0.0 collective-permute-done.2.refs_10_
  17.8 1.7 %collective-permute-done.3.refs_11_ = f32[64,384]{1,0:T(8,128)S(1)} collective-permute-done((f32[64,384]{1,0:T(8,128)S(1)}, f32[64,384]{1,0:T(8,128)S(1)}, u32[]{:S(2)}, u32[]{:S(2)}) %collective-permute-start.3) | collective-permute-done | bytes 98336 | tf_op jit(solution)/shard_map/ppermute | solution.py:673
  19.5 2.9 %edge_kernel.3 = (f32[256,384]{1,0:T(8,128)S(1)}, f32[384,384]{1,0:T(8,128)S(1)}, f32[384,384]{1,0:T(8,128)S(1)}, f32[1152,128]{1,0:T(8,128)S(1)}, f32[1152,128]{1,0:T(8,128)S(1)}, /*index=5*/f32[32,128]{1,0:T(8,128)S(1)}) custom-call(s32[4]{0:T(128)S(1)} %get-tuple-element.133.refs_1_.refs_0_, f32[4,2,256,256]{3,2,1,0:T(8,128)S(1)} %spectra_kernel.1.refs_1_, ...), custom_call_target="tpu_custom_call" | custom-call | tf_op jit(solution)/shard_map/edge_kernel/pallas_call | solution.py:648
  22.4 0.7 collective-permute-start.4
  23.1 4.0 %collective-permute-start.5 = (f32[1152,128]{1,0:T(8,128)S(1)}, f32[1152,128]{1,0:T(8,128)S(1)}, u32[]{:S(2)}, u32[]{:S(2)}) collective-permute-start(f32[1152,128]{1,0:T(8,128)S(1)} %get-tuple-element.83), channel_id=1, source_target_pairs={{0,1},{2,3},{4,5},{6,7},{1,0},{3,2},{5,4},{7,6},{8,9},{10,11},{12,... | collective-permute-start | bytes 1769480 | tf_op jit(solution)/shard_map/ppermute | solution.py:673
  27.1 14.5 %all_to_all.36 = f32[32,1,128]{2,1,0:T(1,128)S(1)} all-to-all(f32[32,1,128]{2,1,0:T(1,128)S(1)} %bitcast.27), channel_id=1, replica_groups=mesh['row'=4,'col'=8] {'row','col'}, dimensions={0} | all-to-all | bytes 32768 | tf_op jit(solution)/shard_map/all_to_all | solution.py:777
  41.6 0.0 collective-permute-done.4.refs_6_.refs_2_
  41.6 0.0 collective-permute-done.5.refs_7_.refs_3_
  41.6 0.6 row_strip_kernel.3
  42.3 0.7 collective-permute-start.7
  42.9 4.5 %collective-permute-start.8 = (f32[128,384]{1,0:T(8,128)S(1)}, f32[128,384]{1,0:T(8,128)S(1)}, u32[]{:S(2)}, u32[]{:S(2)}) collective-permute-start(f32[128,384]{1,0:T(8,128)S(1)} %get-tuple-element.94), channel_id=1, source_target_pairs={{0,8},{16,24},{8,0},{24,16},{1,9},{17,25},{9,1},{25,17},{2,10},{18... | collective-permute-start | bytes 589832 | tf_op jit(solution)/shard_map/ppermute | solution.py:673
  47.5 1.3 %middle_kernel.4 = (f32[896,384]{1,0:T(8,128)S(1)}, f32[640,384]{1,0:T(8,128)S(1)}, f32[3,8,128]{2,1,0:T(8,128)S(1)}, f32[9,8,128]{2,1,0:T(8,128)S(1)}, f32[384,128]{1,0:T(8,128)S(1)}) custom-call(s32[4]{0:T(128)S(1)} %get-tuple-element.133.refs_1_.refs_0_, f32[4,2,256,256]{3,2,1,0:T(8,128)S(1)} %spectra_kernel.1.refs_1_, bf16[512,256]{1,0:T(8,128)(2,1)S(1)} %copy-done.3, ...), custom_call_target="tpu_custom_call" | custom-call | tf_op jit(solution)/shard_map/middle_kernel/pallas_call | solution.py:648
  48.8 0.7 collective-permute-start.6
  49.5 0.0 collective-permute-done.7.refs_13_
  49.5 2.6 %collective-permute-done.8.refs_14_ = f32[128,384]{1,0:T(8,128)S(1)} collective-permute-done((f32[128,384]{1,0:T(8,128)S(1)}, f32[128,384]{1,0:T(8,128)S(1)}, u32[]{:S(2)}, u32[]{:S(2)}) %collective-permute-start.8) | collective-permute-done | bytes 196640 | tf_op jit(solution)/shard_map/ppermute | solution.py:673
  52.1 3.0 %edge_kernel.4 = (f32[256,384]{1,0:T(8,128)S(1)}, f32[384,384]{1,0:T(8,128)S(1)}, f32[384,384]{1,0:T(8,128)S(1)}, f32[1152,128]{1,0:T(8,128)S(1)}, f32[768,128]{1,0:T(8,128)S(1)}, /*index=5*/f32[32,128]{1,0:T(8,128)S(1)}) custom-call(s32[4]{0:T(128)S(1)} %get-tuple-element.133.refs_1_.refs_0_, f32[4,2,256,256]{3,2,1,0:T(8,128)S(1)} %spectra_kernel.1.refs_1_, ...), custom_call_target="tpu_custom_call" | custom-call | tf_op jit(solution)/shard_map/edge_kernel/pallas_call | solution.py:648
  55.1 0.0 collective-permute-done.6.refs_7_.refs_3_
  55.1 4.0 %collective-permute-start.10 = (f32[1152,128]{1,0:T(8,128)S(1)}, f32[1152,128]{1,0:T(8,128)S(1)}, u32[]{:S(2)}, u32[]{:S(2)}) collective-permute-start(f32[1152,128]{1,0:T(8,128)S(1)} %get-tuple-element.103), channel_id=1, source_target_pairs={{0,1},{2,3},{4,5},{6,7},{1,0},{3,2},{5,4},{7,6},{8,9},{10,11},{12,... | collective-permute-start | bytes 1769480 | tf_op jit(solution)/shard_map/ppermute | solution.py:673
  59.1 0.7 collective-permute-start.9
  59.8 12.9 %all_to_all.37 = f32[32,1,128]{2,1,0:T(1,128)S(1)} all-to-all(f32[32,1,128]{2,1,0:T(1,128)S(1)} %bitcast.26), channel_id=1, replica_groups=mesh['row'=4,'col'=8] {'row','col'}, dimensions={0} | all-to-all | bytes 32768 | tf_op jit(solution)/shard_map/all_to_all | solution.py:777
  72.7 0.0 collective-permute-done.9.refs_6_.refs_2_
  72.7 0.0 collective-permute-done.10.refs_8_.refs_4_
  72.7 0.6 row_strip_kernel.4
  73.4 0.9 collective-permute-start.11
  74.2 2.1 %collective-permute-start.12 = (f32[128,384]{1,0:T(8,128)S(1)}, f32[128,384]{1,0:T(8,128)S(1)}, u32[]{:S(2)}, u32[]{:S(2)}) collective-permute-start(f32[128,384]{1,0:T(8,128)S(1)} %get-tuple-element.114), channel_id=1, source_target_pairs={{0,8},{16,24},{8,0},{24,16},{1,9},{17,25},{9,1},{25,17},{2,10},{18... | collective-permute-start | bytes 589832 | tf_op jit(solution)/shard_map/ppermute | solution.py:673
  76.3 1.7 %middle_kernel.5 = (f32[896,384]{1,0:T(8,128)S(1)}, f32[640,384]{1,0:T(8,128)S(1)}, f32[3,8,128]{2,1,0:T(8,128)S(1)}, f32[9,8,128]{2,1,0:T(8,128)S(1)}) custom-call(s32[4]{0:T(128)S(1)} %get-tuple-element.133.refs_1_.refs_0_, f32[4,2,256,256]{3,2,1,0:T(8,128)S(1)} %spectra_kernel.1.refs_1_, bf16[512,256]{1,0:T(8,128)(2,1)S(1)} %copy-done.3, ...), custom_call_target="tpu_custom_call" | custom-call | tf_op jit(solution)/shard_map/middle_kernel/pallas_call | solution.py:648
  78.0 0.0 collective-permute-done.11.refs_15_
  78.0 3.1 %collective-permute-done.12.refs_16_ = f32[128,384]{1,0:T(8,128)S(1)} collective-permute-done((f32[128,384]{1,0:T(8,128)S(1)}, f32[128,384]{1,0:T(8,128)S(1)}, u32[]{:S(2)}, u32[]{:S(2)}) %collective-permute-start.12) | collective-permute-done | bytes 196640 | tf_op jit(solution)/shard_map/ppermute | solution.py:673
  81.1 3.1 %edge_kernel.5 = (f32[256,384]{1,0:T(8,128)S(1)}, f32[384,384]{1,0:T(8,128)S(1)}, f32[384,384]{1,0:T(8,128)S(1)}, f32[576,128]{1,0:T(8,128)S(1)}, f32[576,128]{1,0:T(8,128)S(1)}, /*index=5*/f32[32,128]{1,0:T(8,128)S(1)}) custom-call(s32[4]{0:T(128)S(1)} %get-tuple-element.133.refs_1_.refs_0_, f32[4,2,256,256]{3,2,1,0:T(8,128)S(1)} %spectra_kernel.1.refs_1_, ...), custom_call_target="tpu_custom_call" | custom-call | tf_op jit(solution)/shard_map/edge_kernel/pallas_call | solution.py:648
  84.2 0.7 collective-permute-start.13
  84.9 3.4 %collective-permute-start.14 = (f32[576,128]{1,0:T(8,128)S(1)}, f32[576,128]{1,0:T(8,128)S(1)}, u32[]{:S(2)}, u32[]{:S(2)}) collective-permute-start(f32[576,128]{1,0:T(8,128)S(1)} %get-tuple-element.119), channel_id=1, source_target_pairs={{0,1},{2,3},{4,5},{6,7},{1,0},{3,2},{5,4},{7,6},{8,9},{10,11},{12,... | collective-permute-start | bytes 884744 | tf_op jit(solution)/shard_map/ppermute | solution.py:673
  88.3 10.9 %all_to_all.38 = f32[32,1,128]{2,1,0:T(1,128)S(1)} all-to-all(f32[32,1,128]{2,1,0:T(1,128)S(1)} %bitcast.25), channel_id=1, replica_groups=mesh['row'=4,'col'=8] {'row','col'}, dimensions={0} | all-to-all | bytes 32768 | tf_op jit(solution)/shard_map/all_to_all | solution.py:777
  99.2 0.0 collective-permute-done.13.refs_4_.refs_5_
  99.2 0.0 collective-permute-done.14.refs_5_.refs_6_
  99.2 0.9 row_strip_kernel.5
  100.1 0.7 collective-permute-start.15
  100.7 2.5 %collective-permute-start.16 = (f32[64,256]{1,0:T(8,128)S(1)}, f32[64,256]{1,0:T(8,128)S(1)}, u32[]{:S(2)}, u32[]{:S(2)}) collective-permute-start(f32[64,256]{1,0:T(8,128)S(1)} %get-tuple-element.128), channel_id=1, source_target_pairs={{0,8},{16,24},{8,0},{24,16},{1,9},{17,25},{9,1},{25,17},{2,10},{18... | collective-permute-start | bytes 196616 | tf_op jit(solution)/shard_map/ppermute | solution.py:673
  103.2 2.4 %last_middle_kernel.1 = (f32[1024,256]{1,0:T(8,128)}, f32[1024,256]{1,0:T(8,128)}) custom-call(f32[9,8,128]{2,1,0:T(8,128)S(1)} %get-tuple-element.126.refs_0_, f32[640,384]{1,0:T(8,128)S(1)} %get-tuple-element.116.refs_18_.refs_1_, f32[384,384]{1,0:T(8,128)S(1)} %get-tuple-element.122.refs_2_.refs_3_, f32[384,384]{1,0:T(8,128)S(1)} %get-tuple-element.123.refs_3_.refs_4_, ...), custom_call_target="tpu_custom_call" | custom-call | tf_op jit(solution)/shard_map/last_middle_kernel/pallas_call | solution.py:648
  105.7 0.0 collective-permute-done.15.refs_1_
  105.7 0.0 collective-permute-done.16.refs_2_
  105.7 1.4 %last_edge_kernel.1 = (f32[1024,256]{1,0:T(8,128)}, f32[1024,256]{1,0:T(8,128)}) custom-call(f32[9,8,128]{2,1,0:T(8,128)S(1)} %get-tuple-element.126.refs_0_, f32[64,256]{1,0:T(8,128)S(1)} %collective-permute-done.15.refs_1_, f32[64,256]{1,0:T(8,128)S(1)} %collective-permute-done.16.refs_2_, ...), custom_call_target="tpu_custom_call", output_to_operand_aliasing={{0}: (11, {}), {1}: (12, {})} | custom-call | tf_op jit(solution)/shard_map/last_edge_kernel/pallas_call | solution.py:648
  (8 shorter events, 0.1 us)
Async XLA Ops:
  0.8 1.2 %copy-start = (f32[1024,256]{1,0:T(8,128)S(1)}, f32[1024,256]{1,0:T(8,128)}, u32[]{:S(2)}) copy-start(f32[1024,256]{1,0:T(8,128)} %refs_9_.3) | copy-start | bytes 3145732
  2.0 7.6 %copy-start.6 = (bf16[384,512]{1,0:T(8,128)(2,1)S(1)}, bf16[384,512]{1,0:T(8,128)(2,1)}, u32[]{:S(2)}) copy-start(bf16[384,512]{1,0:T(8,128)(2,1)} %constant.84.clone.refs_4_) | copy-start | bytes 1179652
  2.0 7.6 %copy-start.7 = (bf16[512,384]{1,0:T(8,128)(2,1)S(1)}, bf16[512,384]{1,0:T(8,128)(2,1)}, u32[]{:S(2)}) copy-start(bf16[512,384]{1,0:T(8,128)(2,1)} %constant.83.clone.refs_3_) | copy-start | bytes 1179652
  2.7 8.3 %collective-permute-start = (f32[512,128]{1,0:T(8,128)S(1)}, f32[512,128]{1,0:T(8,128)S(1)}, u32[]{:S(2)}, u32[]{:S(2)}) collective-permute-start(f32[512,128]{1,0:T(8,128)S(1)} %get-tuple-element.67), channel_id=1, source_target_pairs={{1,2},{3,4},{5,6},{2,1},{4,3},{6,5},{9,10},{11,12},{13,14},{10,9},... | collective-permute-start | bytes 786440 | tf_op jit(solution)/shard_map/ppermute | solution.py:673
  3.4 7.6 %collective-permute-start.1 = (f32[512,128]{1,0:T(8,128)S(1)}, f32[512,128]{1,0:T(8,128)S(1)}, u32[]{:S(2)}, u32[]{:S(2)}) collective-permute-start(f32[512,128]{1,0:T(8,128)S(1)} %get-tuple-element.68), channel_id=1, source_target_pairs={{0,1},{2,3},{4,5},{6,7},{1,0},{3,2},{5,4},{7,6},{8,9},{10,11},{12,... | collective-permute-start | bytes 786440 | tf_op jit(solution)/shard_map/ppermute | solution.py:673
  9.6 1.4 %copy-start.1 = (f32[1024,256]{1,0:T(8,128)S(1)}, f32[1024,256]{1,0:T(8,128)}, u32[]{:S(2)}) copy-start(f32[1024,256]{1,0:T(8,128)} %refs_9_.3) | copy-start | bytes 3145732
  11.0 6.0 %copy-start.2 = (bf16[512,256]{1,0:T(8,128)(2,1)S(1)}, bf16[512,256]{1,0:T(8,128)(2,1)}, u32[]{:S(2)}) copy-start(bf16[512,256]{1,0:T(8,128)(2,1)} %constant.80.clone.refs_3_) | copy-start | bytes 786436
  11.0 6.0 %copy-start.3 = (bf16[512,256]{1,0:T(8,128)(2,1)S(1)}, bf16[512,256]{1,0:T(8,128)(2,1)}, u32[]{:S(2)}) copy-start(bf16[512,256]{1,0:T(8,128)(2,1)} %constant.79.clone.refs_2_) | copy-start | bytes 786436
  11.0 6.0 %copy-start.4 = (bf16[256,128]{1,0:T(8,128)(2,1)S(1)}, bf16[256,128]{1,0:T(8,128)(2,1)}, u32[]{:S(2)}) copy-start(bf16[256,128]{1,0:T(8,128)(2,1)} %constant.82.clone.refs_5_) | copy-start | bytes 196612
  11.0 5.9 %copy-start.5 = (bf16[256,128]{1,0:T(8,128)(2,1)S(1)}, bf16[256,128]{1,0:T(8,128)(2,1)}, u32[]{:S(2)}) copy-start(bf16[256,128]{1,0:T(8,128)(2,1)} %constant.81.clone.refs_4_) | copy-start | bytes 196612
  11.7 6.2 %collective-permute-start.2 = (f32[64,384]{1,0:T(8,128)S(1)}, f32[64,384]{1,0:T(8,128)S(1)}, u32[]{:S(2)}, u32[]{:S(2)}) collective-permute-start(f32[64,384]{1,0:T(8,128)S(1)} %get-tuple-element.77), channel_id=1, source_target_pairs={{8,16},{16,8},{9,17},{17,9},{10,18},{18,10},{11,19},{19,11},{12,20... | collective-permute-start | bytes 294920 | tf_op jit(solution)/shard_map/ppermute | solution.py:673
  12.4 7.2 %collective-permute-start.3 = (f32[64,384]{1,0:T(8,128)S(1)}, f32[64,384]{1,0:T(8,128)S(1)}, u32[]{:S(2)}, u32[]{:S(2)}) collective-permute-start(f32[64,384]{1,0:T(8,128)S(1)} %get-tuple-element.78), channel_id=1, source_target_pairs={{0,8},{16,24},{8,0},{24,16},{1,9},{17,25},{9,1},{25,17},{2,10},{18... | collective-permute-start | bytes 294920 | tf_op jit(solution)/shard_map/ppermute | solution.py:673
  22.4 19.2 %collective-permute-start.4 = (f32[1152,128]{1,0:T(8,128)S(1)}, f32[1152,128]{1,0:T(8,128)S(1)}, u32[]{:S(2)}, u32[]{:S(2)}) collective-permute-start(f32[1152,128]{1,0:T(8,128)S(1)} %get-tuple-element.82), channel_id=1, source_target_pairs={{1,2},{3,4},{5,6},{2,1},{4,3},{6,5},{9,10},{11,12},{13,14},{10,9},... | collective-permute-start | bytes 1769480 | tf_op jit(solution)/shard_map/ppermute | solution.py:673
  23.1 18.5 %collective-permute-start.5 = (f32[1152,128]{1,0:T(8,128)S(1)}, f32[1152,128]{1,0:T(8,128)S(1)}, u32[]{:S(2)}, u32[]{:S(2)}) collective-permute-start(f32[1152,128]{1,0:T(8,128)S(1)} %get-tuple-element.83), channel_id=1, source_target_pairs={{0,1},{2,3},{4,5},{6,7},{1,0},{3,2},{5,4},{7,6},{8,9},{10,11},{12,... | collective-permute-start | bytes 1769480 | tf_op jit(solution)/shard_map/ppermute | solution.py:673
  42.3 7.2 %collective-permute-start.7 = (f32[128,384]{1,0:T(8,128)S(1)}, f32[128,384]{1,0:T(8,128)S(1)}, u32[]{:S(2)}, u32[]{:S(2)}) collective-permute-start(f32[128,384]{1,0:T(8,128)S(1)} %get-tuple-element.93), channel_id=1, source_target_pairs={{8,16},{16,8},{9,17},{17,9},{10,18},{18,10},{11,19},{19,11},{12,20... | collective-permute-start | bytes 589832 | tf_op jit(solution)/shard_map/ppermute | solution.py:673
  42.9 9.2 %collective-permute-start.8 = (f32[128,384]{1,0:T(8,128)S(1)}, f32[128,384]{1,0:T(8,128)S(1)}, u32[]{:S(2)}, u32[]{:S(2)}) collective-permute-start(f32[128,384]{1,0:T(8,128)S(1)} %get-tuple-element.94), channel_id=1, source_target_pairs={{0,8},{16,24},{8,0},{24,16},{1,9},{17,25},{9,1},{25,17},{2,10},{18... | collective-permute-start | bytes 589832 | tf_op jit(solution)/shard_map/ppermute | solution.py:673
  48.8 6.3 %collective-permute-start.6 = (f32[384,128]{1,0:T(8,128)S(1)}, f32[384,128]{1,0:T(8,128)S(1)}, u32[]{:S(2)}, u32[]{:S(2)}) collective-permute-start(f32[384,128]{1,0:T(8,128)S(1)} %get-tuple-element.90), channel_id=1, source_target_pairs={{1,2},{3,4},{5,6},{2,1},{4,3},{6,5},{9,10},{11,12},{13,14},{10,9},... | collective-permute-start | bytes 589832 | tf_op jit(solution)/shard_map/ppermute | solution.py:673
  55.1 17.6 %collective-permute-start.10 = (f32[1152,128]{1,0:T(8,128)S(1)}, f32[1152,128]{1,0:T(8,128)S(1)}, u32[]{:S(2)}, u32[]{:S(2)}) collective-permute-start(f32[1152,128]{1,0:T(8,128)S(1)} %get-tuple-element.103), channel_id=1, source_target_pairs={{0,1},{2,3},{4,5},{6,7},{1,0},{3,2},{5,4},{7,6},{8,9},{10,11},{12,... | collective-permute-start | bytes 1769480 | tf_op jit(solution)/shard_map/ppermute | solution.py:673
  59.1 13.6 %collective-permute-start.9 = (f32[768,128]{1,0:T(8,128)S(1)}, f32[768,128]{1,0:T(8,128)S(1)}, u32[]{:S(2)}, u32[]{:S(2)}) collective-permute-start(f32[768,128]{1,0:T(8,128)S(1)} %get-tuple-element.101), channel_id=1, source_target_pairs={{1,2},{3,4},{5,6},{2,1},{4,3},{6,5},{9,10},{11,12},{13,14},{10,9},... | collective-permute-start | bytes 1179656 | tf_op jit(solution)/shard_map/ppermute | solution.py:673
  73.4 4.7 %collective-permute-start.11 = (f32[128,384]{1,0:T(8,128)S(1)}, f32[128,384]{1,0:T(8,128)S(1)}, u32[]{:S(2)}, u32[]{:S(2)}) collective-permute-start(f32[128,384]{1,0:T(8,128)S(1)} %get-tuple-element.113), channel_id=1, source_target_pairs={{8,16},{16,8},{9,17},{17,9},{10,18},{18,10},{11,19},{19,11},{12,20... | collective-permute-start | bytes 589832 | tf_op jit(solution)/shard_map/ppermute | solution.py:673
  74.2 6.9 %collective-permute-start.12 = (f32[128,384]{1,0:T(8,128)S(1)}, f32[128,384]{1,0:T(8,128)S(1)}, u32[]{:S(2)}, u32[]{:S(2)}) collective-permute-start(f32[128,384]{1,0:T(8,128)S(1)} %get-tuple-element.114), channel_id=1, source_target_pairs={{0,8},{16,24},{8,0},{24,16},{1,9},{17,25},{9,1},{25,17},{2,10},{18... | collective-permute-start | bytes 589832 | tf_op jit(solution)/shard_map/ppermute | solution.py:673
  84.2 15.0 %collective-permute-start.13 = (f32[576,128]{1,0:T(8,128)S(1)}, f32[576,128]{1,0:T(8,128)S(1)}, u32[]{:S(2)}, u32[]{:S(2)}) collective-permute-start(f32[576,128]{1,0:T(8,128)S(1)} %get-tuple-element.118), channel_id=1, source_target_pairs={{1,2},{3,4},{5,6},{2,1},{4,3},{6,5},{9,10},{11,12},{13,14},{10,9},... | collective-permute-start | bytes 884744 | tf_op jit(solution)/shard_map/ppermute | solution.py:673
  84.9 14.3 %collective-permute-start.14 = (f32[576,128]{1,0:T(8,128)S(1)}, f32[576,128]{1,0:T(8,128)S(1)}, u32[]{:S(2)}, u32[]{:S(2)}) collective-permute-start(f32[576,128]{1,0:T(8,128)S(1)} %get-tuple-element.119), channel_id=1, source_target_pairs={{0,1},{2,3},{4,5},{6,7},{1,0},{3,2},{5,4},{7,6},{8,9},{10,11},{12,... | collective-permute-start | bytes 884744 | tf_op jit(solution)/shard_map/ppermute | solution.py:673
  100.1 5.6 %collective-permute-start.15 = (f32[64,256]{1,0:T(8,128)S(1)}, f32[64,256]{1,0:T(8,128)S(1)}, u32[]{:S(2)}, u32[]{:S(2)}) collective-permute-start(f32[64,256]{1,0:T(8,128)S(1)} %get-tuple-element.127), channel_id=1, source_target_pairs={{8,16},{16,8},{9,17},{17,9},{10,18},{18,10},{11,19},{19,11},{12,20... | collective-permute-start | bytes 196616 | tf_op jit(solution)/shard_map/ppermute | solution.py:673
  100.7 4.9 %collective-permute-start.16 = (f32[64,256]{1,0:T(8,128)S(1)}, f32[64,256]{1,0:T(8,128)S(1)}, u32[]{:S(2)}, u32[]{:S(2)}) collective-permute-start(f32[64,256]{1,0:T(8,128)S(1)} %get-tuple-element.128), channel_id=1, source_target_pairs={{0,8},{16,24},{8,0},{24,16},{1,9},{17,25},{9,1},{25,17},{2,10},{18... | collective-permute-start | bytes 196616 | tf_op jit(solution)/shard_map/ppermute | solution.py:673

commit v6 on v5

--- a/solution.py
+++ b/solution.py
@@ -535,6 +535,10 @@
         r.low_sum_new[...] = jnp.zeros((WIN, WIN), F32)
         r.curve[...] = jnp.zeros((8, THIRD), F32)
 
+    gamma = total(square)
+    curve = gamma + total(r.acc[2] + r.curve[...])
+    r.part[...] = lanes_of(r.part.shape, gamma, curve, total(cross))
+
     low = lane_mask()
     new = Refs(tiles=r.tiles, top_sum=r.top_sum_new, mid_sum=r.mid_sum_new, low_sum=r.low_sum_new)
     if r.narrow:
@@ -563,9 +567,6 @@
                 r.to_b[rows_at(num), :] = to_b
             elif num < 3 or num >= 3 + middle:
                 r.to_end[rows_at(num if num < 3 else num - middle), :] = to_b
-    gamma = total(square)
-    curve = gamma + total(r.acc[2] + r.curve[...])
-    r.part[...] = lanes_of(r.part.shape, gamma, curve, total(cross))
 
 
 def last_rows(r, start, corrected, residual, at):

time: 108 us -> 108 us (level)
  Pallas kernels: 21.5 us -> 14.7 us
  blocking collectives: 38.3 us -> 42.4 us
  starting transfers between devices: 35.7 us -> 38.8 us
    pallas_call x14, Pallas kernels: 21.5 us -> 14.7 us  [run(): pl.pallas_call(kernel, name=body.__name__, out_shape=[jax.ShapeDtypeStruc...]
    all_to_all x3, blocking collectives: 38.3 us -> 42.4 us  [shards(): parts = lax.all_to_all(part, ('row', 'col'), 0, 0, tiled=True)]
    ppermute x17, starting transfers between devices: 35.7 us -> 38.8 us  [swap(): return lax.ppermute(value, axis, pairs + [(b, a) for a, b in pairs])]
  transfers between devices with their start and end apart: 17 -> 17, of which waited for: 3 -> 3; matrix products, arithmetic and copies ran while one was open for 2% -> 2% of each run, Pallas kernels for 10% -> 7%
where the time goes in v6:
time: 108 us
  blocking collectives  42.4 us (39%)
  starting transfers between devices  38.8 us (36%)
  Pallas kernels  14.7 us (14%)
  waiting for transfers between devices  7.35 us (7%)
  local copies, waits for them, and re-layouts  3.59 us (3%)
  between operations  1.09 us (1%)
    all_to_all x3, blocking collectives, shards(): parts = lax.all_to_all(part, ('row', 'col'), 0, 0, tiled=True)  42.4 us
    ppermute x17, starting transfers between devices, swap(): return lax.ppermute(value, axis, pairs + [(b, a) for a, b in pairs])  38.8 us
    pallas_call x14, Pallas kernels, run(): pl.pallas_call(kernel, name=body.__name__, out_shape=[jax.ShapeDtypeStruc...  14.7 us
    ppermute x17, waiting for transfers between devices, swap(): return lax.ppermute(value, axis, pairs + [(b, a) for a, b in pairs])  7.35 us
    unnamed x17, local copies, waits for them, and re-layouts  2.66 us
  transfers between devices with their start and end apart: 17, of which 3 were waited for; matrix products, arithmetic and copies ran while one was open for 2% of the time, Pallas kernels for 7%

profile of v6, /device:TPU:0, one launch (start us, length us, event | category | flops | bytes accessed | tf_op | source)
XLA Modules:
  0.0 108.0 jit_solution(4526333784127048170)
XLA Ops:
  0.7 0.1 stack.27
  0.8 1.2 %copy-done = f32[1024,256]{1,0:T(8,128)S(1)} copy-done((f32[1024,256]{1,0:T(8,128)S(1)}, f32[1024,256]{1,0:T(8,128)}, u32[]{:S(2)}) %copy-start) | copy-done | bytes 1048600
  2.0 0.7 pack_kernel.1
  2.7 0.7 collective-permute-start
  3.4 4.3 %collective-permute-start.1 = (f32[512,128]{1,0:T(8,128)S(1)}, f32[512,128]{1,0:T(8,128)S(1)}, u32[]{:S(2)}, u32[]{:S(2)}) collective-permute-start(f32[512,128]{1,0:T(8,128)S(1)} %get-tuple-element.68), channel_id=1, source_target_pairs={{0,1},{2,3},{4,5},{6,7},{1,0},{3,2},{5,4},{7,6},{8,9},{10,11},{12,... | collective-permute-start | bytes 786440 | tf_op jit(solution)/shard_map/ppermute | solution.py:674
  7.8 1.0 copy.15
  8.8 0.8 dynamic-slice_bitcast_fusion
  9.6 0.0 copy-done.6
  9.6 0.0 copy-done.7
  9.6 0.8 spectra_kernel.1.refs_1_
  10.4 0.0 copy-start.2
  10.4 0.0 copy-start.3
  10.4 0.0 copy-start.4
  10.4 0.0 copy-start.5
  10.5 0.0 collective-permute-done.refs_2_.refs_7_
  10.5 0.0 collective-permute-done.1.refs_3_.refs_8_
  10.5 0.4 copy-done.1
  10.9 0.6 halo_kernel.1
  11.5 0.7 collective-permute-start.2
  12.2 5.2 %collective-permute-start.3 = (f32[64,384]{1,0:T(8,128)S(1)}, f32[64,384]{1,0:T(8,128)S(1)}, u32[]{:S(2)}, u32[]{:S(2)}) collective-permute-start(f32[64,384]{1,0:T(8,128)S(1)} %get-tuple-element.78), channel_id=1, source_target_pairs={{0,8},{16,24},{8,0},{24,16},{1,9},{17,25},{9,1},{25,17},{2,10},{18... | collective-permute-start | bytes 294920 | tf_op jit(solution)/shard_map/ppermute | solution.py:674
  17.4 0.0 copy-done.2
  17.4 0.0 copy-done.5
  17.4 0.9 middle_kernel.3
  18.3 0.0 collective-permute-done.2.refs_10_
  18.3 1.7 %collective-permute-done.3.refs_11_ = f32[64,384]{1,0:T(8,128)S(1)} collective-permute-done((f32[64,384]{1,0:T(8,128)S(1)}, f32[64,384]{1,0:T(8,128)S(1)}, u32[]{:S(2)}, u32[]{:S(2)}) %collective-permute-start.3) | collective-permute-done | bytes 98336 | tf_op jit(solution)/shard_map/ppermute | solution.py:674
  20.0 0.8 edge_kernel.3
  20.8 0.7 collective-permute-start.4
  21.5 3.4 %collective-permute-start.5 = (f32[1152,128]{1,0:T(8,128)S(1)}, f32[1152,128]{1,0:T(8,128)S(1)}, u32[]{:S(2)}, u32[]{:S(2)}) collective-permute-start(f32[1152,128]{1,0:T(8,128)S(1)} %get-tuple-element.83), channel_id=1, source_target_pairs={{0,1},{2,3},{4,5},{6,7},{1,0},{3,2},{5,4},{7,6},{8,9},{10,11},{12,... | collective-permute-start | bytes 1769480 | tf_op jit(solution)/shard_map/ppermute | solution.py:674
  25.0 14.8 %all_to_all.36 = f32[32,1,128]{2,1,0:T(1,128)S(1)} all-to-all(f32[32,1,128]{2,1,0:T(1,128)S(1)} %bitcast.27), channel_id=1, replica_groups=mesh['row'=4,'col'=8] {'row','col'}, dimensions={0} | all-to-all | bytes 32768 | tf_op jit(solution)/shard_map/all_to_all | solution.py:778
  39.8 0.0 collective-permute-done.4.refs_6_.refs_2_
  39.8 0.0 collective-permute-done.5.refs_7_.refs_3_
  39.8 0.6 row_strip_kernel.3
  40.4 0.7 collective-permute-start.7
  41.1 6.1 %collective-permute-start.8 = (f32[128,384]{1,0:T(8,128)S(1)}, f32[128,384]{1,0:T(8,128)S(1)}, u32[]{:S(2)}, u32[]{:S(2)}) collective-permute-start(f32[128,384]{1,0:T(8,128)S(1)} %get-tuple-element.94), channel_id=1, source_target_pairs={{0,8},{16,24},{8,0},{24,16},{1,9},{17,25},{9,1},{25,17},{2,10},{18... | collective-permute-start | bytes 589832 | tf_op jit(solution)/shard_map/ppermute | solution.py:674
  47.2 1.3 %middle_kernel.4 = (f32[896,384]{1,0:T(8,128)S(1)}, f32[640,384]{1,0:T(8,128)S(1)}, f32[3,8,128]{2,1,0:T(8,128)S(1)}, f32[9,8,128]{2,1,0:T(8,128)S(1)}, f32[384,128]{1,0:T(8,128)S(1)}) custom-call(s32[4]{0:T(128)S(1)} %get-tuple-element.133.refs_1_.refs_0_, f32[4,2,256,256]{3,2,1,0:T(8,128)S(1)} %spectra_kernel.1.refs_1_, bf16[512,256]{1,0:T(8,128)(2,1)S(1)} %copy-done.3, ...), custom_call_target="tpu_custom_call" | custom-call | tf_op jit(solution)/shard_map/middle_kernel/pallas_call | solution.py:649
  48.5 0.7 collective-permute-start.6
  49.2 0.0 collective-permute-done.7.refs_13_
  49.2 2.6 %collective-permute-done.8.refs_14_ = f32[128,384]{1,0:T(8,128)S(1)} collective-permute-done((f32[128,384]{1,0:T(8,128)S(1)}, f32[128,384]{1,0:T(8,128)S(1)}, u32[]{:S(2)}, u32[]{:S(2)}) %collective-permute-start.8) | collective-permute-done | bytes 196640 | tf_op jit(solution)/shard_map/ppermute | solution.py:674
  51.9 0.9 edge_kernel.4
  52.8 0.0 collective-permute-done.6.refs_7_.refs_3_
  52.8 5.6 %collective-permute-start.10 = (f32[1152,128]{1,0:T(8,128)S(1)}, f32[1152,128]{1,0:T(8,128)S(1)}, u32[]{:S(2)}, u32[]{:S(2)}) collective-permute-start(f32[1152,128]{1,0:T(8,128)S(1)} %get-tuple-element.103), channel_id=1, source_target_pairs={{0,1},{2,3},{4,5},{6,7},{1,0},{3,2},{5,4},{7,6},{8,9},{10,11},{12,... | collective-permute-start | bytes 1769480 | tf_op jit(solution)/shard_map/ppermute | solution.py:674
  58.5 0.7 collective-permute-start.9
  59.1 13.9 %all_to_all.37 = f32[32,1,128]{2,1,0:T(1,128)S(1)} all-to-all(f32[32,1,128]{2,1,0:T(1,128)S(1)} %bitcast.26), channel_id=1, replica_groups=mesh['row'=4,'col'=8] {'row','col'}, dimensions={0} | all-to-all | bytes 32768 | tf_op jit(solution)/shard_map/all_to_all | solution.py:778
  73.0 0.0 collective-permute-done.9.refs_6_.refs_2_
  73.0 0.0 collective-permute-done.10.refs_8_.refs_4_
  73.0 0.6 row_strip_kernel.4
  73.7 0.9 collective-permute-start.11
  74.5 3.4 %collective-permute-start.12 = (f32[128,384]{1,0:T(8,128)S(1)}, f32[128,384]{1,0:T(8,128)S(1)}, u32[]{:S(2)}, u32[]{:S(2)}) collective-permute-start(f32[128,384]{1,0:T(8,128)S(1)} %get-tuple-element.114), channel_id=1, source_target_pairs={{0,8},{16,24},{8,0},{24,16},{1,9},{17,25},{9,1},{25,17},{2,10},{18... | collective-permute-start | bytes 589832 | tf_op jit(solution)/shard_map/ppermute | solution.py:674
  78.0 1.7 %middle_kernel.5 = (f32[896,384]{1,0:T(8,128)S(1)}, f32[640,384]{1,0:T(8,128)S(1)}, f32[3,8,128]{2,1,0:T(8,128)S(1)}, f32[9,8,128]{2,1,0:T(8,128)S(1)}) custom-call(s32[4]{0:T(128)S(1)} %get-tuple-element.133.refs_1_.refs_0_, f32[4,2,256,256]{3,2,1,0:T(8,128)S(1)} %spectra_kernel.1.refs_1_, bf16[512,256]{1,0:T(8,128)(2,1)S(1)} %copy-done.3, ...), custom_call_target="tpu_custom_call" | custom-call | tf_op jit(solution)/shard_map/middle_kernel/pallas_call | solution.py:649
  79.7 0.0 collective-permute-done.11.refs_15_
  79.7 3.0 %collective-permute-done.12.refs_16_ = f32[128,384]{1,0:T(8,128)S(1)} collective-permute-done((f32[128,384]{1,0:T(8,128)S(1)}, f32[128,384]{1,0:T(8,128)S(1)}, u32[]{:S(2)}, u32[]{:S(2)}) %collective-permute-start.12) | collective-permute-done | bytes 196640 | tf_op jit(solution)/shard_map/ppermute | solution.py:674
  82.7 1.1 edge_kernel.5
  83.7 0.7 collective-permute-start.13
  84.4 1.8 %collective-permute-start.14 = (f32[576,128]{1,0:T(8,128)S(1)}, f32[576,128]{1,0:T(8,128)S(1)}, u32[]{:S(2)}, u32[]{:S(2)}) collective-permute-start(f32[576,128]{1,0:T(8,128)S(1)} %get-tuple-element.119), channel_id=1, source_target_pairs={{0,1},{2,3},{4,5},{6,7},{1,0},{3,2},{5,4},{7,6},{8,9},{10,11},{12,... | collective-permute-start | bytes 884744 | tf_op jit(solution)/shard_map/ppermute | solution.py:674
  86.2 13.7 %all_to_all.38 = f32[32,1,128]{2,1,0:T(1,128)S(1)} all-to-all(f32[32,1,128]{2,1,0:T(1,128)S(1)} %bitcast.25), channel_id=1, replica_groups=mesh['row'=4,'col'=8] {'row','col'}, dimensions={0} | all-to-all | bytes 32768 | tf_op jit(solution)/shard_map/all_to_all | solution.py:778
  100.0 0.0 collective-permute-done.13.refs_4_.refs_5_
  100.0 0.0 collective-permute-done.14.refs_5_.refs_6_
  100.0 0.9 row_strip_kernel.5
  100.9 0.7 collective-permute-start.15
  101.5 2.5 %collective-permute-start.16 = (f32[64,256]{1,0:T(8,128)S(1)}, f32[64,256]{1,0:T(8,128)S(1)}, u32[]{:S(2)}, u32[]{:S(2)}) collective-permute-start(f32[64,256]{1,0:T(8,128)S(1)} %get-tuple-element.128), channel_id=1, source_target_pairs={{0,8},{16,24},{8,0},{24,16},{1,9},{17,25},{9,1},{25,17},{2,10},{18... | collective-permute-start | bytes 196616 | tf_op jit(solution)/shard_map/ppermute | solution.py:674
  104.0 2.4 %last_middle_kernel.1 = (f32[1024,256]{1,0:T(8,128)}, f32[1024,256]{1,0:T(8,128)}) custom-call(f32[9,8,128]{2,1,0:T(8,128)S(1)} %get-tuple-element.126.refs_0_, f32[640,384]{1,0:T(8,128)S(1)} %get-tuple-element.116.refs_18_.refs_1_, f32[384,384]{1,0:T(8,128)S(1)} %get-tuple-element.122.refs_2_.refs_3_, f32[384,384]{1,0:T(8,128)S(1)} %get-tuple-element.123.refs_3_.refs_4_, ...), custom_call_target="tpu_custom_call" | custom-call | tf_op jit(solution)/shard_map/last_middle_kernel/pallas_call | solution.py:649
  106.4 0.0 collective-permute-done.15.refs_1_
  106.4 0.0 collective-permute-done.16.refs_2_
  106.5 1.4 %last_edge_kernel.1 = (f32[1024,256]{1,0:T(8,128)}, f32[1024,256]{1,0:T(8,128)}) custom-call(f32[9,8,128]{2,1,0:T(8,128)S(1)} %get-tuple-element.126.refs_0_, f32[64,256]{1,0:T(8,128)S(1)} %collective-permute-done.15.refs_1_, f32[64,256]{1,0:T(8,128)S(1)} %collective-permute-done.16.refs_2_, ...), custom_call_target="tpu_custom_call", output_to_operand_aliasing={{0}: (11, {}), {1}: (12, {})} | custom-call | tf_op jit(solution)/shard_map/last_edge_kernel/pallas_call | solution.py:649
  (8 shorter events, 0.1 us)
Async XLA Ops:
  0.8 1.2 %copy-start = (f32[1024,256]{1,0:T(8,128)S(1)}, f32[1024,256]{1,0:T(8,128)}, u32[]{:S(2)}) copy-start(f32[1024,256]{1,0:T(8,128)} %refs_9_.3) | copy-start | bytes 3145732
  2.0 7.6 %copy-start.6 = (bf16[384,512]{1,0:T(8,128)(2,1)S(1)}, bf16[384,512]{1,0:T(8,128)(2,1)}, u32[]{:S(2)}) copy-start(bf16[384,512]{1,0:T(8,128)(2,1)} %constant.84.clone.refs_4_) | copy-start | bytes 1179652
  2.0 7.6 %copy-start.7 = (bf16[512,384]{1,0:T(8,128)(2,1)S(1)}, bf16[512,384]{1,0:T(8,128)(2,1)}, u32[]{:S(2)}) copy-start(bf16[512,384]{1,0:T(8,128)(2,1)} %constant.83.clone.refs_3_) | copy-start | bytes 1179652
  2.7 7.7 %collective-permute-start = (f32[512,128]{1,0:T(8,128)S(1)}, f32[512,128]{1,0:T(8,128)S(1)}, u32[]{:S(2)}, u32[]{:S(2)}) collective-permute-start(f32[512,128]{1,0:T(8,128)S(1)} %get-tuple-element.67), channel_id=1, source_target_pairs={{1,2},{3,4},{5,6},{2,1},{4,3},{6,5},{9,10},{11,12},{13,14},{10,9},... | collective-permute-start | bytes 786440 | tf_op jit(solution)/shard_map/ppermute | solution.py:674
  3.4 7.0 %collective-permute-start.1 = (f32[512,128]{1,0:T(8,128)S(1)}, f32[512,128]{1,0:T(8,128)S(1)}, u32[]{:S(2)}, u32[]{:S(2)}) collective-permute-start(f32[512,128]{1,0:T(8,128)S(1)} %get-tuple-element.68), channel_id=1, source_target_pairs={{0,1},{2,3},{4,5},{6,7},{1,0},{3,2},{5,4},{7,6},{8,9},{10,11},{12,... | collective-permute-start | bytes 786440 | tf_op jit(solution)/shard_map/ppermute | solution.py:674
  9.6 1.2 %copy-start.1 = (f32[1024,256]{1,0:T(8,128)S(1)}, f32[1024,256]{1,0:T(8,128)}, u32[]{:S(2)}) copy-start(f32[1024,256]{1,0:T(8,128)} %refs_9_.3) | copy-start | bytes 3145732
  10.4 7.0 %copy-start.2 = (bf16[512,256]{1,0:T(8,128)(2,1)S(1)}, bf16[512,256]{1,0:T(8,128)(2,1)}, u32[]{:S(2)}) copy-start(bf16[512,256]{1,0:T(8,128)(2,1)} %constant.80.clone.refs_3_) | copy-start | bytes 786436
  10.4 7.0 %copy-start.3 = (bf16[512,256]{1,0:T(8,128)(2,1)S(1)}, bf16[512,256]{1,0:T(8,128)(2,1)}, u32[]{:S(2)}) copy-start(bf16[512,256]{1,0:T(8,128)(2,1)} %constant.79.clone.refs_2_) | copy-start | bytes 786436
  10.4 7.0 %copy-start.4 = (bf16[256,128]{1,0:T(8,128)(2,1)S(1)}, bf16[256,128]{1,0:T(8,128)(2,1)}, u32[]{:S(2)}) copy-start(bf16[256,128]{1,0:T(8,128)(2,1)} %constant.82.clone.refs_5_) | copy-start | bytes 196612
  10.4 7.0 %copy-start.5 = (bf16[256,128]{1,0:T(8,128)(2,1)S(1)}, bf16[256,128]{1,0:T(8,128)(2,1)}, u32[]{:S(2)}) copy-start(bf16[256,128]{1,0:T(8,128)(2,1)} %constant.81.clone.refs_4_) | copy-start | bytes 196612
  11.5 6.8 %collective-permute-start.2 = (f32[64,384]{1,0:T(8,128)S(1)}, f32[64,384]{1,0:T(8,128)S(1)}, u32[]{:S(2)}, u32[]{:S(2)}) collective-permute-start(f32[64,384]{1,0:T(8,128)S(1)} %get-tuple-element.77), channel_id=1, source_target_pairs={{8,16},{16,8},{9,17},{17,9},{10,18},{18,10},{11,19},{19,11},{12,20... | collective-permute-start | bytes 294920 | tf_op jit(solution)/shard_map/ppermute | solution.py:674
  12.2 7.8 %collective-permute-start.3 = (f32[64,384]{1,0:T(8,128)S(1)}, f32[64,384]{1,0:T(8,128)S(1)}, u32[]{:S(2)}, u32[]{:S(2)}) collective-permute-start(f32[64,384]{1,0:T(8,128)S(1)} %get-tuple-element.78), channel_id=1, source_target_pairs={{0,8},{16,24},{8,0},{24,16},{1,9},{17,25},{9,1},{25,17},{2,10},{18... | collective-permute-start | bytes 294920 | tf_op jit(solution)/shard_map/ppermute | solution.py:674
  20.8 19.0 %collective-permute-start.4 = (f32[1152,128]{1,0:T(8,128)S(1)}, f32[1152,128]{1,0:T(8,128)S(1)}, u32[]{:S(2)}, u32[]{:S(2)}) collective-permute-start(f32[1152,128]{1,0:T(8,128)S(1)} %get-tuple-element.82), channel_id=1, source_target_pairs={{1,2},{3,4},{5,6},{2,1},{4,3},{6,5},{9,10},{11,12},{13,14},{10,9},... | collective-permute-start | bytes 1769480 | tf_op jit(solution)/shard_map/ppermute | solution.py:674
  21.5 18.3 %collective-permute-start.5 = (f32[1152,128]{1,0:T(8,128)S(1)}, f32[1152,128]{1,0:T(8,128)S(1)}, u32[]{:S(2)}, u32[]{:S(2)}) collective-permute-start(f32[1152,128]{1,0:T(8,128)S(1)} %get-tuple-element.83), channel_id=1, source_target_pairs={{0,1},{2,3},{4,5},{6,7},{1,0},{3,2},{5,4},{7,6},{8,9},{10,11},{12,... | collective-permute-start | bytes 1769480 | tf_op jit(solution)/shard_map/ppermute | solution.py:674
  40.4 8.8 %collective-permute-start.7 = (f32[128,384]{1,0:T(8,128)S(1)}, f32[128,384]{1,0:T(8,128)S(1)}, u32[]{:S(2)}, u32[]{:S(2)}) collective-permute-start(f32[128,384]{1,0:T(8,128)S(1)} %get-tuple-element.93), channel_id=1, source_target_pairs={{8,16},{16,8},{9,17},{17,9},{10,18},{18,10},{11,19},{19,11},{12,20... | collective-permute-start | bytes 589832 | tf_op jit(solution)/shard_map/ppermute | solution.py:674
  41.1 10.8 %collective-permute-start.8 = (f32[128,384]{1,0:T(8,128)S(1)}, f32[128,384]{1,0:T(8,128)S(1)}, u32[]{:S(2)}, u32[]{:S(2)}) collective-permute-start(f32[128,384]{1,0:T(8,128)S(1)} %get-tuple-element.94), channel_id=1, source_target_pairs={{0,8},{16,24},{8,0},{24,16},{1,9},{17,25},{9,1},{25,17},{2,10},{18... | collective-permute-start | bytes 589832 | tf_op jit(solution)/shard_map/ppermute | solution.py:674
  48.5 4.2 %collective-permute-start.6 = (f32[384,128]{1,0:T(8,128)S(1)}, f32[384,128]{1,0:T(8,128)S(1)}, u32[]{:S(2)}, u32[]{:S(2)}) collective-permute-start(f32[384,128]{1,0:T(8,128)S(1)} %get-tuple-element.90), channel_id=1, source_target_pairs={{1,2},{3,4},{5,6},{2,1},{4,3},{6,5},{9,10},{11,12},{13,14},{10,9},... | collective-permute-start | bytes 589832 | tf_op jit(solution)/shard_map/ppermute | solution.py:674
  52.8 20.2 %collective-permute-start.10 = (f32[1152,128]{1,0:T(8,128)S(1)}, f32[1152,128]{1,0:T(8,128)S(1)}, u32[]{:S(2)}, u32[]{:S(2)}) collective-permute-start(f32[1152,128]{1,0:T(8,128)S(1)} %get-tuple-element.103), channel_id=1, source_target_pairs={{0,1},{2,3},{4,5},{6,7},{1,0},{3,2},{5,4},{7,6},{8,9},{10,11},{12,... | collective-permute-start | bytes 1769480 | tf_op jit(solution)/shard_map/ppermute | solution.py:674
  58.5 14.6 %collective-permute-start.9 = (f32[768,128]{1,0:T(8,128)S(1)}, f32[768,128]{1,0:T(8,128)S(1)}, u32[]{:S(2)}, u32[]{:S(2)}) collective-permute-start(f32[768,128]{1,0:T(8,128)S(1)} %get-tuple-element.101), channel_id=1, source_target_pairs={{1,2},{3,4},{5,6},{2,1},{4,3},{6,5},{9,10},{11,12},{13,14},{10,9},... | collective-permute-start | bytes 1179656 | tf_op jit(solution)/shard_map/ppermute | solution.py:674
  73.7 6.0 %collective-permute-start.11 = (f32[128,384]{1,0:T(8,128)S(1)}, f32[128,384]{1,0:T(8,128)S(1)}, u32[]{:S(2)}, u32[]{:S(2)}) collective-permute-start(f32[128,384]{1,0:T(8,128)S(1)} %get-tuple-element.113), channel_id=1, source_target_pairs={{8,16},{16,8},{9,17},{17,9},{10,18},{18,10},{11,19},{19,11},{12,20... | collective-permute-start | bytes 589832 | tf_op jit(solution)/shard_map/ppermute | solution.py:674
  74.5 8.1 %collective-permute-start.12 = (f32[128,384]{1,0:T(8,128)S(1)}, f32[128,384]{1,0:T(8,128)S(1)}, u32[]{:S(2)}, u32[]{:S(2)}) collective-permute-start(f32[128,384]{1,0:T(8,128)S(1)} %get-tuple-element.114), channel_id=1, source_target_pairs={{0,8},{16,24},{8,0},{24,16},{1,9},{17,25},{9,1},{25,17},{2,10},{18... | collective-permute-start | bytes 589832 | tf_op jit(solution)/shard_map/ppermute | solution.py:674
  83.7 16.3 %collective-permute-start.13 = (f32[576,128]{1,0:T(8,128)S(1)}, f32[576,128]{1,0:T(8,128)S(1)}, u32[]{:S(2)}, u32[]{:S(2)}) collective-permute-start(f32[576,128]{1,0:T(8,128)S(1)} %get-tuple-element.118), channel_id=1, source_target_pairs={{1,2},{3,4},{5,6},{2,1},{4,3},{6,5},{9,10},{11,12},{13,14},{10,9},... | collective-permute-start | bytes 884744 | tf_op jit(solution)/shard_map/ppermute | solution.py:674
  84.4 15.6 %collective-permute-start.14 = (f32[576,128]{1,0:T(8,128)S(1)}, f32[576,128]{1,0:T(8,128)S(1)}, u32[]{:S(2)}, u32[]{:S(2)}) collective-permute-start(f32[576,128]{1,0:T(8,128)S(1)} %get-tuple-element.119), channel_id=1, source_target_pairs={{0,1},{2,3},{4,5},{6,7},{1,0},{3,2},{5,4},{7,6},{8,9},{10,11},{12,... | collective-permute-start | bytes 884744 | tf_op jit(solution)/shard_map/ppermute | solution.py:674
  100.9 5.6 %collective-permute-start.15 = (f32[64,256]{1,0:T(8,128)S(1)}, f32[64,256]{1,0:T(8,128)S(1)}, u32[]{:S(2)}, u32[]{:S(2)}) collective-permute-start(f32[64,256]{1,0:T(8,128)S(1)} %get-tuple-element.127), channel_id=1, source_target_pairs={{8,16},{16,8},{9,17},{17,9},{10,18},{18,10},{11,19},{19,11},{12,20... | collective-permute-start | bytes 196616 | tf_op jit(solution)/shard_map/ppermute | solution.py:674
  101.5 4.9 %collective-permute-start.16 = (f32[64,256]{1,0:T(8,128)S(1)}, f32[64,256]{1,0:T(8,128)S(1)}, u32[]{:S(2)}, u32[]{:S(2)}) collective-permute-start(f32[64,256]{1,0:T(8,128)S(1)} %get-tuple-element.128), channel_id=1, source_target_pairs={{0,8},{16,24},{8,0},{24,16},{1,9},{17,25},{9,1},{25,17},{2,10},{18... | collective-permute-start | bytes 196616 | tf_op jit(solution)/shard_map/ppermute | solution.py:674

commit v7 on v5

--- a/solution.py
+++ b/solution.py
@@ -305,17 +305,19 @@
 
 
 def from_columns(r, start, size):
-    second = getattr(r, "side_b", None)
-    there = start
-    if second is None:
-        middle = r.side_mid.shape[0]
-        if start < WIN:
-            second = r.side_end
-        elif start < WIN + middle:
-            second, there = r.side_mid, start - WIN
-        else:
-            second, there = r.side_end, start - middle
-    return pick(r.edge[4] != 0, r.side_z[pl.ds(start, size), :], second[pl.ds(there, size), :])
+    def part(whole, middle, ends):
+        if whole is not None:
+            return whole[pl.ds(start, size), :]
+        count = middle.shape[0]
+        if WIN <= start < WIN + count:
+            return middle[pl.ds(start - WIN, size), :]
+        return ends[pl.ds(start if start < WIN else start - count, size), :]
+
+    names = r.__dict__
+    return pick(
+        r.edge[4] != 0,
+        *(part(*(names.get(kind + pair) for kind in ("side", "middle", "ends"))) for pair in "zb"),
+    )
 
 
 def from_rows(r, side, here):
@@ -371,7 +373,7 @@
 
 
 def unpacked_sides(r, start, size):
-    half = r.side_z.shape[0]
+    half = r.sidez.shape[0]
     low = lane_mask()
     out = []
     while size:
@@ -480,9 +482,9 @@
         r.mid_sum_new[...] = jnp.zeros(r.mid_sum_new.shape, F32)
 
     if r.parted:
-        for num in range(r.to_mid.shape[0] // THIRD):
+        for num in range(r.mid_a.shape[0] // THIRD):
             strips = strips_of([(r.mid_sum_new, num + 1)])
-            r.to_mid[rows_at(num), :] = pick(r.edge[4] != 0, *strips)[1]
+            r.mid_a[rows_at(num), :], r.mid_b[rows_at(num), :] = pick(r.edge[4] != 0, *strips)
 
 
 def edge_kernel(r):
@@ -557,12 +559,11 @@
     else:
         middle = blocks - 6
         for num in range(blocks):
-            to_a, to_b = pick(r.edge[4] != 0, *strips_of(own_sum(new, num)))
-            r.to_a[rows_at(num), :] = to_a
+            strips = strips_of(own_sum(new, num))
             if not r.parted:
-                r.to_b[rows_at(num), :] = to_b
+                send_columns(r, rows_at(num), *strips)
             elif num < 3 or num >= 3 + middle:
-                r.to_end[rows_at(num if num < 3 else num - middle), :] = to_b
+                send_columns(r, rows_at(num if num < 3 else num - middle), *strips)
     gamma = total(square)
     curve = gamma + total(r.acc[2] + r.curve[...])
     r.part[...] = lanes_of(r.part.shape, gamma, curve, total(cross))
@@ -686,8 +687,8 @@
     ).astype(jnp.int32)
     host = {name: jnp.asarray(table) for name, table in tables().items()}
     sent = run(pack_kernel, dict(edge=edge, observed=observed), dict(to_a=(half, THIRD), to_b=(half, THIRD)))
-    side_b = swap(sent["to_b"], "col", 1)
-    side_z = swap(sent["to_a"], "col", 0)
+    sideb = swap(sent["to_b"], "col", 1)
+    sidez = swap(sent["to_a"], "col", 0)
     spec = run(
         spectra_kernel,
         dict(
@@ -699,8 +700,8 @@
         ),
         dict(spec=(tiles, 2, SLOTS, SLOTS)),
     )["spec"]
-    side_b, side_z, spec = lax.optimization_barrier((side_b, side_z, spec))
-    sides = dict(edge=edge, side_b=side_b, side_z=side_z)
+    sideb, sidez, spec = lax.optimization_barrier((sideb, sidez, spec))
+    sides = dict(edge=edge, sideb=sideb, sidez=sidez)
     sent = run(halo_kernel, dict(observed=observed, **sides), dict(to_a=(HALO, WIN), to_b=(HALO, WIN)))
     sides, sent = lax.optimization_barrier((sides, sent))
     row_b, row_a = swap(sent["to_b"], "row", 1), swap(sent["to_a"], "row", 0)
@@ -728,17 +729,16 @@
                 "mid_sum_new": (mid - TILE, WIN),
                 "acc": (3, 8, THIRD),
                 **(dict(coef_new=COEFS) if stage else {}),
-                **({"to_mid": (ext - 2 * WIN, THIRD)} if parted else {}),
+                **({name: (ext - 2 * WIN, THIRD) for name in ("mid_a", "mid_b") if parted}),
             },
             stage=stage,
             tiles=tiles,
             parted=parted,
         )
         if parted:
-            side_mid = swap(middle["to_mid"], "col", 1)
+            middleb, middlez = swap(middle["mid_b"], "col", 1), swap(middle["mid_a"], "col", 0)
         outs = {"res_edge_new": (TILE, WIN), "top_sum_new": (WIN, WIN), "low_sum_new": (WIN, WIN)}
-        outs["to_a"] = (ext // 2 if narrow else ext, THIRD)
-        outs["to_end" if parted else "to_b"] = (2 * WIN if parted else outs["to_a"][0], THIRD)
+        outs["to_a"] = outs["to_b"] = (ext // 2 if narrow else 2 * WIN if parted else ext, THIRD)
         outs["part"] = (devices, THIRD)
         edges = run(
             edge_kernel,
@@ -763,17 +763,13 @@
         state["mid_sum"] = middle["mid_sum_new"]
         state["top_sum"] = edges["top_sum_new"]
         state["low_sum"] = edges["low_sum_new"]
-        part, to_a = edges["part"], edges["to_a"]
-        sides = {}
+        part, to_a, to_b = edges["part"], edges["to_a"], edges["to_b"]
         if parted:
-            sides["side_mid"], part, to_a, to_end = lax.optimization_barrier(
-                (side_mid, part, to_a, edges["to_end"])
-            )
-        sides["side_z"] = swap(to_a, "col", 0)
+            middleb, middlez, to_b, to_a, part = lax.optimization_barrier((middleb, middlez, to_b, to_a, part))
+        keys = ("endsb", "endsz") if parted else ("sideb", "sidez")
+        sides = dict(zip(keys, (swap(to_b, "col", 1), swap(to_a, "col", 0))))
         if parted:
-            sides["side_end"] = swap(to_end, "col", 1)
-        else:
-            sides["side_b"] = swap(edges["to_b"], "col", 1)
+            sides.update(middleb=middleb, middlez=middlez)
         parts = lax.all_to_all(part, ("row", "col"), 0, 0, tiled=True)
         sides, parts = lax.optimization_barrier((sides, parts))
         sides["edge"] = edge

time: 108 us -> 108 us (level)
  starting transfers between devices: 35.7 us -> 47.1 us
  Pallas kernels: 21.5 us -> 14.7 us
  waiting for transfers between devices: 7.41 us -> 4.71 us
  blocking collectives: 38.3 us -> 36.5 us
    ppermute x17 -> x18, starting transfers between devices: 35.7 us -> 47.1 us  [swap(): return lax.ppermute(value, axis, pairs + [(b, a) for a, b in pairs])]
    pallas_call x14, Pallas kernels: 21.5 us -> 14.7 us  [run(): pl.pallas_call(kernel, name=body.__name__, out_shape=[jax.ShapeDtypeStruc...]
    ppermute x17 -> x18, waiting for transfers between devices: 7.41 us -> 4.71 us  [swap(): return lax.ppermute(value, axis, pairs + [(b, a) for a, b in pairs])]
    all_to_all x3, blocking collectives: 38.3 us -> 36.5 us  [shards(): parts = lax.all_to_all(part, ('row', 'col'), 0, 0, tiled=True)]
  transfers between devices with their start and end apart: 17 -> 18, of which waited for: 3 -> 3; matrix products, arithmetic and copies ran while one was open for 2% -> 2% of each run, Pallas kernels for 10% -> 7%
where the time goes in v7:
time: 108 us
  starting transfers between devices  47.1 us (44%)
  blocking collectives  36.5 us (34%)
  Pallas kernels  14.7 us (14%)
  waiting for transfers between devices  4.71 us (4%)
  local copies, waits for them, and re-layouts  3.59 us (3%)
  between operations  1.08 us (1%)
    ppermute x18, starting transfers between devices, swap(): return lax.ppermute(value, axis, pairs + [(b, a) for a, b in pairs])  47.1 us
    all_to_all x3, blocking collectives, shards(): parts = lax.all_to_all(part, ('row', 'col'), 0, 0, tiled=True)  36.5 us
    pallas_call x14, Pallas kernels, run(): pl.pallas_call(kernel, name=body.__name__, out_shape=[jax.ShapeDtypeStruc...  14.7 us
    ppermute x18, waiting for transfers between devices, swap(): return lax.ppermute(value, axis, pairs + [(b, a) for a, b in pairs])  4.71 us
    unnamed x17, local copies, waits for them, and re-layouts  2.66 us
  transfers between devices with their start and end apart: 18, of which 3 were waited for; matrix products, arithmetic and copies ran while one was open for 2% of the time, Pallas kernels for 7%

profile of v7, /device:TPU:0, one launch (start us, length us, event | category | flops | bytes accessed | tf_op | source)
XLA Modules:
  0.0 107.7 jit_solution(17291304536760686353)
XLA Ops:
  0.7 0.1 stack.27
  0.8 1.2 %copy-done = f32[1024,256]{1,0:T(8,128)S(1)} copy-done((f32[1024,256]{1,0:T(8,128)S(1)}, f32[1024,256]{1,0:T(8,128)}, u32[]{:S(2)}) %copy-start) | copy-done | bytes 1048600
  2.0 0.7 pack_kernel.1
  2.7 0.7 collective-permute-start
  3.4 4.3 %collective-permute-start.1 = (f32[512,128]{1,0:T(8,128)S(1)}, f32[512,128]{1,0:T(8,128)S(1)}, u32[]{:S(2)}, u32[]{:S(2)}) collective-permute-start(f32[512,128]{1,0:T(8,128)S(1)} %get-tuple-element.71), channel_id=1, source_target_pairs={{0,1},{2,3},{4,5},{6,7},{1,0},{3,2},{5,4},{7,6},{8,9},{10,11},{12,... | collective-permute-start | bytes 786440 | tf_op jit(solution)/shard_map/ppermute | solution.py:674
  7.8 1.0 copy.15
  8.8 0.8 dynamic-slice_bitcast_fusion
  9.6 0.0 copy-done.6
  9.6 0.8 spectra_kernel.1.refs_1_
  10.4 0.0 copy-start.2
  10.4 0.0 copy-start.3
  10.4 0.0 copy-start.4
  10.4 0.0 copy-start.5
  10.5 0.0 collective-permute-done.refs_2_.refs_7_
  10.5 0.0 collective-permute-done.1.refs_3_.refs_8_
  10.5 0.4 copy-done.1
  10.9 0.6 halo_kernel.1
  11.5 0.7 collective-permute-start.2
  12.2 4.5 %collective-permute-start.3 = (f32[64,384]{1,0:T(8,128)S(1)}, f32[64,384]{1,0:T(8,128)S(1)}, u32[]{:S(2)}, u32[]{:S(2)}) collective-permute-start(f32[64,384]{1,0:T(8,128)S(1)} %get-tuple-element.81), channel_id=1, source_target_pairs={{0,8},{16,24},{8,0},{24,16},{1,9},{17,25},{9,1},{25,17},{2,10},{18... | collective-permute-start | bytes 294920 | tf_op jit(solution)/shard_map/ppermute | solution.py:674
  16.6 0.0 copy-done.5
  16.6 0.9 middle_kernel.3
  17.5 0.0 collective-permute-done.2.refs_10_
  17.5 1.7 %collective-permute-done.3.refs_11_ = f32[64,384]{1,0:T(8,128)S(1)} collective-permute-done((f32[64,384]{1,0:T(8,128)S(1)}, f32[64,384]{1,0:T(8,128)S(1)}, u32[]{:S(2)}, u32[]{:S(2)}) %collective-permute-start.3) | collective-permute-done | bytes 98336 | tf_op jit(solution)/shard_map/ppermute | solution.py:674
  19.2 0.8 edge_kernel.3
  20.1 0.7 collective-permute-start.4
  20.8 6.0 %collective-permute-start.5 = (f32[1152,128]{1,0:T(8,128)S(1)}, f32[1152,128]{1,0:T(8,128)S(1)}, u32[]{:S(2)}, u32[]{:S(2)}) collective-permute-start(f32[1152,128]{1,0:T(8,128)S(1)} %get-tuple-element.86), channel_id=1, source_target_pairs={{0,1},{2,3},{4,5},{6,7},{1,0},{3,2},{5,4},{7,6},{8,9},{10,11},{12,... | collective-permute-start | bytes 1769480 | tf_op jit(solution)/shard_map/ppermute | solution.py:674
  26.8 14.1 %all_to_all.36 = f32[32,1,128]{2,1,0:T(1,128)S(1)} all-to-all(f32[32,1,128]{2,1,0:T(1,128)S(1)} %bitcast.27), channel_id=1, replica_groups=mesh['row'=4,'col'=8] {'row','col'}, dimensions={0} | all-to-all | bytes 32768 | tf_op jit(solution)/shard_map/all_to_all | solution.py:773
  40.9 0.0 collective-permute-done.4.refs_6_.refs_2_
  40.9 0.0 collective-permute-done.5.refs_7_.refs_3_
  40.9 0.6 row_strip_kernel.3
  41.5 0.7 collective-permute-start.8
  42.2 3.3 %collective-permute-start.9 = (f32[128,384]{1,0:T(8,128)S(1)}, f32[128,384]{1,0:T(8,128)S(1)}, u32[]{:S(2)}, u32[]{:S(2)}) collective-permute-start(f32[128,384]{1,0:T(8,128)S(1)} %get-tuple-element.98), channel_id=1, source_target_pairs={{0,8},{16,24},{8,0},{24,16},{1,9},{17,25},{9,1},{25,17},{2,10},{18... | collective-permute-start | bytes 589832 | tf_op jit(solution)/shard_map/ppermute | solution.py:674
  45.5 1.3 %middle_kernel.4 = (f32[896,384]{1,0:T(8,128)S(1)}, f32[640,384]{1,0:T(8,128)S(1)}, f32[3,8,128]{2,1,0:T(8,128)S(1)}, f32[9,8,128]{2,1,0:T(8,128)S(1)}, f32[384,128]{1,0:T(8,128)S(1)}, /*index=5*/f32[384,128]{1,0:T(8,128)S(1)}) custom-call(s32[4]{0:T(128)S(1)} %get-tuple-element.139.refs_1_.refs_0_, f32[4,2,256,256]{3,2,1,0:T(8,128)S(1)} %spectra_kernel.1.refs_1_, ...), custom_call_target="tpu_custom_call" | custom-call | tf_op jit(solution)/shard_map/middle_kernel/pallas_call | solution.py:649
  46.8 0.7 collective-permute-start.6
  47.5 6.4 %collective-permute-start.7 = (f32[384,128]{1,0:T(8,128)S(1)}, f32[384,128]{1,0:T(8,128)S(1)}, u32[]{:S(2)}, u32[]{:S(2)}) collective-permute-start(f32[384,128]{1,0:T(8,128)S(1)} %get-tuple-element.94), channel_id=1, source_target_pairs={{0,1},{2,3},{4,5},{6,7},{1,0},{3,2},{5,4},{7,6},{8,9},{10,11},{12,... | collective-permute-start | bytes 589832 | tf_op jit(solution)/shard_map/ppermute | solution.py:674
  53.9 0.0 collective-permute-done.8.refs_13_
  53.9 0.0 collective-permute-done.9.refs_14_
  53.9 0.9 edge_kernel.4
  54.8 0.0 collective-permute-done.6.refs_8_.refs_4_
  54.8 0.2 collective-permute-done.7.refs_9_.refs_5_
  55.0 0.7 collective-permute-start.10
  55.7 5.2 %collective-permute-start.11 = (f32[768,128]{1,0:T(8,128)S(1)}, f32[768,128]{1,0:T(8,128)S(1)}, u32[]{:S(2)}, u32[]{:S(2)}) collective-permute-start(f32[768,128]{1,0:T(8,128)S(1)} %get-tuple-element.106), channel_id=1, source_target_pairs={{0,1},{2,3},{4,5},{6,7},{1,0},{3,2},{5,4},{7,6},{8,9},{10,11},{12,... | collective-permute-start | bytes 1179656 | tf_op jit(solution)/shard_map/ppermute | solution.py:674
  60.9 12.4 %all_to_all.37 = f32[32,1,128]{2,1,0:T(1,128)S(1)} all-to-all(f32[32,1,128]{2,1,0:T(1,128)S(1)} %bitcast.25), channel_id=1, replica_groups=mesh['row'=4,'col'=8] {'row','col'}, dimensions={0} | all-to-all | bytes 32768 | tf_op jit(solution)/shard_map/all_to_all | solution.py:773
  73.4 0.0 collective-permute-done.10.refs_6_.refs_2_
  73.4 0.0 collective-permute-done.11.refs_7_.refs_3_
  73.4 0.6 row_strip_kernel.4
  74.0 0.9 collective-permute-start.12
  74.9 2.5 %collective-permute-start.13 = (f32[128,384]{1,0:T(8,128)S(1)}, f32[128,384]{1,0:T(8,128)S(1)}, u32[]{:S(2)}, u32[]{:S(2)}) collective-permute-start(f32[128,384]{1,0:T(8,128)S(1)} %get-tuple-element.120), channel_id=1, source_target_pairs={{0,8},{16,24},{8,0},{24,16},{1,9},{17,25},{9,1},{25,17},{2,10},{18... | collective-permute-start | bytes 589832 | tf_op jit(solution)/shard_map/ppermute | solution.py:674
  77.3 1.7 %middle_kernel.5 = (f32[896,384]{1,0:T(8,128)S(1)}, f32[640,384]{1,0:T(8,128)S(1)}, f32[3,8,128]{2,1,0:T(8,128)S(1)}, f32[9,8,128]{2,1,0:T(8,128)S(1)}) custom-call(s32[4]{0:T(128)S(1)} %get-tuple-element.139.refs_1_.refs_0_, f32[4,2,256,256]{3,2,1,0:T(8,128)S(1)} %spectra_kernel.1.refs_1_, bf16[512,256]{1,0:T(8,128)(2,1)S(1)} %copy-done.3, ...), custom_call_target="tpu_custom_call" | custom-call | tf_op jit(solution)/shard_map/middle_kernel/pallas_call | solution.py:649
  79.0 0.0 collective-permute-done.12.refs_16_
  79.0 2.8 %collective-permute-done.13.refs_17_ = f32[128,384]{1,0:T(8,128)S(1)} collective-permute-done((f32[128,384]{1,0:T(8,128)S(1)}, f32[128,384]{1,0:T(8,128)S(1)}, u32[]{:S(2)}, u32[]{:S(2)}) %collective-permute-start.13) | collective-permute-done | bytes 196640 | tf_op jit(solution)/shard_map/ppermute | solution.py:674
  81.8 1.1 edge_kernel.5
  82.9 0.7 collective-permute-start.14
  83.6 6.1 %collective-permute-start.15 = (f32[576,128]{1,0:T(8,128)S(1)}, f32[576,128]{1,0:T(8,128)S(1)}, u32[]{:S(2)}, u32[]{:S(2)}) collective-permute-start(f32[576,128]{1,0:T(8,128)S(1)} %get-tuple-element.125), channel_id=1, source_target_pairs={{0,1},{2,3},{4,5},{6,7},{1,0},{3,2},{5,4},{7,6},{8,9},{10,11},{12,... | collective-permute-start | bytes 884744 | tf_op jit(solution)/shard_map/ppermute | solution.py:674
  89.8 9.9 %all_to_all.38 = f32[32,1,128]{2,1,0:T(1,128)S(1)} all-to-all(f32[32,1,128]{2,1,0:T(1,128)S(1)} %bitcast.26), channel_id=1, replica_groups=mesh['row'=4,'col'=8] {'row','col'}, dimensions={0} | all-to-all | bytes 32768 | tf_op jit(solution)/shard_map/all_to_all | solution.py:773
  99.7 0.0 collective-permute-done.14.refs_4_.refs_5_
  99.7 0.0 collective-permute-done.15.refs_5_.refs_6_
  99.7 0.9 row_strip_kernel.5
  100.6 0.7 collective-permute-start.16
  101.3 2.5 %collective-permute-start.17 = (f32[64,256]{1,0:T(8,128)S(1)}, f32[64,256]{1,0:T(8,128)S(1)}, u32[]{:S(2)}, u32[]{:S(2)}) collective-permute-start(f32[64,256]{1,0:T(8,128)S(1)} %get-tuple-element.134), channel_id=1, source_target_pairs={{0,8},{16,24},{8,0},{24,16},{1,9},{17,25},{9,1},{25,17},{2,10},{18... | collective-permute-start | bytes 196616 | tf_op jit(solution)/shard_map/ppermute | solution.py:674
  103.7 2.4 %last_middle_kernel.1 = (f32[1024,256]{1,0:T(8,128)}, f32[1024,256]{1,0:T(8,128)}) custom-call(f32[9,8,128]{2,1,0:T(8,128)S(1)} %get-tuple-element.132.refs_0_, f32[640,384]{1,0:T(8,128)S(1)} %get-tuple-element.122.refs_19_.refs_1_, f32[384,384]{1,0:T(8,128)S(1)} %get-tuple-element.128.refs_2_.refs_3_, f32[384,384]{1,0:T(8,128)S(1)} %get-tuple-element.129.refs_3_.refs_4_, ...), custom_call_target="tpu_custom_call" | custom-call | tf_op jit(solution)/shard_map/last_middle_kernel/pallas_call | solution.py:649
  106.2 0.0 collective-permute-done.16.refs_1_
  106.2 0.0 collective-permute-done.17.refs_2_
  106.2 1.4 %last_edge_kernel.1 = (f32[1024,256]{1,0:T(8,128)}, f32[1024,256]{1,0:T(8,128)}) custom-call(f32[9,8,128]{2,1,0:T(8,128)S(1)} %get-tuple-element.132.refs_0_, f32[64,256]{1,0:T(8,128)S(1)} %collective-permute-done.16.refs_1_, f32[64,256]{1,0:T(8,128)S(1)} %collective-permute-done.17.refs_2_, ...), custom_call_target="tpu_custom_call", output_to_operand_aliasing={{0}: (11, {}), {1}: (12, {})} | custom-call | tf_op jit(solution)/shard_map/last_edge_kernel/pallas_call | solution.py:649
  (10 shorter events, 0.1 us)
Async XLA Ops:
  0.8 1.2 %copy-start = (f32[1024,256]{1,0:T(8,128)S(1)}, f32[1024,256]{1,0:T(8,128)}, u32[]{:S(2)}) copy-start(f32[1024,256]{1,0:T(8,128)} %refs_9_.3) | copy-start | bytes 3145732
  2.0 7.6 %copy-start.6 = (bf16[384,512]{1,0:T(8,128)(2,1)S(1)}, bf16[384,512]{1,0:T(8,128)(2,1)}, u32[]{:S(2)}) copy-start(bf16[384,512]{1,0:T(8,128)(2,1)} %constant.84.clone.refs_4_) | copy-start | bytes 1179652
  2.0 7.6 %copy-start.7 = (bf16[512,384]{1,0:T(8,128)(2,1)S(1)}, bf16[512,384]{1,0:T(8,128)(2,1)}, u32[]{:S(2)}) copy-start(bf16[512,384]{1,0:T(8,128)(2,1)} %constant.83.clone.refs_3_) | copy-start | bytes 1179652
  2.7 7.7 %collective-permute-start = (f32[512,128]{1,0:T(8,128)S(1)}, f32[512,128]{1,0:T(8,128)S(1)}, u32[]{:S(2)}, u32[]{:S(2)}) collective-permute-start(f32[512,128]{1,0:T(8,128)S(1)} %get-tuple-element.70), channel_id=1, source_target_pairs={{1,2},{3,4},{5,6},{2,1},{4,3},{6,5},{9,10},{11,12},{13,14},{10,9},... | collective-permute-start | bytes 786440 | tf_op jit(solution)/shard_map/ppermute | solution.py:674
  3.4 7.0 %collective-permute-start.1 = (f32[512,128]{1,0:T(8,128)S(1)}, f32[512,128]{1,0:T(8,128)S(1)}, u32[]{:S(2)}, u32[]{:S(2)}) collective-permute-start(f32[512,128]{1,0:T(8,128)S(1)} %get-tuple-element.71), channel_id=1, source_target_pairs={{0,1},{2,3},{4,5},{6,7},{1,0},{3,2},{5,4},{7,6},{8,9},{10,11},{12,... | collective-permute-start | bytes 786440 | tf_op jit(solution)/shard_map/ppermute | solution.py:674
  9.6 1.2 %copy-start.1 = (f32[1024,256]{1,0:T(8,128)S(1)}, f32[1024,256]{1,0:T(8,128)}, u32[]{:S(2)}) copy-start(f32[1024,256]{1,0:T(8,128)} %refs_9_.3) | copy-start | bytes 3145732
  10.4 6.2 %copy-start.2 = (bf16[512,256]{1,0:T(8,128)(2,1)S(1)}, bf16[512,256]{1,0:T(8,128)(2,1)}, u32[]{:S(2)}) copy-start(bf16[512,256]{1,0:T(8,128)(2,1)} %constant.80.clone.refs_3_) | copy-start | bytes 786436
  10.4 6.2 %copy-start.3 = (bf16[512,256]{1,0:T(8,128)(2,1)S(1)}, bf16[512,256]{1,0:T(8,128)(2,1)}, u32[]{:S(2)}) copy-start(bf16[512,256]{1,0:T(8,128)(2,1)} %constant.79.clone.refs_2_) | copy-start | bytes 786436
  10.4 6.2 %copy-start.4 = (bf16[256,128]{1,0:T(8,128)(2,1)S(1)}, bf16[256,128]{1,0:T(8,128)(2,1)}, u32[]{:S(2)}) copy-start(bf16[256,128]{1,0:T(8,128)(2,1)} %constant.82.clone.refs_5_) | copy-start | bytes 196612
  10.4 6.2 %copy-start.5 = (bf16[256,128]{1,0:T(8,128)(2,1)S(1)}, bf16[256,128]{1,0:T(8,128)(2,1)}, u32[]{:S(2)}) copy-start(bf16[256,128]{1,0:T(8,128)(2,1)} %constant.81.clone.refs_4_) | copy-start | bytes 196612
  11.5 6.0 %collective-permute-start.2 = (f32[64,384]{1,0:T(8,128)S(1)}, f32[64,384]{1,0:T(8,128)S(1)}, u32[]{:S(2)}, u32[]{:S(2)}) collective-permute-start(f32[64,384]{1,0:T(8,128)S(1)} %get-tuple-element.80), channel_id=1, source_target_pairs={{8,16},{16,8},{9,17},{17,9},{10,18},{18,10},{11,19},{19,11},{12,20... | collective-permute-start | bytes 294920 | tf_op jit(solution)/shard_map/ppermute | solution.py:674
  12.2 7.1 %collective-permute-start.3 = (f32[64,384]{1,0:T(8,128)S(1)}, f32[64,384]{1,0:T(8,128)S(1)}, u32[]{:S(2)}, u32[]{:S(2)}) collective-permute-start(f32[64,384]{1,0:T(8,128)S(1)} %get-tuple-element.81), channel_id=1, source_target_pairs={{0,8},{16,24},{8,0},{24,16},{1,9},{17,25},{9,1},{25,17},{2,10},{18... | collective-permute-start | bytes 294920 | tf_op jit(solution)/shard_map/ppermute | solution.py:674
  20.1 20.8 %collective-permute-start.4 = (f32[1152,128]{1,0:T(8,128)S(1)}, f32[1152,128]{1,0:T(8,128)S(1)}, u32[]{:S(2)}, u32[]{:S(2)}) collective-permute-start(f32[1152,128]{1,0:T(8,128)S(1)} %get-tuple-element.85), channel_id=1, source_target_pairs={{1,2},{3,4},{5,6},{2,1},{4,3},{6,5},{9,10},{11,12},{13,14},{10,9},... | collective-permute-start | bytes 1769480 | tf_op jit(solution)/shard_map/ppermute | solution.py:674
  20.8 20.1 %collective-permute-start.5 = (f32[1152,128]{1,0:T(8,128)S(1)}, f32[1152,128]{1,0:T(8,128)S(1)}, u32[]{:S(2)}, u32[]{:S(2)}) collective-permute-start(f32[1152,128]{1,0:T(8,128)S(1)} %get-tuple-element.86), channel_id=1, source_target_pairs={{0,1},{2,3},{4,5},{6,7},{1,0},{3,2},{5,4},{7,6},{8,9},{10,11},{12,... | collective-permute-start | bytes 1769480 | tf_op jit(solution)/shard_map/ppermute | solution.py:674
  41.5 12.4 %collective-permute-start.8 = (f32[128,384]{1,0:T(8,128)S(1)}, f32[128,384]{1,0:T(8,128)S(1)}, u32[]{:S(2)}, u32[]{:S(2)}) collective-permute-start(f32[128,384]{1,0:T(8,128)S(1)} %get-tuple-element.97), channel_id=1, source_target_pairs={{8,16},{16,8},{9,17},{17,9},{10,18},{18,10},{11,19},{19,11},{12,20... | collective-permute-start | bytes 589832 | tf_op jit(solution)/shard_map/ppermute | solution.py:674
  42.2 11.7 %collective-permute-start.9 = (f32[128,384]{1,0:T(8,128)S(1)}, f32[128,384]{1,0:T(8,128)S(1)}, u32[]{:S(2)}, u32[]{:S(2)}) collective-permute-start(f32[128,384]{1,0:T(8,128)S(1)} %get-tuple-element.98), channel_id=1, source_target_pairs={{0,8},{16,24},{8,0},{24,16},{1,9},{17,25},{9,1},{25,17},{2,10},{18... | collective-permute-start | bytes 589832 | tf_op jit(solution)/shard_map/ppermute | solution.py:674
  46.8 8.0 %collective-permute-start.6 = (f32[384,128]{1,0:T(8,128)S(1)}, f32[384,128]{1,0:T(8,128)S(1)}, u32[]{:S(2)}, u32[]{:S(2)}) collective-permute-start(f32[384,128]{1,0:T(8,128)S(1)} %get-tuple-element.93), channel_id=1, source_target_pairs={{1,2},{3,4},{5,6},{2,1},{4,3},{6,5},{9,10},{11,12},{13,14},{10,9},... | collective-permute-start | bytes 589832 | tf_op jit(solution)/shard_map/ppermute | solution.py:674
  47.5 7.5 %collective-permute-start.7 = (f32[384,128]{1,0:T(8,128)S(1)}, f32[384,128]{1,0:T(8,128)S(1)}, u32[]{:S(2)}, u32[]{:S(2)}) collective-permute-start(f32[384,128]{1,0:T(8,128)S(1)} %get-tuple-element.94), channel_id=1, source_target_pairs={{0,1},{2,3},{4,5},{6,7},{1,0},{3,2},{5,4},{7,6},{8,9},{10,11},{12,... | collective-permute-start | bytes 589832 | tf_op jit(solution)/shard_map/ppermute | solution.py:674
  55.0 18.4 %collective-permute-start.10 = (f32[768,128]{1,0:T(8,128)S(1)}, f32[768,128]{1,0:T(8,128)S(1)}, u32[]{:S(2)}, u32[]{:S(2)}) collective-permute-start(f32[768,128]{1,0:T(8,128)S(1)} %get-tuple-element.105), channel_id=1, source_target_pairs={{1,2},{3,4},{5,6},{2,1},{4,3},{6,5},{9,10},{11,12},{13,14},{10,9},... | collective-permute-start | bytes 1179656 | tf_op jit(solution)/shard_map/ppermute | solution.py:674
  55.7 17.7 %collective-permute-start.11 = (f32[768,128]{1,0:T(8,128)S(1)}, f32[768,128]{1,0:T(8,128)S(1)}, u32[]{:S(2)}, u32[]{:S(2)}) collective-permute-start(f32[768,128]{1,0:T(8,128)S(1)} %get-tuple-element.106), channel_id=1, source_target_pairs={{0,1},{2,3},{4,5},{6,7},{1,0},{3,2},{5,4},{7,6},{8,9},{10,11},{12,... | collective-permute-start | bytes 1179656 | tf_op jit(solution)/shard_map/ppermute | solution.py:674
  74.0 5.0 %collective-permute-start.12 = (f32[128,384]{1,0:T(8,128)S(1)}, f32[128,384]{1,0:T(8,128)S(1)}, u32[]{:S(2)}, u32[]{:S(2)}) collective-permute-start(f32[128,384]{1,0:T(8,128)S(1)} %get-tuple-element.119), channel_id=1, source_target_pairs={{8,16},{16,8},{9,17},{17,9},{10,18},{18,10},{11,19},{19,11},{12,20... | collective-permute-start | bytes 589832 | tf_op jit(solution)/shard_map/ppermute | solution.py:674
  74.9 7.0 %collective-permute-start.13 = (f32[128,384]{1,0:T(8,128)S(1)}, f32[128,384]{1,0:T(8,128)S(1)}, u32[]{:S(2)}, u32[]{:S(2)}) collective-permute-start(f32[128,384]{1,0:T(8,128)S(1)} %get-tuple-element.120), channel_id=1, source_target_pairs={{0,8},{16,24},{8,0},{24,16},{1,9},{17,25},{9,1},{25,17},{2,10},{18... | collective-permute-start | bytes 589832 | tf_op jit(solution)/shard_map/ppermute | solution.py:674
  82.9 16.8 %collective-permute-start.14 = (f32[576,128]{1,0:T(8,128)S(1)}, f32[576,128]{1,0:T(8,128)S(1)}, u32[]{:S(2)}, u32[]{:S(2)}) collective-permute-start(f32[576,128]{1,0:T(8,128)S(1)} %get-tuple-element.124), channel_id=1, source_target_pairs={{1,2},{3,4},{5,6},{2,1},{4,3},{6,5},{9,10},{11,12},{13,14},{10,9},... | collective-permute-start | bytes 884744 | tf_op jit(solution)/shard_map/ppermute | solution.py:674
  83.6 16.1 %collective-permute-start.15 = (f32[576,128]{1,0:T(8,128)S(1)}, f32[576,128]{1,0:T(8,128)S(1)}, u32[]{:S(2)}, u32[]{:S(2)}) collective-permute-start(f32[576,128]{1,0:T(8,128)S(1)} %get-tuple-element.125), channel_id=1, source_target_pairs={{0,1},{2,3},{4,5},{6,7},{1,0},{3,2},{5,4},{7,6},{8,9},{10,11},{12,... | collective-permute-start | bytes 884744 | tf_op jit(solution)/shard_map/ppermute | solution.py:674
  100.6 5.6 %collective-permute-start.16 = (f32[64,256]{1,0:T(8,128)S(1)}, f32[64,256]{1,0:T(8,128)S(1)}, u32[]{:S(2)}, u32[]{:S(2)}) collective-permute-start(f32[64,256]{1,0:T(8,128)S(1)} %get-tuple-element.133), channel_id=1, source_target_pairs={{8,16},{16,8},{9,17},{17,9},{10,18},{18,10},{11,19},{19,11},{12,20... | collective-permute-start | bytes 196616 | tf_op jit(solution)/shard_map/ppermute | solution.py:674
  101.3 4.9 %collective-permute-start.17 = (f32[64,256]{1,0:T(8,128)S(1)}, f32[64,256]{1,0:T(8,128)S(1)}, u32[]{:S(2)}, u32[]{:S(2)}) collective-permute-start(f32[64,256]{1,0:T(8,128)S(1)} %get-tuple-element.134), channel_id=1, source_target_pairs={{0,8},{16,24},{8,0},{24,16},{1,9},{17,25},{9,1},{25,17},{2,10},{18... | collective-permute-start | bytes 196616 | tf_op jit(solution)/shard_map/ppermute | solution.py:674

commit v8 on v7

--- a/solution.py
+++ b/solution.py
@@ -537,6 +537,10 @@
         r.low_sum_new[...] = jnp.zeros((WIN, WIN), F32)
         r.curve[...] = jnp.zeros((8, THIRD), F32)
 
+    gamma = total(square)
+    curve = gamma + total(r.acc[2] + r.curve[...])
+    r.part[...] = lanes_of(r.part.shape, gamma, curve, total(cross))
+
     low = lane_mask()
     new = Refs(tiles=r.tiles, top_sum=r.top_sum_new, mid_sum=r.mid_sum_new, low_sum=r.low_sum_new)
     if r.narrow:
@@ -564,9 +568,6 @@
                 send_columns(r, rows_at(num), *strips)
             elif num < 3 or num >= 3 + middle:
                 send_columns(r, rows_at(num if num < 3 else num - middle), *strips)
-    gamma = total(square)
-    curve = gamma + total(r.acc[2] + r.curve[...])
-    r.part[...] = lanes_of(r.part.shape, gamma, curve, total(cross))
 
 
 def last_rows(r, start, corrected, residual, at):

time: 108 us -> 108 us (level); the launches traced: 108 us -> 107 us
  starting transfers between devices: 47.1 us -> 42.7 us
  blocking collectives: 36.5 us -> 39.5 us
    ppermute x18, starting transfers between devices: 47.1 us -> 42.7 us  [swap(): return lax.ppermute(value, axis, pairs + [(b, a) for a, b in pairs])]
    all_to_all x3, blocking collectives: 36.5 us -> 39.5 us  [shards(): parts = lax.all_to_all(part, ('row', 'col'), 0, 0, tiled=True)]
where the time goes in v8:
time: 108 us; the launch traced here: 107 us
  starting transfers between devices  42.7 us (40%)
  blocking collectives  39.5 us (37%)
  Pallas kernels  14.7 us (14%)
  waiting for transfers between devices  4.91 us (5%)
  local copies, waits for them, and re-layouts  3.59 us (3%)
  between operations  1.08 us (1%)
    ppermute x18, starting transfers between devices, swap(): return lax.ppermute(value, axis, pairs + [(b, a) for a, b in pairs])  42.7 us
    all_to_all x3, blocking collectives, shards(): parts = lax.all_to_all(part, ('row', 'col'), 0, 0, tiled=True)  39.5 us
    pallas_call x14, Pallas kernels, run(): pl.pallas_call(kernel, name=body.__name__, out_shape=[jax.ShapeDtypeStruc...  14.7 us
    ppermute x18, waiting for transfers between devices, swap(): return lax.ppermute(value, axis, pairs + [(b, a) for a, b in pairs])  4.91 us
    unnamed x17, local copies, waits for them, and re-layouts  2.66 us
  transfers between devices with their start and end apart: 18, of which 3 were waited for; matrix products, arithmetic and copies ran while one was open for 2% of the time, Pallas kernels for 7%

profile of v8, /device:TPU:0, one launch (start us, length us, event | category | flops | bytes accessed | tf_op | source)
XLA Modules:
  0.0 106.5 jit_solution(15031060613140006091)
XLA Ops:
  0.7 0.1 stack.27
  0.8 1.2 %copy-done = f32[1024,256]{1,0:T(8,128)S(1)} copy-done((f32[1024,256]{1,0:T(8,128)S(1)}, f32[1024,256]{1,0:T(8,128)}, u32[]{:S(2)}) %copy-start) | copy-done | bytes 1048600
  2.0 0.7 pack_kernel.1
  2.7 0.7 collective-permute-start
  3.4 4.3 %collective-permute-start.1 = (f32[512,128]{1,0:T(8,128)S(1)}, f32[512,128]{1,0:T(8,128)S(1)}, u32[]{:S(2)}, u32[]{:S(2)}) collective-permute-start(f32[512,128]{1,0:T(8,128)S(1)} %get-tuple-element.71), channel_id=1, source_target_pairs={{0,1},{2,3},{4,5},{6,7},{1,0},{3,2},{5,4},{7,6},{8,9},{10,11},{12,... | collective-permute-start | bytes 786440 | tf_op jit(solution)/shard_map/ppermute | solution.py:675
  7.8 1.0 copy.15
  8.8 0.8 dynamic-slice_bitcast_fusion
  9.6 0.0 copy-done.7
  9.6 0.8 spectra_kernel.1.refs_1_
  10.4 0.0 copy-start.2
  10.4 0.0 copy-start.3
  10.4 0.0 copy-start.4
  10.4 0.0 copy-start.5
  10.5 0.0 collective-permute-done.refs_2_.refs_7_
  10.5 0.0 collective-permute-done.1.refs_3_.refs_8_
  10.5 0.4 copy-done.1
  10.9 0.6 halo_kernel.1
  11.5 0.7 collective-permute-start.2
  12.2 4.8 %collective-permute-start.3 = (f32[64,384]{1,0:T(8,128)S(1)}, f32[64,384]{1,0:T(8,128)S(1)}, u32[]{:S(2)}, u32[]{:S(2)}) collective-permute-start(f32[64,384]{1,0:T(8,128)S(1)} %get-tuple-element.81), channel_id=1, source_target_pairs={{0,8},{16,24},{8,0},{24,16},{1,9},{17,25},{9,1},{25,17},{2,10},{18... | collective-permute-start | bytes 294920 | tf_op jit(solution)/shard_map/ppermute | solution.py:675
  16.9 0.0 copy-done.3
  17.0 0.9 middle_kernel.3
  17.8 0.0 collective-permute-done.2.refs_10_
  17.8 1.7 %collective-permute-done.3.refs_11_ = f32[64,384]{1,0:T(8,128)S(1)} collective-permute-done((f32[64,384]{1,0:T(8,128)S(1)}, f32[64,384]{1,0:T(8,128)S(1)}, u32[]{:S(2)}, u32[]{:S(2)}) %collective-permute-start.3) | collective-permute-done | bytes 98336 | tf_op jit(solution)/shard_map/ppermute | solution.py:675
  19.5 0.8 edge_kernel.3
  20.4 0.7 collective-permute-start.4
  21.1 5.7 %collective-permute-start.5 = (f32[1152,128]{1,0:T(8,128)S(1)}, f32[1152,128]{1,0:T(8,128)S(1)}, u32[]{:S(2)}, u32[]{:S(2)}) collective-permute-start(f32[1152,128]{1,0:T(8,128)S(1)} %get-tuple-element.86), channel_id=1, source_target_pairs={{0,1},{2,3},{4,5},{6,7},{1,0},{3,2},{5,4},{7,6},{8,9},{10,11},{12,... | collective-permute-start | bytes 1769480 | tf_op jit(solution)/shard_map/ppermute | solution.py:675
  26.8 14.9 %all_to_all.36 = f32[32,1,128]{2,1,0:T(1,128)S(1)} all-to-all(f32[32,1,128]{2,1,0:T(1,128)S(1)} %bitcast.27), channel_id=1, replica_groups=mesh['row'=4,'col'=8] {'row','col'}, dimensions={0} | all-to-all | bytes 32768 | tf_op jit(solution)/shard_map/all_to_all | solution.py:774
  41.6 0.0 collective-permute-done.4.refs_6_.refs_2_
  41.6 0.0 collective-permute-done.5.refs_7_.refs_3_
  41.6 0.6 row_strip_kernel.3
  42.3 0.7 collective-permute-start.8
  43.0 4.5 %collective-permute-start.9 = (f32[128,384]{1,0:T(8,128)S(1)}, f32[128,384]{1,0:T(8,128)S(1)}, u32[]{:S(2)}, u32[]{:S(2)}) collective-permute-start(f32[128,384]{1,0:T(8,128)S(1)} %get-tuple-element.98), channel_id=1, source_target_pairs={{0,8},{16,24},{8,0},{24,16},{1,9},{17,25},{9,1},{25,17},{2,10},{18... | collective-permute-start | bytes 589832 | tf_op jit(solution)/shard_map/ppermute | solution.py:675
  47.5 1.3 %middle_kernel.4 = (f32[896,384]{1,0:T(8,128)S(1)}, f32[640,384]{1,0:T(8,128)S(1)}, f32[3,8,128]{2,1,0:T(8,128)S(1)}, f32[9,8,128]{2,1,0:T(8,128)S(1)}, f32[384,128]{1,0:T(8,128)S(1)}, /*index=5*/f32[384,128]{1,0:T(8,128)S(1)}) custom-call(s32[4]{0:T(128)S(1)} %get-tuple-element.139.refs_1_.refs_0_, f32[4,2,256,256]{3,2,1,0:T(8,128)S(1)} %spectra_kernel.1.refs_1_, ...), custom_call_target="tpu_custom_call" | custom-call | tf_op jit(solution)/shard_map/middle_kernel/pallas_call | solution.py:650
  48.8 0.7 collective-permute-start.6
  49.5 3.0 %collective-permute-start.7 = (f32[384,128]{1,0:T(8,128)S(1)}, f32[384,128]{1,0:T(8,128)S(1)}, u32[]{:S(2)}, u32[]{:S(2)}) collective-permute-start(f32[384,128]{1,0:T(8,128)S(1)} %get-tuple-element.94), channel_id=1, source_target_pairs={{0,1},{2,3},{4,5},{6,7},{1,0},{3,2},{5,4},{7,6},{8,9},{10,11},{12,... | collective-permute-start | bytes 589832 | tf_op jit(solution)/shard_map/ppermute | solution.py:675
  52.5 0.0 collective-permute-done.8.refs_13_
  52.5 0.0 collective-permute-done.9.refs_14_
  52.5 0.9 edge_kernel.4
  53.4 0.0 collective-permute-done.6.refs_8_.refs_4_
  53.4 0.2 collective-permute-done.7.refs_9_.refs_5_
  53.5 0.7 collective-permute-start.10
  54.2 5.2 %collective-permute-start.11 = (f32[768,128]{1,0:T(8,128)S(1)}, f32[768,128]{1,0:T(8,128)S(1)}, u32[]{:S(2)}, u32[]{:S(2)}) collective-permute-start(f32[768,128]{1,0:T(8,128)S(1)} %get-tuple-element.106), channel_id=1, source_target_pairs={{0,1},{2,3},{4,5},{6,7},{1,0},{3,2},{5,4},{7,6},{8,9},{10,11},{12,... | collective-permute-start | bytes 1179656 | tf_op jit(solution)/shard_map/ppermute | solution.py:675
  59.5 12.4 %all_to_all.37 = f32[32,1,128]{2,1,0:T(1,128)S(1)} all-to-all(f32[32,1,128]{2,1,0:T(1,128)S(1)} %bitcast.25), channel_id=1, replica_groups=mesh['row'=4,'col'=8] {'row','col'}, dimensions={0} | all-to-all | bytes 32768 | tf_op jit(solution)/shard_map/all_to_all | solution.py:774
  71.9 0.0 collective-permute-done.10.refs_6_.refs_2_
  71.9 0.0 collective-permute-done.11.refs_7_.refs_3_
  71.9 0.6 row_strip_kernel.4
  72.5 0.9 collective-permute-start.12
  73.4 3.3 %collective-permute-start.13 = (f32[128,384]{1,0:T(8,128)S(1)}, f32[128,384]{1,0:T(8,128)S(1)}, u32[]{:S(2)}, u32[]{:S(2)}) collective-permute-start(f32[128,384]{1,0:T(8,128)S(1)} %get-tuple-element.120), channel_id=1, source_target_pairs={{0,8},{16,24},{8,0},{24,16},{1,9},{17,25},{9,1},{25,17},{2,10},{18... | collective-permute-start | bytes 589832 | tf_op jit(solution)/shard_map/ppermute | solution.py:675
  76.7 1.7 %middle_kernel.5 = (f32[896,384]{1,0:T(8,128)S(1)}, f32[640,384]{1,0:T(8,128)S(1)}, f32[3,8,128]{2,1,0:T(8,128)S(1)}, f32[9,8,128]{2,1,0:T(8,128)S(1)}) custom-call(s32[4]{0:T(128)S(1)} %get-tuple-element.139.refs_1_.refs_0_, f32[4,2,256,256]{3,2,1,0:T(8,128)S(1)} %spectra_kernel.1.refs_1_, bf16[512,256]{1,0:T(8,128)(2,1)S(1)} %copy-done.3, ...), custom_call_target="tpu_custom_call" | custom-call | tf_op jit(solution)/shard_map/middle_kernel/pallas_call | solution.py:650
  78.4 0.0 collective-permute-done.12.refs_16_
  78.4 3.0 %collective-permute-done.13.refs_17_ = f32[128,384]{1,0:T(8,128)S(1)} collective-permute-done((f32[128,384]{1,0:T(8,128)S(1)}, f32[128,384]{1,0:T(8,128)S(1)}, u32[]{:S(2)}, u32[]{:S(2)}) %collective-permute-start.13) | collective-permute-done | bytes 196640 | tf_op jit(solution)/shard_map/ppermute | solution.py:675
  81.4 1.1 edge_kernel.5
  82.5 0.7 collective-permute-start.14
  83.2 3.1 %collective-permute-start.15 = (f32[576,128]{1,0:T(8,128)S(1)}, f32[576,128]{1,0:T(8,128)S(1)}, u32[]{:S(2)}, u32[]{:S(2)}) collective-permute-start(f32[576,128]{1,0:T(8,128)S(1)} %get-tuple-element.125), channel_id=1, source_target_pairs={{0,1},{2,3},{4,5},{6,7},{1,0},{3,2},{5,4},{7,6},{8,9},{10,11},{12,... | collective-permute-start | bytes 884744 | tf_op jit(solution)/shard_map/ppermute | solution.py:675
  86.3 12.2 %all_to_all.38 = f32[32,1,128]{2,1,0:T(1,128)S(1)} all-to-all(f32[32,1,128]{2,1,0:T(1,128)S(1)} %bitcast.26), channel_id=1, replica_groups=mesh['row'=4,'col'=8] {'row','col'}, dimensions={0} | all-to-all | bytes 32768 | tf_op jit(solution)/shard_map/all_to_all | solution.py:774
  98.6 0.0 collective-permute-done.14.refs_4_.refs_5_
  98.6 0.0 collective-permute-done.15.refs_5_.refs_6_
  98.6 0.9 row_strip_kernel.5
  99.4 0.7 collective-permute-start.16
  100.1 2.5 %collective-permute-start.17 = (f32[64,256]{1,0:T(8,128)S(1)}, f32[64,256]{1,0:T(8,128)S(1)}, u32[]{:S(2)}, u32[]{:S(2)}) collective-permute-start(f32[64,256]{1,0:T(8,128)S(1)} %get-tuple-element.134), channel_id=1, source_target_pairs={{0,8},{16,24},{8,0},{24,16},{1,9},{17,25},{9,1},{25,17},{2,10},{18... | collective-permute-start | bytes 196616 | tf_op jit(solution)/shard_map/ppermute | solution.py:675
  102.6 2.4 %last_middle_kernel.1 = (f32[1024,256]{1,0:T(8,128)}, f32[1024,256]{1,0:T(8,128)}) custom-call(f32[9,8,128]{2,1,0:T(8,128)S(1)} %get-tuple-element.132.refs_0_, f32[640,384]{1,0:T(8,128)S(1)} %get-tuple-element.122.refs_19_.refs_1_, f32[384,384]{1,0:T(8,128)S(1)} %get-tuple-element.128.refs_2_.refs_3_, f32[384,384]{1,0:T(8,128)S(1)} %get-tuple-element.129.refs_3_.refs_4_, ...), custom_call_target="tpu_custom_call" | custom-call | tf_op jit(solution)/shard_map/last_middle_kernel/pallas_call | solution.py:650
  105.0 0.0 collective-permute-done.16.refs_1_
  105.0 0.0 collective-permute-done.17.refs_2_
  105.0 1.4 %last_edge_kernel.1 = (f32[1024,256]{1,0:T(8,128)}, f32[1024,256]{1,0:T(8,128)}) custom-call(f32[9,8,128]{2,1,0:T(8,128)S(1)} %get-tuple-element.132.refs_0_, f32[64,256]{1,0:T(8,128)S(1)} %collective-permute-done.16.refs_1_, f32[64,256]{1,0:T(8,128)S(1)} %collective-permute-done.17.refs_2_, ...), custom_call_target="tpu_custom_call", output_to_operand_aliasing={{0}: (11, {}), {1}: (12, {})} | custom-call | tf_op jit(solution)/shard_map/last_edge_kernel/pallas_call | solution.py:650
  (10 shorter events, 0.1 us)
Async XLA Ops:
  0.8 1.2 %copy-start = (f32[1024,256]{1,0:T(8,128)S(1)}, f32[1024,256]{1,0:T(8,128)}, u32[]{:S(2)}) copy-start(f32[1024,256]{1,0:T(8,128)} %refs_9_.3) | copy-start | bytes 3145732
  2.0 7.6 %copy-start.6 = (bf16[384,512]{1,0:T(8,128)(2,1)S(1)}, bf16[384,512]{1,0:T(8,128)(2,1)}, u32[]{:S(2)}) copy-start(bf16[384,512]{1,0:T(8,128)(2,1)} %constant.84.clone.refs_4_) | copy-start | bytes 1179652
  2.0 7.6 %copy-start.7 = (bf16[512,384]{1,0:T(8,128)(2,1)S(1)}, bf16[512,384]{1,0:T(8,128)(2,1)}, u32[]{:S(2)}) copy-start(bf16[512,384]{1,0:T(8,128)(2,1)} %constant.83.clone.refs_3_) | copy-start | bytes 1179652
  2.7 7.7 %collective-permute-start = (f32[512,128]{1,0:T(8,128)S(1)}, f32[512,128]{1,0:T(8,128)S(1)}, u32[]{:S(2)}, u32[]{:S(2)}) collective-permute-start(f32[512,128]{1,0:T(8,128)S(1)} %get-tuple-element.70), channel_id=1, source_target_pairs={{1,2},{3,4},{5,6},{2,1},{4,3},{6,5},{9,10},{11,12},{13,14},{10,9},... | collective-permute-start | bytes 786440 | tf_op jit(solution)/shard_map/ppermute | solution.py:675
  3.4 7.0 %collective-permute-start.1 = (f32[512,128]{1,0:T(8,128)S(1)}, f32[512,128]{1,0:T(8,128)S(1)}, u32[]{:S(2)}, u32[]{:S(2)}) collective-permute-start(f32[512,128]{1,0:T(8,128)S(1)} %get-tuple-element.71), channel_id=1, source_target_pairs={{0,1},{2,3},{4,5},{6,7},{1,0},{3,2},{5,4},{7,6},{8,9},{10,11},{12,... | collective-permute-start | bytes 786440 | tf_op jit(solution)/shard_map/ppermute | solution.py:675
  9.6 1.2 %copy-start.1 = (f32[1024,256]{1,0:T(8,128)S(1)}, f32[1024,256]{1,0:T(8,128)}, u32[]{:S(2)}) copy-start(f32[1024,256]{1,0:T(8,128)} %refs_9_.3) | copy-start | bytes 3145732
  10.4 6.5 %copy-start.2 = (bf16[512,256]{1,0:T(8,128)(2,1)S(1)}, bf16[512,256]{1,0:T(8,128)(2,1)}, u32[]{:S(2)}) copy-start(bf16[512,256]{1,0:T(8,128)(2,1)} %constant.80.clone.refs_3_) | copy-start | bytes 786436
  10.4 6.5 %copy-start.3 = (bf16[512,256]{1,0:T(8,128)(2,1)S(1)}, bf16[512,256]{1,0:T(8,128)(2,1)}, u32[]{:S(2)}) copy-start(bf16[512,256]{1,0:T(8,128)(2,1)} %constant.79.clone.refs_2_) | copy-start | bytes 786436
  10.4 6.5 %copy-start.4 = (bf16[256,128]{1,0:T(8,128)(2,1)S(1)}, bf16[256,128]{1,0:T(8,128)(2,1)}, u32[]{:S(2)}) copy-start(bf16[256,128]{1,0:T(8,128)(2,1)} %constant.82.clone.refs_5_) | copy-start | bytes 196612
  10.4 6.5 %copy-start.5 = (bf16[256,128]{1,0:T(8,128)(2,1)S(1)}, bf16[256,128]{1,0:T(8,128)(2,1)}, u32[]{:S(2)}) copy-start(bf16[256,128]{1,0:T(8,128)(2,1)} %constant.81.clone.refs_4_) | copy-start | bytes 196612
  11.5 6.3 %collective-permute-start.2 = (f32[64,384]{1,0:T(8,128)S(1)}, f32[64,384]{1,0:T(8,128)S(1)}, u32[]{:S(2)}, u32[]{:S(2)}) collective-permute-start(f32[64,384]{1,0:T(8,128)S(1)} %get-tuple-element.80), channel_id=1, source_target_pairs={{8,16},{16,8},{9,17},{17,9},{10,18},{18,10},{11,19},{19,11},{12,20... | collective-permute-start | bytes 294920 | tf_op jit(solution)/shard_map/ppermute | solution.py:675
  12.2 7.4 %collective-permute-start.3 = (f32[64,384]{1,0:T(8,128)S(1)}, f32[64,384]{1,0:T(8,128)S(1)}, u32[]{:S(2)}, u32[]{:S(2)}) collective-permute-start(f32[64,384]{1,0:T(8,128)S(1)} %get-tuple-element.81), channel_id=1, source_target_pairs={{0,8},{16,24},{8,0},{24,16},{1,9},{17,25},{9,1},{25,17},{2,10},{18... | collective-permute-start | bytes 294920 | tf_op jit(solution)/shard_map/ppermute | solution.py:675
  20.4 21.2 %collective-permute-start.4 = (f32[1152,128]{1,0:T(8,128)S(1)}, f32[1152,128]{1,0:T(8,128)S(1)}, u32[]{:S(2)}, u32[]{:S(2)}) collective-permute-start(f32[1152,128]{1,0:T(8,128)S(1)} %get-tuple-element.85), channel_id=1, source_target_pairs={{1,2},{3,4},{5,6},{2,1},{4,3},{6,5},{9,10},{11,12},{13,14},{10,9},... | collective-permute-start | bytes 1769480 | tf_op jit(solution)/shard_map/ppermute | solution.py:675
  21.1 20.5 %collective-permute-start.5 = (f32[1152,128]{1,0:T(8,128)S(1)}, f32[1152,128]{1,0:T(8,128)S(1)}, u32[]{:S(2)}, u32[]{:S(2)}) collective-permute-start(f32[1152,128]{1,0:T(8,128)S(1)} %get-tuple-element.86), channel_id=1, source_target_pairs={{0,1},{2,3},{4,5},{6,7},{1,0},{3,2},{5,4},{7,6},{8,9},{10,11},{12,... | collective-permute-start | bytes 1769480 | tf_op jit(solution)/shard_map/ppermute | solution.py:675
  42.3 10.2 %collective-permute-start.8 = (f32[128,384]{1,0:T(8,128)S(1)}, f32[128,384]{1,0:T(8,128)S(1)}, u32[]{:S(2)}, u32[]{:S(2)}) collective-permute-start(f32[128,384]{1,0:T(8,128)S(1)} %get-tuple-element.97), channel_id=1, source_target_pairs={{8,16},{16,8},{9,17},{17,9},{10,18},{18,10},{11,19},{19,11},{12,20... | collective-permute-start | bytes 589832 | tf_op jit(solution)/shard_map/ppermute | solution.py:675
  43.0 9.5 %collective-permute-start.9 = (f32[128,384]{1,0:T(8,128)S(1)}, f32[128,384]{1,0:T(8,128)S(1)}, u32[]{:S(2)}, u32[]{:S(2)}) collective-permute-start(f32[128,384]{1,0:T(8,128)S(1)} %get-tuple-element.98), channel_id=1, source_target_pairs={{0,8},{16,24},{8,0},{24,16},{1,9},{17,25},{9,1},{25,17},{2,10},{18... | collective-permute-start | bytes 589832 | tf_op jit(solution)/shard_map/ppermute | solution.py:675
  48.8 4.6 %collective-permute-start.6 = (f32[384,128]{1,0:T(8,128)S(1)}, f32[384,128]{1,0:T(8,128)S(1)}, u32[]{:S(2)}, u32[]{:S(2)}) collective-permute-start(f32[384,128]{1,0:T(8,128)S(1)} %get-tuple-element.93), channel_id=1, source_target_pairs={{1,2},{3,4},{5,6},{2,1},{4,3},{6,5},{9,10},{11,12},{13,14},{10,9},... | collective-permute-start | bytes 589832 | tf_op jit(solution)/shard_map/ppermute | solution.py:675
  49.5 4.1 %collective-permute-start.7 = (f32[384,128]{1,0:T(8,128)S(1)}, f32[384,128]{1,0:T(8,128)S(1)}, u32[]{:S(2)}, u32[]{:S(2)}) collective-permute-start(f32[384,128]{1,0:T(8,128)S(1)} %get-tuple-element.94), channel_id=1, source_target_pairs={{0,1},{2,3},{4,5},{6,7},{1,0},{3,2},{5,4},{7,6},{8,9},{10,11},{12,... | collective-permute-start | bytes 589832 | tf_op jit(solution)/shard_map/ppermute | solution.py:675
  53.5 18.3 %collective-permute-start.10 = (f32[768,128]{1,0:T(8,128)S(1)}, f32[768,128]{1,0:T(8,128)S(1)}, u32[]{:S(2)}, u32[]{:S(2)}) collective-permute-start(f32[768,128]{1,0:T(8,128)S(1)} %get-tuple-element.105), channel_id=1, source_target_pairs={{1,2},{3,4},{5,6},{2,1},{4,3},{6,5},{9,10},{11,12},{13,14},{10,9},... | collective-permute-start | bytes 1179656 | tf_op jit(solution)/shard_map/ppermute | solution.py:675
  54.2 17.7 %collective-permute-start.11 = (f32[768,128]{1,0:T(8,128)S(1)}, f32[768,128]{1,0:T(8,128)S(1)}, u32[]{:S(2)}, u32[]{:S(2)}) collective-permute-start(f32[768,128]{1,0:T(8,128)S(1)} %get-tuple-element.106), channel_id=1, source_target_pairs={{0,1},{2,3},{4,5},{6,7},{1,0},{3,2},{5,4},{7,6},{8,9},{10,11},{12,... | collective-permute-start | bytes 1179656 | tf_op jit(solution)/shard_map/ppermute | solution.py:675
  72.5 5.9 %collective-permute-start.12 = (f32[128,384]{1,0:T(8,128)S(1)}, f32[128,384]{1,0:T(8,128)S(1)}, u32[]{:S(2)}, u32[]{:S(2)}) collective-permute-start(f32[128,384]{1,0:T(8,128)S(1)} %get-tuple-element.119), channel_id=1, source_target_pairs={{8,16},{16,8},{9,17},{17,9},{10,18},{18,10},{11,19},{19,11},{12,20... | collective-permute-start | bytes 589832 | tf_op jit(solution)/shard_map/ppermute | solution.py:675
  73.4 8.0 %collective-permute-start.13 = (f32[128,384]{1,0:T(8,128)S(1)}, f32[128,384]{1,0:T(8,128)S(1)}, u32[]{:S(2)}, u32[]{:S(2)}) collective-permute-start(f32[128,384]{1,0:T(8,128)S(1)} %get-tuple-element.120), channel_id=1, source_target_pairs={{0,8},{16,24},{8,0},{24,16},{1,9},{17,25},{9,1},{25,17},{2,10},{18... | collective-permute-start | bytes 589832 | tf_op jit(solution)/shard_map/ppermute | solution.py:675
  82.5 16.1 %collective-permute-start.14 = (f32[576,128]{1,0:T(8,128)S(1)}, f32[576,128]{1,0:T(8,128)S(1)}, u32[]{:S(2)}, u32[]{:S(2)}) collective-permute-start(f32[576,128]{1,0:T(8,128)S(1)} %get-tuple-element.124), channel_id=1, source_target_pairs={{1,2},{3,4},{5,6},{2,1},{4,3},{6,5},{9,10},{11,12},{13,14},{10,9},... | collective-permute-start | bytes 884744 | tf_op jit(solution)/shard_map/ppermute | solution.py:675
  83.2 15.4 %collective-permute-start.15 = (f32[576,128]{1,0:T(8,128)S(1)}, f32[576,128]{1,0:T(8,128)S(1)}, u32[]{:S(2)}, u32[]{:S(2)}) collective-permute-start(f32[576,128]{1,0:T(8,128)S(1)} %get-tuple-element.125), channel_id=1, source_target_pairs={{0,1},{2,3},{4,5},{6,7},{1,0},{3,2},{5,4},{7,6},{8,9},{10,11},{12,... | collective-permute-start | bytes 884744 | tf_op jit(solution)/shard_map/ppermute | solution.py:675
  99.4 5.6 %collective-permute-start.16 = (f32[64,256]{1,0:T(8,128)S(1)}, f32[64,256]{1,0:T(8,128)S(1)}, u32[]{:S(2)}, u32[]{:S(2)}) collective-permute-start(f32[64,256]{1,0:T(8,128)S(1)} %get-tuple-element.133), channel_id=1, source_target_pairs={{8,16},{16,8},{9,17},{17,9},{10,18},{18,10},{11,19},{19,11},{12,20... | collective-permute-start | bytes 196616 | tf_op jit(solution)/shard_map/ppermute | solution.py:675
  100.1 4.9 %collective-permute-start.17 = (f32[64,256]{1,0:T(8,128)S(1)}, f32[64,256]{1,0:T(8,128)S(1)}, u32[]{:S(2)}, u32[]{:S(2)}) collective-permute-start(f32[64,256]{1,0:T(8,128)S(1)} %get-tuple-element.134), channel_id=1, source_target_pairs={{0,8},{16,24},{8,0},{24,16},{1,9},{17,25},{9,1},{25,17},{2,10},{18... | collective-permute-start | bytes 196616 | tf_op jit(solution)/shard_map/ppermute | solution.py:675
